TPU v7x, 256 devices: a whole 4x4x8 slice. The times are simulated.
256 devices in a mesh: group: 8 (over z), owner: 32 (over y, x, core).
Axes of the slice: x: 4, y: 4, z: 8, core: 2. Of those that a mesh axis runs over, the one named last changes fastest.
Arguments:
- port_rows: bfloat16 [131072, 1024], P(('group', 'owner')), may hold values from -6 to 6
- defect_owner: int32 [131072, 1], P(('group', 'owner')), may hold values from 0 to 31; in each aligned block of 512 rows (0 to 511, 512 to 1023, ...) at most 32 rows name the same one
- defect_half: int32 [131072], P(('group', 'owner')), may hold values from 0 to 1
- defect_port: int32 [131072], P(('group', 'owner')), may hold values from 0 to 1023
- subcircuit_maps: bfloat16 [512, 1024, 1024], P(('group', 'owner')), may hold values from -0.1875 to 0.1875
- schur_off: bfloat16 [8192, 1024], P(('group', 'owner')), may hold values from -0.1875 to 0.1875
- schur_diag: float32 [8192], P(('group', 'owner')), may hold values from 1 to 4
- pivot_order: int32 [3, 1024], replicated, may hold values from 0 to 1023, each once within a row
Outputs:
- panel: float32 [131072, 1024], P(('group', 'owner'))
Inputs may be any that keep to these rules, and one draw needn't show every extreme that they name: `defect_owner`: within the rows of one device, no owner is named by more than 32 defects, a bound that some block reaches. `pivot_order`: each row is a permutation of the ports.
All inputs are finite; a program needn't handle non-finite values.
Results may differ from a plain program's by a relative error of at most 0.012.
Values may be sent and summed in bfloat16 or wider, within the bound.
No kernel may reach another device: no remote copies, remote signals or barrier semaphores. Data moves between devices by JAX's collectives and lax.ppermute only.
A program may use at most 128 MiB of HBM per device.

v0:
```python
import jax
import jax.numpy as jnp
from jax import lax
from jax.sharding import PartitionSpec as P


def swapped(shard, axis, stride):
    return lax.ppermute(shard, axis, [(i, i ^ 1 << stride) for i in range(lax.axis_size(axis))])


def slot_routes(keys, key_count, capacity, own_rows):
    matches = (keys[:, None] == jnp.arange(key_count, dtype=jnp.int32)[None, :]).astype(jnp.int32)
    before = jnp.cumsum(matches, axis=0) - matches
    slot_rank = jnp.sum(before * matches, axis=1)
    target = keys * capacity + slot_rank
    return (
        lax.broadcasted_iota(jnp.int32, (key_count * capacity, own_rows), 0) == target[None, :]
    ).astype(jnp.bfloat16)


def body(
    port_rows,
    defect_owner,
    defect_half,
    defect_port,
    subcircuit_maps,
    schur_off,
    schur_diag,
    pivot_order,
):
    own_rows, port_width = port_rows.shape
    owner_count = lax.axis_size("owner")
    sub_count = subcircuit_maps.shape[0]
    all_subs = owner_count * sub_count
    capacity = max(2, 2 * own_rows // owner_count)
    owner_ids = defect_owner[:, 0]
    columns = lax.broadcasted_iota(jnp.int32, (own_rows, port_width), 1)
    stimulus = (
        port_rows.astype(jnp.float32) + jnp.where(columns == defect_port[:, None], 8.0, 0.0)
    ).astype(jnp.bfloat16)
    sub_ids = owner_ids * sub_count + defect_half
    route_table = slot_routes(sub_ids, all_subs, capacity, own_rows)
    outgoing = jnp.dot(route_table, stimulus, preferred_element_type=jnp.float32).astype(
        jnp.bfloat16
    )
    outgoing = outgoing.reshape(owner_count, sub_count, capacity, port_width)
    answer = jnp.einsum(
        "oskp,spq->oskq",
        lax.all_to_all(outgoing, "owner", split_axis=0, concat_axis=0, tiled=True),
        subcircuit_maps,
        preferred_element_type=jnp.float32,
    ).astype(jnp.bfloat16)
    returned = lax.all_to_all(answer, "owner", split_axis=0, concat_axis=0, tiled=True)
    returned = returned.reshape(all_subs * capacity, port_width)
    response = lax.dot_general(
        route_table, returned, (((0,), (0,)), ((), ())), preferred_element_type=jnp.float32
    )
    first_diag = lax.all_gather(schur_diag, "owner", axis=0, tiled=True)
    level_count = lax.axis_size("group").bit_length() - 1
    assembled = []
    off_rows = schur_off.astype(jnp.float32)
    diag_rows = schur_diag
    for level in range(level_count):
        sibling_off, sibling_diag = (
            swapped(off_rows.astype(jnp.bfloat16), "group", level).astype(off_rows.dtype),
            swapped(diag_rows.astype(jnp.bfloat16), "group", level).astype(diag_rows.dtype),
        )
        off_rows = off_rows + jnp.take(sibling_off, pivot_order[level], axis=1)
        diag_rows = diag_rows + sibling_diag
        assembled.append(
            (
                lax.all_gather(off_rows.astype(jnp.bfloat16), "owner", axis=0, tiled=True),
                lax.all_gather(diag_rows.astype(jnp.bfloat16), "owner", axis=0, tiled=True).astype(
                    diag_rows.dtype
                ),
            )
        )
    panel = response / first_diag[None, :]
    for full_off, full_diag in assembled:
        coupled = lax.dot_general(
            panel.astype(jnp.bfloat16),
            full_off,
            (((1,), (1,)), ((), ())),
            preferred_element_type=jnp.float32,
        )
        panel = (response - coupled) / full_diag[None, :]
    return panel


def solution(mesh):
    return jax.shard_map(
        body,
        mesh=mesh,
        in_specs=(
            P(("group", "owner"), None),
            P(("group", "owner"), None),
            P(("group", "owner")),
            P(("group", "owner")),
            P(("group", "owner"), None, None),
            P(("group", "owner"), None),
            P(("group", "owner")),
            P(),
        ),
        out_specs=P(("group", "owner"), None),
        check_vma=False,
    )
```

profile of v0, /device:TPU:1, one launch (start us, length us, event | category | flops | bytes accessed | tf_op | source)
XLA Modules:
  0.0 309.5 jit_solution(244428925415076492)
XLA Ops:
  6.6 1.1 copy.28
  7.7 2.6 collective-permute-start
  10.3 0.8 fusion.30
  11.1 4.1 %collective-permute-done = bf16[32,1024]{0,1:T(8,128)(2,1)S(1)} collective-permute-done((bf16[32,1024]{0,1:T(8,128)(2,1)S(1)}, bf16[32,1024]{0,1:T(8,128)(2,1)S(1)}, u32[]{:S(2)}, u32[]{:S(2)}) %collective-permute-start) | collective-permute-done | bytes 65568 | tf_op jit(solution)/shard_map/ppermute | solution.py:8
  15.3 2.8 gather_fusion
  18.3 0.7 fusion.21
  19.0 1.2 reduce-window.6
  20.7 4.6 %fusion.5 = bf16[2048,1024]{1,0:T(8,128)(2,1)} fusion(s32[512]{0:T(512)S(1)} %multiply_add_fusion, bf16[512,1024]{1,0:T(8,128)(2,1)S(1)} %copy-done.6, s32[512]{0:T(512)S(1)} %copy-done.7), kind=kOutput, calls=%fused_computation.10 | convolution fusion | flops 2153250816 | bytes 5246976 | tf_op jit(solution)/shard_map/dot_general | solution.py:43
  25.3 9.6 %all-to-all-start = ((bf16[32,2,32,1024]{3,2,1,0:T(8,128)(2,1)}), bf16[32,2,32,1024]{3,2,1,0:T(8,128)(2,1)}, u32[]{:S(2)}, u32[]{:S(2)}) async-start(bf16[32,2,32,1024]{3,2,1,0:T(8,128)(2,1)} %bitcast.61), calls=%async_computation | async-start | bytes 8388608 | tf_op jit(solution)/shard_map/all_to_all | solution.py:49
  34.9 3.1 collective-permute-start.2
  38.0 2.3 collective-permute-done.2
  40.4 2.8 gather_fusion.1
  43.4 0.7 fusion.25
  44.1 41.5 %all-to-all-done = bf16[32,2,32,1024]{3,2,1,0:T(8,128)(2,1)} async-done(((bf16[32,2,32,1024]{3,2,1,0:T(8,128)(2,1)}), bf16[32,2,32,1024]{3,2,1,0:T(8,128)(2,1)}, u32[]{:S(2)}, u32[]{:S(2)}) %all-to-all-start) | async-done | bytes 4194336 | tf_op jit(solution)/shard_map/all_to_all | solution.py:49
  85.6 8.1 %convert_bitcast_fusion = bf16[32,2,32,1024]{3,2,0,1:T(8,128)(2,1)S(1)} fusion(bf16[2,1024,1024]{2,1,0:T(8,128)(2,1)} %param.14, bf16[32,2,32,1024]{3,2,1,0:T(8,128)(2,1)} %all-to-all-done), kind=kOutput, calls=%fused_computation.6 | convolution fusion | flops 4297064448 | bytes 12582912 | tf_op jit(solution)/shard_map/oskp,spq->oskq/dot_general | solution.py:47
  93.7 2.5 copy.27
  96.2 9.1 %all-to-all-start.1 = ((bf16[32,2,32,1024]{3,2,1,0:T(8,128)(2,1)}), bf16[32,2,32,1024]{3,2,1,0:T(8,128)(2,1)}, u32[]{:S(2)}, u32[]{:S(2)}) async-start(bf16[32,2,32,1024]{3,2,1,0:T(8,128)(2,1)} %copy.27), calls=%async_computation.1 | async-start | bytes 8388608 | tf_op jit(solution)/shard_map/all_to_all | solution.py:53
  105.4 7.9 %collective-permute-start.4 = (bf16[32,1024]{1,0:T(8,128)(2,1)S(1)}, bf16[32,1024]{1,0:T(8,128)(2,1)S(1)}, u32[]{:S(2)}, u32[]{:S(2)}) collective-permute-start(bf16[32,1024]{1,0:T(8,128)(2,1)S(1)} %copy-done.2), channel_id=1, source_target_pairs={{0,128},{32,160},{64,192},{96,224},{128,0},{160,32},{192,64},{224,... | collective-permute-start | bytes 196616 | tf_op jit(solution)/shard_map/ppermute | solution.py:8
  113.4 2.1 collective-permute-done.4
  115.6 2.8 gather_fusion.2
  118.6 0.7 fusion.19
  119.3 0.7 collective-permute-start.1
  120.0 0.6 dynamic-slice
  121.5 87.9 %all-reduce = f32[1024]{0:T(1024)S(1)} all-reduce(f32[1024]{0:T(1024)S(1)} %dynamic-update-slice), channel_id=1, replica_groups=mesh['group'=8,'owner'=32] {'owner'}, use_global_device_ids=true, to_apply=%add | all-reduce | flops 1024 | bytes 8192
  209.4 3.9 %collective-permute-start.3 = (bf16[32]{0:T(256)(128)(2,1)S(1)}, bf16[32]{0:T(256)(128)(2,1)S(1)}, u32[]{:S(2)}, u32[]{:S(2)}) collective-permute-start(bf16[32]{0:T(256)(128)(2,1)S(1)} %fusion.26), channel_id=1, source_target_pairs={{0,64},{32,96},{64,0},{96,32},{128,192},{160,224},{192,128},{224,1... | collective-permute-start | bytes 200 | tf_op jit(solution)/shard_map/ppermute | solution.py:8
  213.5 0.7 collective-permute-done.3
  214.2 6.6 %collective-permute-start.5 = (bf16[32]{0:T(256)(128)(2,1)S(1)}, bf16[32]{0:T(256)(128)(2,1)S(1)}, u32[]{:S(2)}, u32[]{:S(2)}) collective-permute-start(bf16[32]{0:T(256)(128)(2,1)S(1)} %fusion.29), channel_id=1, source_target_pairs={{0,128},{32,160},{64,192},{96,224},{128,0},{160,32},{192,64},{224,... | collective-permute-start | bytes 200 | tf_op jit(solution)/shard_map/ppermute | solution.py:8
  221.0 0.7 collective-permute-done.5
  222.0 67.3 %all-reduce.4 = (bf16[1024]{0:T(1024)(128)(2,1)S(1)}, bf16[1024]{0:T(1024)(128)(2,1)S(1)}, bf16[1024]{0:T(1024)(128)(2,1)S(1)}) all-reduce(bf16[1024]{0:T(1024)(128)(2,1)S(1)} %dynamic-update-slice.2, bf16[1024]{0:T(1024)(128)(2,1)S(1)} %dynamic-update-slice.1, ...), channel_id=1, replica_groups=mesh['group'=8,'owner'=32] {'owner'}, use_global_device_ids=true, to_apply=%add.2 | all-reduce | flops 3072 | bytes 12288
  289.4 4.6 %fusion.3 = f32[512,1024]{1,0:T(8,128)S(1)} fusion(bf16[2048,1024]{1,0:T(8,128)(2,1)} %bitcast.7, s32[512]{0:T(512)S(1)} %multiply_add_fusion), kind=kOutput, calls=%fused_computation.8 | convolution fusion | flops 2148532224 | bytes 6293504 | tf_op jit(solution)/shard_map/dot_general | solution.py:55
  294.0 4.7 %divide_convert_fusion = bf16[512,1024]{1,0:T(8,128)(2,1)S(1)} fusion(f32[512,1024]{1,0:T(8,128)S(1)} %fusion.3, bf16[1024,1024]{1,0:T(8,128)(2,1)} %all-gather.6.cloned.1.call-done, f32[1024]{0:T(1024)S(1)} %convert_element_type.108, bf16[1024,1024]{1,0:T(8,128)(2,1)} %all-gather.4.cloned.1.call-done, f32[1024]{0:T(1024)S(1)} %convert_element_type.102, ...), kind=kOutput, calls=%fused_computation.12 | convolution fusion | flops 2151677952 | bytes 7352320 | tf_op jit(solution)/shard_map/dot_general | solution.py:80
  298.7 4.2 %subtract_divide_fusion = f32[512,1024]{1,0:T(8,128)} fusion(f32[512,1024]{1,0:T(8,128)S(1)} %fusion.3, bf16[512,1024]{1,0:T(8,128)(2,1)S(1)} %divide_convert_fusion, bf16[1024,1024]{1,0:T(8,128)(2,1)} %all-gather.8.cloned.1.call-done, f32[1024]{0:T(1024)S(1)} %convert_element_type.114), kind=kOutput, calls=%fused_computation.11 | convolution fusion | flops 1074790400 | bytes 7344128 | tf_op jit(solution)/shard_map/dot_general | solution.py:80
  (63 shorter events, 2.4 us)
Async XLA Ops:
  6.5 11.7 %copy-start = (bf16[32,1024]{1,0:T(8,128)(2,1)S(1)}, bf16[32,1024]{1,0:T(8,128)(2,1)}, u32[]{:S(2)}) copy-start(bf16[32,1024]{1,0:T(8,128)(2,1)} %param.15) | copy-start | bytes 196612
  6.5 12.4 %copy-start.4 = (s32[512,1]{0,1:T(1,128)S(1)}, s32[512,1]{0,1:T(1,128)}, u32[]{:S(2)}) copy-start(s32[512,1]{0,1:T(1,128)} %param.11) | copy-start | bytes 6148
  6.5 12.4 %copy-start.3 = (s32[512]{0:T(512)S(1)}, s32[512]{0:T(512)}, u32[]{:S(2)}) copy-start(s32[512]{0:T(512)} %param.12) | copy-start | bytes 6148
  6.5 14.1 %copy-start.6 = (bf16[512,1024]{1,0:T(8,128)(2,1)S(1)}, bf16[512,1024]{1,0:T(8,128)(2,1)}, u32[]{:S(2)}) copy-start(bf16[512,1024]{1,0:T(8,128)(2,1)} %param.10) | copy-start | bytes 3145732
  6.5 14.1 %copy-start.7 = (s32[512]{0:T(512)S(1)}, s32[512]{0:T(512)}, u32[]{:S(2)}) copy-start(s32[512]{0:T(512)} %param.13) | copy-start | bytes 6148
  6.5 287.5 %all-gather.4.cloned.1.call-start = ((), (), s32[]{:S(2)}) async-start(), calls=%async_computation.2 | async-start | bytes 2162688 | tf_op jit(solution)/shard_map/all_gather | solution.py:72
  7.7 7.5 %collective-permute-start = (bf16[32,1024]{0,1:T(8,128)(2,1)S(1)}, bf16[32,1024]{0,1:T(8,128)(2,1)S(1)}, u32[]{:S(2)}, u32[]{:S(2)}) collective-permute-start(bf16[32,1024]{0,1:T(8,128)(2,1)S(1)} %copy.28), channel_id=1, source_target_pairs={{0,32},{32,0},{64,96},{96,64},{128,160},{160,128},{192,224},{224,1... | collective-permute-start | bytes 196616 | tf_op jit(solution)/shard_map/ppermute | solution.py:8
  25.3 9.6 %copy-start.1 = (bf16[32,1024]{1,0:T(8,128)(2,1)S(1)}, bf16[32,1024]{1,0:T(8,128)(2,1)}, u32[]{:S(2)}) copy-start(bf16[32,1024]{1,0:T(8,128)(2,1)} %fusion.21) | copy-start | bytes 196612
  25.3 60.3 %all-to-all-start = ((bf16[32,2,32,1024]{3,2,1,0:T(8,128)(2,1)}), bf16[32,2,32,1024]{3,2,1,0:T(8,128)(2,1)}, u32[]{:S(2)}, u32[]{:S(2)}) async-start(bf16[32,2,32,1024]{3,2,1,0:T(8,128)(2,1)} %bitcast.61), calls=%async_computation | async-start | bytes 8388608 | tf_op jit(solution)/shard_map/all_to_all | solution.py:49
  34.8 259.2 %all-gather.6.cloned.1.call-start = ((), (), s32[]{:S(2)}) async-start(), calls=%async_computation.3 | async-start | bytes 2162688 | tf_op jit(solution)/shard_map/all_gather | solution.py:72
  34.9 5.4 %collective-permute-start.2 = (bf16[32,1024]{1,0:T(8,128)(2,1)S(1)}, bf16[32,1024]{1,0:T(8,128)(2,1)S(1)}, u32[]{:S(2)}, u32[]{:S(2)}) collective-permute-start(bf16[32,1024]{1,0:T(8,128)(2,1)S(1)} %copy-done.1), channel_id=1, source_target_pairs={{0,64},{32,96},{64,0},{96,32},{128,192},{160,224},{192,128},{224,1... | collective-permute-start | bytes 196616 | tf_op jit(solution)/shard_map/ppermute | solution.py:8
  96.2 9.2 %copy-start.2 = (bf16[32,1024]{1,0:T(8,128)(2,1)S(1)}, bf16[32,1024]{1,0:T(8,128)(2,1)}, u32[]{:S(2)}) copy-start(bf16[32,1024]{1,0:T(8,128)(2,1)} %fusion.25) | copy-start | bytes 196612
  96.2 193.2 %all-to-all-start.1 = ((bf16[32,2,32,1024]{3,2,1,0:T(8,128)(2,1)}), bf16[32,2,32,1024]{3,2,1,0:T(8,128)(2,1)}, u32[]{:S(2)}, u32[]{:S(2)}) async-start(bf16[32,2,32,1024]{3,2,1,0:T(8,128)(2,1)} %copy.27), calls=%async_computation.1 | async-start | bytes 8388608 | tf_op jit(solution)/shard_map/all_to_all | solution.py:53
  105.3 14.0 %copy-start.5 = (f32[32]{0:T(128)S(1)}, f32[32]{0:T(128)}, u32[]{:S(2)}) copy-start(f32[32]{0:T(128)} %param.16) | copy-start | bytes 388
  105.3 14.7 %copy-start.8 = (u32[256]{0:T(256)S(1)}, u32[256]{0:T(256)}, u32[]{:S(2)}) copy-start(u32[256]{0:T(256)} %constant.29) | copy-start | bytes 3076
  105.3 193.4 %all-gather.8.cloned.1.call-start = ((), (), s32[]{:S(2)}) async-start(), calls=%async_computation.4 | async-start | bytes 2162688 | tf_op jit(solution)/shard_map/all_gather | solution.py:72
  105.4 10.1 %collective-permute-start.4 = (bf16[32,1024]{1,0:T(8,128)(2,1)S(1)}, bf16[32,1024]{1,0:T(8,128)(2,1)S(1)}, u32[]{:S(2)}, u32[]{:S(2)}) collective-permute-start(bf16[32,1024]{1,0:T(8,128)(2,1)S(1)} %copy-done.2), channel_id=1, source_target_pairs={{0,128},{32,160},{64,192},{96,224},{128,0},{160,32},{192,64},{224,... | collective-permute-start | bytes 196616 | tf_op jit(solution)/shard_map/ppermute | solution.py:8
  119.3 90.1 %collective-permute-start.1 = (bf16[32]{0:T(256)(128)(2,1)S(1)}, bf16[32]{0:T(256)(128)(2,1)S(1)}, u32[]{:S(2)}, u32[]{:S(2)}) collective-permute-start(bf16[32]{0:T(256)(128)(2,1)S(1)} %convert_element_type.99), channel_id=1, source_target_pairs={{0,32},{32,0},{64,96},{96,64},{128,160},{160,128},{192,224},{224,1... | collective-permute-start | bytes 200 | tf_op jit(solution)/shard_map/ppermute | solution.py:8
  209.4 4.8 %collective-permute-start.3 = (bf16[32]{0:T(256)(128)(2,1)S(1)}, bf16[32]{0:T(256)(128)(2,1)S(1)}, u32[]{:S(2)}, u32[]{:S(2)}) collective-permute-start(bf16[32]{0:T(256)(128)(2,1)S(1)} %fusion.26), channel_id=1, source_target_pairs={{0,64},{32,96},{64,0},{96,32},{128,192},{160,224},{192,128},{224,1... | collective-permute-start | bytes 200 | tf_op jit(solution)/shard_map/ppermute | solution.py:8
  214.2 7.5 %collective-permute-start.5 = (bf16[32]{0:T(256)(128)(2,1)S(1)}, bf16[32]{0:T(256)(128)(2,1)S(1)}, u32[]{:S(2)}, u32[]{:S(2)}) collective-permute-start(bf16[32]{0:T(256)(128)(2,1)S(1)} %fusion.29), channel_id=1, source_target_pairs={{0,128},{32,160},{64,192},{96,224},{128,0},{160,32},{192,64},{224,... | collective-permute-start | bytes 200 | tf_op jit(solution)/shard_map/ppermute | solution.py:8
Sparse Core Ops, SparseCore 0:
  19.1 78.0 all-gather.3
  99.7 76.3 all-gather.5
  178.6 48.1 all-gather.7
where the time goes:
time: 310 us; the launch traced here: 309 us
  blocking collectives  155 us (50%)
  waiting for transfers between devices  51.6 us (17%)
  starting transfers between devices  43.5 us (14%)
  matrix products  26.2 us (8%)
  local copies, waits for them, and re-layouts  15.4 us (5%)
  between operations  14.1 us (5%)
  other arithmetic  3.52 us (1%)
    unnamed x2, blocking collectives  155 us
    all_to_all x1, waiting for transfers between devices, body(): lax.all_to_all(outgoing, 'owner', split_axis=0, concat_axis=0, tiled=True)  41.5 us
    ppermute x6, starting transfers between devices, swapped(): lax.ppermute(shard, axis, [(i, i ^ 1 << stride) for i in range(lax.axis_s...  24.7 us
    ppermute x6, waiting for transfers between devices, swapped(): lax.ppermute(shard, axis, [(i, i ^ 1 << stride) for i in range(lax.axis_s...  10 us
    all_to_all x1, starting transfers between devices, body(): lax.all_to_all(outgoing, 'owner', split_axis=0, concat_axis=0, tiled=True)  9.56 us
    all_to_all x1, starting transfers between devices, body(): lax.all_to_all(answer, 'owner', split_axis=0, concat_axis=0, tiled=True)  9.1 us
    gather x6, local copies, waits for them, and re-layouts, body(): off_rows = off_rows + jnp.take(sibling_off, pivot_order[level], axis=1)  8.94 us
    dot_general x2, matrix products, body(): lax.dot_general(panel.astype(jnp.bfloat16), full_off, (((1,), (1,)), ((),...  8.89 us
  transfers between devices with their start and end apart: 11, of which 6 were waited for; matrix products, arithmetic and copies ran while one was open for 12% of the time, Pallas kernels for 0%

commit v1 on v0

v1 whole, which is shorter than its diff:
```python
import jax
import jax.numpy as jnp
from jax import lax
from jax.experimental import pallas as pl
from jax.experimental.pallas import tpu as pltpu
from jax.sharding import PartitionSpec as P

BF16 = jnp.bfloat16
F32 = jnp.float32
I32 = jnp.int32

ROWS = 512
PORTS = 1024
OWNERS = 32
CAP = 32
SLOTS = OWNERS * CAP
OWN = 32
DROWS = 8
ZROWS = OWN + DROWS
PACK = 3 * OWN + DROWS
HALF_SCALE = 64.0
HALF_MARK = 32.0
STEPS = (1, -1, 2)
NEAR = (0, -1, 1, -2)


def iota(shape, dim):
    return lax.broadcasted_iota(I32, shape, dim)


def params(limit=48, dims=None):
    return pltpu.CompilerParams(vmem_limit_bytes=limit << 20, dimension_semantics=dims)


def cost(flops, nbytes):
    return pl.CostEstimate(flops=flops, bytes_accessed=nbytes, transcendentals=0)


def split(value, parts):
    pieces = []
    for _ in range(parts):
        piece = value.astype(BF16).astype(F32)
        pieces.append(piece)
        value = value - piece
    return pieces


def rows_of(pieces, count):
    r = iota((count, PORTS), 0)
    out = jnp.zeros((count, PORTS), F32)
    for k, piece in enumerate(pieces):
        out = jnp.where(r == k, piece, out)
    return out.astype(BF16)


def own_lanes():
    own = lax.axis_index("owner")
    return iota((OWN, PORTS), 1) == own * OWN + iota((OWN, PORTS), 0)


def prep_kernel(owner_ref, half_ref, port_ref, rows_ref, off_ref, diag_ref, out_ref, target_ref, z_ref, stim):
    step = pl.program_id(0)
    tile = out_ref.shape[0]

    @pl.when(step == 0)
    def _():
        owner = owner_ref[...]
        named = iota((OWNERS, ROWS), 0) == owner
        earlier = jnp.where(iota((ROWS, ROWS), 0) < iota((ROWS, ROWS), 1), 1.0, 0.0).astype(BF16)
        before = jnp.dot(jnp.where(named, 1.0, 0.0).astype(BF16), earlier, preferred_element_type=F32)
        rank = jnp.sum(jnp.where(named, before, 0.0), axis=0, keepdims=True)
        target_ref[...] = owner * CAP + rank.astype(I32)
        port = jnp.transpose(jnp.broadcast_to(port_ref[...], (128, ROWS)))
        for j in range(PORTS // 128):
            lanes = slice(128 * j, 128 * j + 128)
            bump = jnp.where(iota((ROWS, 128), 1) + 128 * j == port, 8.0, 0.0)
            stim[:, lanes] = (rows_ref[:, lanes].astype(F32) + bump).astype(BF16)
        z_ref[:OWN, :] = off_ref[...]
        diag = jnp.sum(
            jnp.where(iota((OWN, OWN), 0) == iota((OWN, OWN), 1), diag_ref[...], 0.0), axis=1, keepdims=True
        )
        placed = jnp.sum(jnp.where(own_lanes(), diag, 0.0), axis=0, keepdims=True)
        z_ref[OWN:, :] = rows_of(split(placed, 3), DROWS)

    scale = jnp.where(half_ref[...] == 1, HALF_SCALE, 1.0)
    route = jnp.where(iota((tile, ROWS), 0) + step * tile == target_ref[...], scale, 0.0).astype(BF16)
    out_ref[...] = jnp.dot(route, stim[...], preferred_element_type=F32).astype(BF16)


def prep(owner, half, port, rows, off, diag):
    tile = 256
    whole = lambda *shape: pl.BlockSpec(shape, lambda i: (0,) * len(shape))
    return pl.pallas_call(
        prep_kernel,
        grid=(SLOTS // tile,),
        in_specs=[
            whole(1, ROWS), whole(1, ROWS), whole(1, ROWS), whole(ROWS, PORTS), whole(OWN, PORTS), whole(1, OWN),
        ],
        out_specs=[pl.BlockSpec((tile, PORTS), lambda i: (i, 0)), whole(1, ROWS), whole(ZROWS, PORTS)],
        out_shape=[
            jax.ShapeDtypeStruct((SLOTS, PORTS), BF16),
            jax.ShapeDtypeStruct((1, ROWS), I32),
            jax.ShapeDtypeStruct((ZROWS, PORTS), BF16),
        ],
        scratch_shapes=[pltpu.VMEM((ROWS, PORTS), BF16)],
        compiler_params=params(),
        cost_estimate=cost(2 * SLOTS * ROWS * PORTS, 4 << 20),
        name="prep",
    )(owner, half, port, rows, off, diag)


def maps_kernel(x_ref, maps_ref, out_ref):
    x = x_ref[...]
    second = jnp.max(jnp.abs(x.astype(F32)), axis=1, keepdims=True) > HALF_MARK
    first_rows = jnp.where(second, 0.0, x.astype(F32)).astype(BF16)
    second_rows = jnp.where(second, x.astype(F32) * (1.0 / HALF_SCALE), 0.0).astype(BF16)
    acc = jnp.dot(first_rows, maps_ref[0], preferred_element_type=F32)
    acc = acc + jnp.dot(second_rows, maps_ref[1], preferred_element_type=F32)
    out_ref[...] = acc.astype(BF16)


def apply_maps(x, maps):
    tile = 256
    return pl.pallas_call(
        maps_kernel,
        grid=(SLOTS // tile,),
        in_specs=[
            pl.BlockSpec((tile, PORTS), lambda i: (i, 0)),
            pl.BlockSpec((2, PORTS, PORTS), lambda i: (0, 0, 0)),
        ],
        out_specs=pl.BlockSpec((tile, PORTS), lambda i: (i, 0)),
        out_shape=jax.ShapeDtypeStruct((SLOTS, PORTS), BF16),
        compiler_params=params(),
        cost_estimate=cost(4 * SLOTS * PORTS * PORTS, 8 << 20),
        name="apply_maps",
    )(x, maps)


def permuted(values, order):
    out = jnp.zeros(values.shape, F32)
    for j in range(0, PORTS, 256):
        pick = jnp.where(iota((256, PORTS), 0) + j == order, 1.0, 0.0).astype(BF16)
        out = out + jnp.dot(values[:, j : j + 256], pick, preferred_element_type=F32)
    return out


def read_diag(z_ref):
    z = z_ref[OWN:, :].astype(F32)
    return z[0:1] + z[1:2] + z[2:3]


def column(placed):
    return jnp.sum(jnp.where(own_lanes(), placed, 0.0), axis=1, keepdims=True)


def inverse(placed):
    held = placed > 0.0
    return jnp.where(held, 1.0 / jnp.where(held, placed, 1.0), 0.0)


def low_levels_kernel(z0_ref, z1_ref, z2_ref, z3_ref, order_ref, z_ref, off_ref, diag_ref, gb_ref):
    picked = permuted(jnp.concatenate([z1_ref[:OWN, :], z3_ref[:OWN, :]], axis=0), order_ref[0:1, :])
    off1 = z0_ref[:OWN, :].astype(F32) + picked[:OWN]
    picked2 = permuted(jnp.concatenate([z2_ref[:OWN, :], picked[OWN:].astype(BF16)], axis=0), order_ref[1:2, :])
    off2 = off1 + (picked2[:OWN] + picked2[OWN:])
    d0 = read_diag(z0_ref)
    d1 = d0 + read_diag(z1_ref)
    d2 = d1 + (read_diag(z2_ref) + read_diag(z3_ref))
    z_ref[:OWN, :] = off2.astype(BF16)
    z_ref[OWN:, :] = rows_of(split(d2, 3), DROWS)
    off_ref[...] = off2
    r = iota((DROWS, PORTS), 0)
    diag_ref[...] = jnp.where(r == 0, d0, jnp.where(r == 1, d2, 0.0))
    gb_ref[:OWN, :] = ((jnp.where(own_lanes(), d0, 0.0) - off1) / column(d1)).astype(BF16)
    gb_ref[OWN:, :] = (off2 / column(d2)).astype(BF16)


def low_levels(z0, z1, z2, z3, order):
    return pl.pallas_call(
        low_levels_kernel,
        out_shape=[
            jax.ShapeDtypeStruct((ZROWS, PORTS), BF16),
            jax.ShapeDtypeStruct((OWN, PORTS), F32),
            jax.ShapeDtypeStruct((DROWS, PORTS), F32),
            jax.ShapeDtypeStruct((2 * OWN, PORTS), BF16),
        ],
        compiler_params=params(),
        cost_estimate=cost(4 * 64 * PORTS * PORTS, 1 << 20),
        name="low_levels",
    )(z0, z1, z2, z3, order)


def top_level_kernel(z4_ref, off_ref, diag_ref, gb_ref, order_ref, pack_ref):
    off3 = off_ref[...] + permuted(z4_ref[:OWN, :], order_ref[2:3, :])
    d0, d2 = diag_ref[0:1, :], diag_ref[1:2, :]
    d3 = d2 + read_diag(z4_ref)
    pack_ref[: 2 * OWN, :] = gb_ref[...]
    pack_ref[2 * OWN : 3 * OWN, :] = (off3 / column(d3)).astype(BF16)
    pieces = split(inverse(d0), 3) + split(inverse(d3), 3) + split(d0 * inverse(d2), 2)
    pack_ref[3 * OWN :, :] = rows_of(pieces, DROWS)


def top_level(z4, off, diag, gb, order):
    return pl.pallas_call(
        top_level_kernel,
        out_shape=jax.ShapeDtypeStruct((PACK, PORTS), BF16),
        compiler_params=params(),
        cost_estimate=cost(2 * 32 * PORTS * PORTS, 1 << 20),
        name="top_level",
    )(z4, off, diag, gb, order)


def fold_kernel(*refs):
    parts, (f_ref, diag_ref, held, marks, mid, sems) = refs[:8], refs[8:]
    own = lax.axis_index("owner")
    core, x, y = own & 1, (own >> 1) & 3, own >> 3
    copies = []
    slot = 0
    for side in range(2):
        c = core if side == 0 else 1 - core
        for m in range(4):
            for k in range(4):
                dx = jnp.where(c == 0, NEAR[k], NEAR[m])
                dy = jnp.where(c == 0, NEAR[m], NEAR[k])
                start = ((((y + dy) & 3) * 4 + ((x + dx) & 3)) * 2 + c) * OWN
                start = pl.multiple_of(start, OWN)
                block = parts[side * 4 + m].at[k]
                for j in range(3):
                    copies.append(
                        pltpu.make_async_copy(
                            block.at[pl.ds(j * OWN, OWN), :], held.at[j, pl.ds(start, OWN), :], sems.at[j]
                        )
                    )
                copies.append(pltpu.make_async_copy(block.at[pl.ds(3 * OWN, DROWS), :], marks.at[slot], sems.at[3]))
                slot += 1
    for copy in copies:
        copy.start()
    for copy in copies:
        copy.wait()
    total = jnp.sum(marks[...].astype(F32), axis=0)
    inv0 = total[0:1] + total[1:2] + total[2:3]
    inv3 = total[3:4] + total[4:5] + total[5:6]
    ratio = total[6:7] + total[7:8]
    r = iota((DROWS, PORTS), 0)
    diag_ref[...] = jnp.where(r == 0, inv0, jnp.where(r == 1, inv3, 0.0))
    tile = 256

    @pl.loop(0, PORTS // tile)
    def _(t):
        at = pl.ds(pl.multiple_of(t * tile, tile), tile)
        acc = jnp.dot(held[1, at, :], held[0], preferred_element_type=F32)
        on = iota((tile, PORTS), 1) == iota((tile, PORTS), 0) + t * tile
        mid[at, :] = (jnp.where(on, ratio, 0.0) - acc).astype(BF16)

    @pl.loop(0, PORTS // tile)
    def _(t):
        at = pl.ds(pl.multiple_of(t * tile, tile), tile)
        f_ref[at, :] = jnp.dot(held[2, at, :], mid[...], preferred_element_type=F32).astype(BF16)


def fold(parts):
    return pl.pallas_call(
        fold_kernel,
        in_specs=[pl.BlockSpec(memory_space=pl.ANY)] * 8,
        out_shape=[jax.ShapeDtypeStruct((PORTS, PORTS), BF16), jax.ShapeDtypeStruct((DROWS, PORTS), F32)],
        scratch_shapes=[
            pltpu.VMEM((3, PORTS, PORTS), BF16),
            pltpu.VMEM((32, DROWS, PORTS), BF16),
            pltpu.VMEM((PORTS, PORTS), BF16),
            pltpu.SemaphoreType.DMA((4,)),
        ],
        compiler_params=params(),
        cost_estimate=cost(4 * PORTS**3, 9 << 20),
        name="fold",
    )(*parts)


def finish_kernel(target_ref, ret_ref, f_ref, diag_ref, out_ref):
    tile = out_ref.shape[0]
    target = jnp.transpose(jnp.broadcast_to(target_ref[...], (128, tile)))
    route = jnp.concatenate(
        [
            jnp.where(iota((tile, 128), 1) + 128 * j == target, 1.0, 0.0).astype(BF16)
            for j in range(SLOTS // 128)
        ],
        axis=1,
    )
    response = jnp.dot(route, ret_ref[...], preferred_element_type=F32)
    scaled = (response * diag_ref[0:1, :]).astype(BF16)
    coupled = lax.dot_general(scaled, f_ref[...], (((1,), (1,)), ((), ())), preferred_element_type=F32)
    out_ref[...] = response * diag_ref[1:2, :] - coupled


def finish(target, returned, f, diag):
    tile = 128
    whole = lambda *shape: pl.BlockSpec(shape, lambda i: (0,) * len(shape))
    return pl.pallas_call(
        finish_kernel,
        grid=(ROWS // tile,),
        in_specs=[
            pl.BlockSpec((1, tile), lambda i: (0, i)), whole(SLOTS, PORTS), whole(PORTS, PORTS), whole(DROWS, PORTS),
        ],
        out_specs=pl.BlockSpec((tile, PORTS), lambda i: (i, 0)),
        out_shape=jax.ShapeDtypeStruct((ROWS, PORTS), F32),
        compiler_params=params(),
        cost_estimate=cost(4 * ROWS * PORTS * PORTS, 6 << 20),
        name="finish",
    )(target, returned, f, diag)


def group_swap(value, mask):
    return lax.ppermute(value, "group", [(i, i ^ mask) for i in range(8)])


def chip_shift(value, step, turn):
    pairs = []
    for o in range(OWNERS):
        c, x, y = o & 1, (o >> 1) & 3, o >> 3
        if (c ^ turn) == 0:
            x = (x + step) % 4
        else:
            y = (y + step) % 4
        pairs.append((o, (y * 4 + x) * 2 + c))
    return lax.ppermute(value, "owner", pairs)


def core_swap(value):
    return lax.ppermute(value, "owner", [(o, o ^ 1) for o in range(OWNERS)])


def exchange(value):
    shape = value.shape
    value = value.reshape(OWNERS, CAP, PORTS)
    return lax.all_to_all(value, "owner", split_axis=0, concat_axis=0, tiled=True).reshape(shape)


def body(port_rows, defect_owner, defect_half, defect_port, subcircuit_maps, schur_off, schur_diag, pivot_order):
    outgoing, target, z0 = prep(
        defect_owner.reshape(1, ROWS),
        defect_half.reshape(1, ROWS),
        defect_port.reshape(1, ROWS),
        port_rows,
        schur_off,
        schur_diag.reshape(1, OWN),
    )
    arrived = exchange(outgoing)
    z1, z2, z3 = (group_swap(z0, mask) for mask in (1, 2, 3))
    z, off, diag, gb = low_levels(z0, z1, z2, z3, pivot_order)
    pack = top_level(group_swap(z, 4), off, diag, gb, pivot_order)
    line = jnp.stack([pack] + [chip_shift(pack, step, 0) for step in STEPS])
    parts = [line] + [chip_shift(line, step, 1) for step in STEPS]
    parts = parts + [core_swap(part) for part in parts]
    f, inverses = fold(parts)
    answers = apply_maps(arrived, subcircuit_maps)
    returned = exchange(answers)
    return finish(target, returned, f, inverses)


def solution(mesh):
    return jax.shard_map(
        body,
        mesh=mesh,
        in_specs=(
            P(("group", "owner"), None),
            P(("group", "owner"), None),
            P(("group", "owner")),
            P(("group", "owner")),
            P(("group", "owner"), None, None),
            P(("group", "owner"), None),
            P(("group", "owner")),
            P(),
        ),
        out_specs=P(("group", "owner"), None),
        check_vma=False,
    )
```

time: 310 us -> 115 us (0.37)
  the two profiles are of different devices: /device:TPU:1 before, /device:TPU:41 now
where the time goes in v1:
time: 115 us; the launch traced here: 114 us
  starting transfers between devices  55.5 us (48%)
  Pallas kernels  30.6 us (27%)
  waiting for transfers between devices  19.2 us (17%)
  local copies, waits for them, and re-layouts  8.98 us (8%)
    ppermute x4, starting transfers between devices, core_swap(): return lax.ppermute(value, 'owner', [(o, o ^ 1) for o in range(OWNERS)])  21.8 us
    all_to_all x2, starting transfers between devices, exchange(): lax.all_to_all(value, 'owner', split_axis=0, concat_axis=0, tiled=True)  17 us
    pallas_call x1, Pallas kernels, fold(): pl.pallas_call(fold_kernel, in_specs=[pl.BlockSpec(memory_space=pl.ANY)]...  13.7 us
    unnamed x22, local copies, waits for them, and re-layouts  8.98 us
    ppermute x4, waiting for transfers between devices, group_swap(): return lax.ppermute(value, 'group', [(i, i ^ mask) for i in range(8)])  8.74 us
    ppermute x4, starting transfers between devices, group_swap(): return lax.ppermute(value, 'group', [(i, i ^ mask) for i in range(8)])  8.56 us
    ppermute x6, waiting for transfers between devices, chip_shift(): return lax.ppermute(value, 'owner', pairs)  8.25 us
    ppermute x6, starting transfers between devices, chip_shift(): return lax.ppermute(value, 'owner', pairs)  8.17 us
  transfers between devices with their start and end apart: 16, of which 7 were waited for; matrix products, arithmetic and copies ran while one was open for 0% of the time, Pallas kernels for 20%

profile of v1, /device:TPU:41, one launch (start us, length us, event | category | flops | bytes accessed | tf_op | source)
XLA Modules:
  0.0 114.5 jit_solution(1078769802047702324)
XLA Ops:
  0.0 1.2 %copy-done.3 = bf16[512,1024]{1,0:T(8,128)(2,1)S(1)} copy-done((bf16[512,1024]{1,0:T(8,128)(2,1)S(1)}, bf16[512,1024]{1,0:T(8,128)(2,1)}, u32[]{:S(2)}) %copy-start.3) | copy-done | bytes 1048600
  1.2 0.8 copy-done.4
  2.1 0.7 copy-done.5
  2.8 0.7 copy-done.6
  3.4 0.7 copy-done.7
  4.1 0.7 copy-done.8
  4.8 2.3 %prep.1 = (bf16[1024,1024]{1,0:T(8,128)(2,1)S(1)}, s32[1,512]{1,0:T(1,128)S(1)}, bf16[40,1024]{1,0:T(8,128)(2,1)S(1)}) custom-call(s32[1,512]{1,0:T(1,128)S(1)} %bitcast.17, s32[1,512]{1,0:T(1,128)S(1)} %bitcast.18, s32[1,512]{1,0:T(1,128)S(1)} %bitcast.19, bf16[512,1024]{1,0:T(8,128)(2,1)S(1)} %copy-done.3, bf16[32,1024]{1,0:T(8,128)(2,1)S(1)} %copy-done.4, ...), custom_call_target="tpu_custom_call" | custom-call | flops 1073741824 | bytes 4194304 | tf_op jit(solution)/shard_map/prep/pallas_call | solution.py:93
  7.1 1.3 %copy-done = bf16[1024,1024]{1,0:T(8,128)(2,1)} copy-done((bf16[1024,1024]{1,0:T(8,128)(2,1)}, bf16[1024,1024]{1,0:T(8,128)(2,1)S(1)}, u32[]{:S(2)}) %copy-start) | copy-done | bytes 2097176
  8.4 8.0 %all-to-all-start = ((bf16[32,32,1024]{2,1,0:T(8,128)(2,1)}), bf16[32,32,1024]{2,1,0:T(8,128)(2,1)S(1)}, u32[]{:S(2)}, u32[]{:S(2)}) async-start(bf16[32,32,1024]{2,1,0:T(8,128)(2,1)} %bitcast.13), calls=%async_computation | async-start | bytes 4194304 | tf_op jit(solution)/shard_map/all_to_all | solution.py:334
  16.4 1.7 %collective-permute-start.2 = (bf16[40,1024]{1,0:T(8,128)(2,1)S(1)}, bf16[40,1024]{1,0:T(8,128)(2,1)S(1)}, u32[]{:S(2)}, u32[]{:S(2)}) collective-permute-start(bf16[40,1024]{1,0:T(8,128)(2,1)S(1)} %get-tuple-element.16.z0_ref), channel_id=1, source_target_pairs={{0,96},{32,64},{64,32},{96,0},{128,224},{160,192},{192,160},{224,1... | collective-permute-start | bytes 245768 | tf_op jit(solution)/shard_map/ppermute | solution.py:312
  18.1 1.5 %collective-permute-start.1 = (bf16[40,1024]{1,0:T(8,128)(2,1)S(1)}, bf16[40,1024]{1,0:T(8,128)(2,1)S(1)}, u32[]{:S(2)}, u32[]{:S(2)}) collective-permute-start(bf16[40,1024]{1,0:T(8,128)(2,1)S(1)} %get-tuple-element.16.z0_ref), channel_id=1, source_target_pairs={{0,64},{32,96},{64,0},{96,32},{128,192},{160,224},{192,128},{224,1... | collective-permute-start | bytes 245768 | tf_op jit(solution)/shard_map/ppermute | solution.py:312
  19.6 1.1 collective-permute-start
  20.7 3.9 %collective-permute-done.1.z2_ref = bf16[40,1024]{1,0:T(8,128)(2,1)S(1)} collective-permute-done((bf16[40,1024]{1,0:T(8,128)(2,1)S(1)}, bf16[40,1024]{1,0:T(8,128)(2,1)S(1)}, u32[]{:S(2)}, u32[]{:S(2)}) %collective-permute-start.1) | collective-permute-done | bytes 81952 | tf_op jit(solution)/shard_map/ppermute | solution.py:312
  24.6 1.8 %collective-permute-done.z1_ref = bf16[40,1024]{1,0:T(8,128)(2,1)S(1)} collective-permute-done((bf16[40,1024]{1,0:T(8,128)(2,1)S(1)}, bf16[40,1024]{1,0:T(8,128)(2,1)S(1)}, u32[]{:S(2)}, u32[]{:S(2)}) %collective-permute-start) | collective-permute-done | bytes 81952 | tf_op jit(solution)/shard_map/ppermute | solution.py:312
  26.4 1.0 low_levels.1
  27.4 4.3 %collective-permute-start.3 = (bf16[40,1024]{1,0:T(8,128)(2,1)S(1)}, bf16[40,1024]{1,0:T(8,128)(2,1)S(1)}, u32[]{:S(2)}, u32[]{:S(2)}) collective-permute-start(bf16[40,1024]{1,0:T(8,128)(2,1)S(1)} %get-tuple-element.17), channel_id=1, source_target_pairs={{0,128},{32,160},{64,192},{96,224},{128,0},{160,32},{192,64},{224,... | collective-permute-start | bytes 245768 | tf_op jit(solution)/shard_map/ppermute | solution.py:312
  31.7 3.0 %collective-permute-done.3.z4_ref = bf16[40,1024]{1,0:T(8,128)(2,1)S(1)} collective-permute-done((bf16[40,1024]{1,0:T(8,128)(2,1)S(1)}, bf16[40,1024]{1,0:T(8,128)(2,1)S(1)}, u32[]{:S(2)}, u32[]{:S(2)}) %collective-permute-start.3) | collective-permute-done | bytes 81952 | tf_op jit(solution)/shard_map/ppermute | solution.py:312
  35.2 2.2 %collective-permute-start.6 = (bf16[104,1024]{1,0:T(8,128)(2,1)S(1)}, bf16[104,1024]{1,0:T(8,128)(2,1)S(1)}, u32[]{:S(2)}, u32[]{:S(2)}) collective-permute-start(bf16[104,1024]{1,0:T(8,128)(2,1)S(1)} %top_level.1), channel_id=1, source_target_pairs={{0,4},{1,17},{2,6},{3,19},{4,0},{5,21},{6,2},{7,23},{8,12},{9,25},... | collective-permute-start | bytes 638984 | tf_op jit(solution)/shard_map/ppermute | solution.py:324
  37.4 0.8 collective-permute-start.5
  38.9 6.4 %collective-permute-done.6 = bf16[104,1024]{1,0:T(8,128)(2,1)S(1)} collective-permute-done((bf16[104,1024]{1,0:T(8,128)(2,1)S(1)}, bf16[104,1024]{1,0:T(8,128)(2,1)S(1)}, u32[]{:S(2)}, u32[]{:S(2)}) %collective-permute-start.6) | collective-permute-done | bytes 213024 | tf_op jit(solution)/shard_map/ppermute | solution.py:324
  45.3 1.7 %collective-permute-done.5 = bf16[104,1024]{1,0:T(8,128)(2,1)S(1)} collective-permute-done((bf16[104,1024]{1,0:T(8,128)(2,1)S(1)}, bf16[104,1024]{1,0:T(8,128)(2,1)S(1)}, u32[]{:S(2)}, u32[]{:S(2)}) %collective-permute-start.5) | collective-permute-done | bytes 213024 | tf_op jit(solution)/shard_map/ppermute | solution.py:324
  47.1 2.4 %collective-permute-start.9 = (bf16[4,104,1024]{2,1,0:T(8,128)(2,1)S(1)}, bf16[4,104,1024]{2,1,0:T(8,128)(2,1)}, u32[]{:S(2)}, u32[]{:S(2)}) collective-permute-start(bf16[4,104,1024]{2,1,0:T(8,128)(2,1)S(1)} %pad_maximum_fusion.refs_0_), channel_id=1, source_target_pairs={{0,16},{1,5},{2,18},{3,7},{4,20},{5,1},{6,22},{7,3},{8,24},{9,13},... | collective-permute-start | bytes 2555912 | tf_op jit(solution)/shard_map/ppermute | solution.py:324
  49.5 2.1 %collective-permute-start.8 = (bf16[4,104,1024]{2,1,0:T(8,128)(2,1)S(1)}, bf16[4,104,1024]{2,1,0:T(8,128)(2,1)}, u32[]{:S(2)}, u32[]{:S(2)}) collective-permute-start(bf16[4,104,1024]{2,1,0:T(8,128)(2,1)S(1)} %pad_maximum_fusion.refs_0_), channel_id=1, source_target_pairs={{0,24},{1,7},{2,26},{3,1},{4,28},{5,3},{6,30},{7,5},{8,0},{9,15},{... | collective-permute-start | bytes 2555912 | tf_op jit(solution)/shard_map/ppermute | solution.py:324
  51.6 7.6 %apply_maps.1 = bf16[1024,1024]{1,0:T(8,128)(2,1)S(1)} custom-call(bf16[1024,1024]{1,0:T(8,128)(2,1)S(1)} %bitcast.12, bf16[2,1024,1024]{2,1,0:T(8,128)(2,1)} %maps_ref.1), custom_call_target="tpu_custom_call" | custom-call | flops 4294967296 | bytes 8388608 | tf_op jit(solution)/shard_map/apply_maps/pallas_call | solution.py:124
  59.2 1.3 %copy-done.1 = bf16[1024,1024]{1,0:T(8,128)(2,1)} copy-done((bf16[1024,1024]{1,0:T(8,128)(2,1)}, bf16[1024,1024]{1,0:T(8,128)(2,1)S(1)}, u32[]{:S(2)}) %copy-start.1) | copy-done | bytes 2097176
  60.5 9.0 %all-to-all-start.1 = ((bf16[32,32,1024]{2,1,0:T(8,128)(2,1)}), bf16[32,32,1024]{2,1,0:T(8,128)(2,1)S(1)}, u32[]{:S(2)}, u32[]{:S(2)}) async-start(bf16[32,32,1024]{2,1,0:T(8,128)(2,1)} %bitcast.15), calls=%async_computation.1 | async-start | bytes 4194304 | tf_op jit(solution)/shard_map/all_to_all | solution.py:334
  70.2 7.5 %collective-permute-start.12 = (bf16[4,104,1024]{2,1,0:T(8,128)(2,1)}, bf16[4,104,1024]{2,1,0:T(8,128)(2,1)S(1)}, u32[]{:S(2)}, u32[]{:S(2)}) collective-permute-start(bf16[4,104,1024]{2,1,0:T(8,128)(2,1)} %collective-permute-done.8.refs_2_), channel_id=1, source_target_pairs={{0,1},{1,0},{2,3},{3,2},{4,5},{5,4},{6,7},{7,6},{8,9},{9,8},{10,11... | collective-permute-start | bytes 2555912 | tf_op jit(solution)/shard_map/ppermute | solution.py:328
  77.7 13.7 %collective-permute-start.11 = (bf16[4,104,1024]{2,1,0:T(8,128)(2,1)}, bf16[4,104,1024]{2,1,0:T(8,128)(2,1)S(1)}, u32[]{:S(2)}, u32[]{:S(2)}) collective-permute-start(bf16[4,104,1024]{2,1,0:T(8,128)(2,1)} %collective-permute-done.7.refs_1_), channel_id=1, source_target_pairs={{0,1},{1,0},{2,3},{3,2},{4,5},{5,4},{6,7},{7,6},{8,9},{9,8},{10,11... | collective-permute-start | bytes 2555912 | tf_op jit(solution)/shard_map/ppermute | solution.py:328
  91.4 2.2 %collective-permute-done.11.refs_5_ = bf16[4,104,1024]{2,1,0:T(8,128)(2,1)S(1)} collective-permute-done((bf16[4,104,1024]{2,1,0:T(8,128)(2,1)}, bf16[4,104,1024]{2,1,0:T(8,128)(2,1)S(1)}, u32[]{:S(2)}, u32[]{:S(2)}) %collective-permute-start.11) | collective-permute-done | bytes 852000 | tf_op jit(solution)/shard_map/ppermute | solution.py:328
  93.6 13.7 %fold.1 = (bf16[1024,1024]{1,0:T(8,128)(2,1)}, f32[8,1024]{1,0:T(8,128)S(1)}) custom-call(bf16[4,104,1024]{2,1,0:T(8,128)(2,1)S(1)} %pad_maximum_fusion.refs_0_, bf16[4,104,1024]{2,1,0:T(8,128)(2,1)} %collective-permute-done.7.refs_1_, bf16[4,104,1024]{2,1,0:T(8,128)(2,1)} %collective-permute-done.8.refs_2_, ...), custom_call_target="tpu_custom_call" | custom-call | flops 4294967296 | bytes 9437184 | tf_op jit(solution)/shard_map/fold/pallas_call | solution.py:262
  107.4 1.6 %copy-done.9 = bf16[1024,1024]{1,0:T(8,128)(2,1)S(1)} copy-done((bf16[1024,1024]{1,0:T(8,128)(2,1)S(1)}, bf16[1024,1024]{1,0:T(8,128)(2,1)}, u32[]{:S(2)}) %copy-start.9) | copy-done | bytes 2097176
  109.0 5.5 %finish.1 = f32[512,1024]{1,0:T(8,128)} custom-call(s32[1,512]{1,0:T(1,128)S(1)} %get-tuple-element.14.target_ref, bf16[1024,1024]{1,0:T(8,128)(2,1)S(1)} %bitcast.14, bf16[1024,1024]{1,0:T(8,128)(2,1)S(1)} %copy-done.9, f32[8,1024]{1,0:T(8,128)S(1)} %get-tuple-element.22.diag_ref), custom_call_target="tpu_custom_call" | custom-call | flops 2147483648 | bytes 6291456 | tf_op jit(solution)/shard_map/finish/pallas_call | solution.py:297
  (29 shorter events, 2.0 us)
Async XLA Ops:
  0.0 1.2 %copy-start.3 = (bf16[512,1024]{1,0:T(8,128)(2,1)S(1)}, bf16[512,1024]{1,0:T(8,128)(2,1)}, u32[]{:S(2)}) copy-start(bf16[512,1024]{1,0:T(8,128)(2,1)} %rows_ref.1) | copy-start | bytes 3145732
  1.2 0.8 copy-start.4
  2.1 0.7 copy-start.5
  2.7 0.7 copy-start.6
  3.4 0.7 copy-start.7
  4.1 0.7 copy-start.8
  7.1 1.3 %copy-start = (bf16[1024,1024]{1,0:T(8,128)(2,1)}, bf16[1024,1024]{1,0:T(8,128)(2,1)S(1)}, u32[]{:S(2)}) copy-start(bf16[1024,1024]{1,0:T(8,128)(2,1)S(1)} %get-tuple-element.15) | copy-start | bytes 6291460
  8.4 18.0 %copy-start.2 = (s32[3,1024]{1,0:T(4,128)S(1)}, s32[3,1024]{1,0:T(4,128)}, u32[]{:S(2)}) copy-start(s32[3,1024]{1,0:T(4,128)} %order_ref.3) | copy-start | bytes 36868
  8.4 43.2 %all-to-all-start = ((bf16[32,32,1024]{2,1,0:T(8,128)(2,1)}), bf16[32,32,1024]{2,1,0:T(8,128)(2,1)S(1)}, u32[]{:S(2)}, u32[]{:S(2)}) async-start(bf16[32,32,1024]{2,1,0:T(8,128)(2,1)} %bitcast.13), calls=%async_computation | async-start | bytes 4194304 | tf_op jit(solution)/shard_map/all_to_all | solution.py:334
  16.4 4.3 %collective-permute-start.2 = (bf16[40,1024]{1,0:T(8,128)(2,1)S(1)}, bf16[40,1024]{1,0:T(8,128)(2,1)S(1)}, u32[]{:S(2)}, u32[]{:S(2)}) collective-permute-start(bf16[40,1024]{1,0:T(8,128)(2,1)S(1)} %get-tuple-element.16.z0_ref), channel_id=1, source_target_pairs={{0,96},{32,64},{64,32},{96,0},{128,224},{160,192},{192,160},{224,1... | collective-permute-start | bytes 245768 | tf_op jit(solution)/shard_map/ppermute | solution.py:312
  18.1 6.5 %collective-permute-start.1 = (bf16[40,1024]{1,0:T(8,128)(2,1)S(1)}, bf16[40,1024]{1,0:T(8,128)(2,1)S(1)}, u32[]{:S(2)}, u32[]{:S(2)}) collective-permute-start(bf16[40,1024]{1,0:T(8,128)(2,1)S(1)} %get-tuple-element.16.z0_ref), channel_id=1, source_target_pairs={{0,64},{32,96},{64,0},{96,32},{128,192},{160,224},{192,128},{224,1... | collective-permute-start | bytes 245768 | tf_op jit(solution)/shard_map/ppermute | solution.py:312
  19.6 6.8 %collective-permute-start = (bf16[40,1024]{1,0:T(8,128)(2,1)S(1)}, bf16[40,1024]{1,0:T(8,128)(2,1)S(1)}, u32[]{:S(2)}, u32[]{:S(2)}) collective-permute-start(bf16[40,1024]{1,0:T(8,128)(2,1)S(1)} %get-tuple-element.16.z0_ref), channel_id=1, source_target_pairs={{0,32},{32,0},{64,96},{96,64},{128,160},{160,128},{192,224},{224,1... | collective-permute-start | bytes 245768 | tf_op jit(solution)/shard_map/ppermute | solution.py:312
  27.4 7.3 %collective-permute-start.3 = (bf16[40,1024]{1,0:T(8,128)(2,1)S(1)}, bf16[40,1024]{1,0:T(8,128)(2,1)S(1)}, u32[]{:S(2)}, u32[]{:S(2)}) collective-permute-start(bf16[40,1024]{1,0:T(8,128)(2,1)S(1)} %get-tuple-element.17), channel_id=1, source_target_pairs={{0,128},{32,160},{64,192},{96,224},{128,0},{160,32},{192,64},{224,... | collective-permute-start | bytes 245768 | tf_op jit(solution)/shard_map/ppermute | solution.py:312
  35.2 10.1 %collective-permute-start.6 = (bf16[104,1024]{1,0:T(8,128)(2,1)S(1)}, bf16[104,1024]{1,0:T(8,128)(2,1)S(1)}, u32[]{:S(2)}, u32[]{:S(2)}) collective-permute-start(bf16[104,1024]{1,0:T(8,128)(2,1)S(1)} %top_level.1), channel_id=1, source_target_pairs={{0,4},{1,17},{2,6},{3,19},{4,0},{5,21},{6,2},{7,23},{8,12},{9,25},... | collective-permute-start | bytes 638984 | tf_op jit(solution)/shard_map/ppermute | solution.py:324
  37.4 9.6 %collective-permute-start.5 = (bf16[104,1024]{1,0:T(8,128)(2,1)S(1)}, bf16[104,1024]{1,0:T(8,128)(2,1)S(1)}, u32[]{:S(2)}, u32[]{:S(2)}) collective-permute-start(bf16[104,1024]{1,0:T(8,128)(2,1)S(1)} %top_level.1), channel_id=1, source_target_pairs={{0,6},{1,25},{2,0},{3,27},{4,2},{5,29},{6,4},{7,31},{8,14},{9,1},{... | collective-permute-start | bytes 638984 | tf_op jit(solution)/shard_map/ppermute | solution.py:324
  38.2 8.8 %collective-permute-start.4 = (bf16[104,1024]{1,0:T(8,128)(2,1)S(1)}, bf16[104,1024]{1,0:T(8,128)(2,1)S(1)}, u32[]{:S(2)}, u32[]{:S(2)}) collective-permute-start(bf16[104,1024]{1,0:T(8,128)(2,1)S(1)} %top_level.1), channel_id=1, source_target_pairs={{0,2},{1,9},{2,4},{3,11},{4,6},{5,13},{6,0},{7,15},{8,10},{9,17},{... | collective-permute-start | bytes 638984 | tf_op jit(solution)/shard_map/ppermute | solution.py:324
  47.1 22.8 %collective-permute-start.9 = (bf16[4,104,1024]{2,1,0:T(8,128)(2,1)S(1)}, bf16[4,104,1024]{2,1,0:T(8,128)(2,1)}, u32[]{:S(2)}, u32[]{:S(2)}) collective-permute-start(bf16[4,104,1024]{2,1,0:T(8,128)(2,1)S(1)} %pad_maximum_fusion.refs_0_), channel_id=1, source_target_pairs={{0,16},{1,5},{2,18},{3,7},{4,20},{5,1},{6,22},{7,3},{8,24},{9,13},... | collective-permute-start | bytes 2555912 | tf_op jit(solution)/shard_map/ppermute | solution.py:324
  49.5 20.7 %collective-permute-start.8 = (bf16[4,104,1024]{2,1,0:T(8,128)(2,1)S(1)}, bf16[4,104,1024]{2,1,0:T(8,128)(2,1)}, u32[]{:S(2)}, u32[]{:S(2)}) collective-permute-start(bf16[4,104,1024]{2,1,0:T(8,128)(2,1)S(1)} %pad_maximum_fusion.refs_0_), channel_id=1, source_target_pairs={{0,24},{1,7},{2,26},{3,1},{4,28},{5,3},{6,30},{7,5},{8,0},{9,15},{... | collective-permute-start | bytes 2555912 | tf_op jit(solution)/shard_map/ppermute | solution.py:324
  51.6 26.1 %collective-permute-start.7 = (bf16[4,104,1024]{2,1,0:T(8,128)(2,1)S(1)}, bf16[4,104,1024]{2,1,0:T(8,128)(2,1)}, u32[]{:S(2)}, u32[]{:S(2)}) collective-permute-start(bf16[4,104,1024]{2,1,0:T(8,128)(2,1)S(1)} %pad_maximum_fusion.refs_0_), channel_id=1, source_target_pairs={{0,8},{1,3},{2,10},{3,5},{4,12},{5,7},{6,14},{7,1},{8,16},{9,11},{... | collective-permute-start | bytes 2555912 | tf_op jit(solution)/shard_map/ppermute | solution.py:324
  59.2 1.3 %copy-start.1 = (bf16[1024,1024]{1,0:T(8,128)(2,1)}, bf16[1024,1024]{1,0:T(8,128)(2,1)S(1)}, u32[]{:S(2)}) copy-start(bf16[1024,1024]{1,0:T(8,128)(2,1)S(1)} %apply_maps.1) | copy-start | bytes 6291460
  60.5 46.9 %all-to-all-start.1 = ((bf16[32,32,1024]{2,1,0:T(8,128)(2,1)}), bf16[32,32,1024]{2,1,0:T(8,128)(2,1)S(1)}, u32[]{:S(2)}, u32[]{:S(2)}) async-start(bf16[32,32,1024]{2,1,0:T(8,128)(2,1)} %bitcast.15), calls=%async_computation.1 | async-start | bytes 4194304 | tf_op jit(solution)/shard_map/all_to_all | solution.py:334
  69.5 21.9 %collective-permute-start.10 = (bf16[4,104,1024]{2,1,0:T(8,128)(2,1)S(1)}, bf16[4,104,1024]{2,1,0:T(8,128)(2,1)S(1)}, u32[]{:S(2)}, u32[]{:S(2)}) collective-permute-start(bf16[4,104,1024]{2,1,0:T(8,128)(2,1)S(1)} %pad_maximum_fusion.refs_0_), channel_id=1, source_target_pairs={{0,1},{1,0},{2,3},{3,2},{4,5},{5,4},{6,7},{7,6},{8,9},{9,8},{10,11... | collective-permute-start | bytes 2555912 | tf_op jit(solution)/shard_map/ppermute | solution.py:328
  69.9 21.5 %collective-permute-start.13 = (bf16[4,104,1024]{2,1,0:T(8,128)(2,1)}, bf16[4,104,1024]{2,1,0:T(8,128)(2,1)S(1)}, u32[]{:S(2)}, u32[]{:S(2)}) collective-permute-start(bf16[4,104,1024]{2,1,0:T(8,128)(2,1)} %collective-permute-done.9.refs_3_), channel_id=1, source_target_pairs={{0,1},{1,0},{2,3},{3,2},{4,5},{5,4},{6,7},{7,6},{8,9},{9,8},{10,11... | collective-permute-start | bytes 2555912 | tf_op jit(solution)/shard_map/ppermute | solution.py:328
  70.2 21.2 %collective-permute-start.12 = (bf16[4,104,1024]{2,1,0:T(8,128)(2,1)}, bf16[4,104,1024]{2,1,0:T(8,128)(2,1)S(1)}, u32[]{:S(2)}, u32[]{:S(2)}) collective-permute-start(bf16[4,104,1024]{2,1,0:T(8,128)(2,1)} %collective-permute-done.8.refs_2_), channel_id=1, source_target_pairs={{0,1},{1,0},{2,3},{3,2},{4,5},{5,4},{6,7},{7,6},{8,9},{9,8},{10,11... | collective-permute-start | bytes 2555912 | tf_op jit(solution)/shard_map/ppermute | solution.py:328
  77.7 15.9 %collective-permute-start.11 = (bf16[4,104,1024]{2,1,0:T(8,128)(2,1)}, bf16[4,104,1024]{2,1,0:T(8,128)(2,1)S(1)}, u32[]{:S(2)}, u32[]{:S(2)}) collective-permute-start(bf16[4,104,1024]{2,1,0:T(8,128)(2,1)} %collective-permute-done.7.refs_1_), channel_id=1, source_target_pairs={{0,1},{1,0},{2,3},{3,2},{4,5},{5,4},{6,7},{7,6},{8,9},{9,8},{10,11... | collective-permute-start | bytes 2555912 | tf_op jit(solution)/shard_map/ppermute | solution.py:328
  91.4 2.2 %copy-start.10 = (bf16[4,104,1024]{2,1,0:T(8,128)(2,1)}, bf16[4,104,1024]{2,1,0:T(8,128)(2,1)S(1)}, u32[]{:S(2)}) copy-start(bf16[4,104,1024]{2,1,0:T(8,128)(2,1)S(1)} %collective-permute-done.13.refs_7_) | copy-start | bytes 2555908
  107.4 1.6 %copy-start.9 = (bf16[1024,1024]{1,0:T(8,128)(2,1)S(1)}, bf16[1024,1024]{1,0:T(8,128)(2,1)}, u32[]{:S(2)}) copy-start(bf16[1024,1024]{1,0:T(8,128)(2,1)} %get-tuple-element.21.f_ref) | copy-start | bytes 6291460

commit v2 on v1

--- a/solution.py
+++ b/solution.py
@@ -36,6 +36,14 @@
     return pl.CostEstimate(flops=flops, bytes_accessed=nbytes, transcendentals=0)
 
 
+def hbm(value):
+    return pltpu.with_memory_space_constraint(value, pltpu.HBM)
+
+
+def whole(*shape):
+    return pl.BlockSpec(shape, lambda i: (0,) * len(shape))
+
+
 def split(value, parts):
     pieces = []
     for _ in range(parts):
@@ -58,7 +66,24 @@
     return iota((OWN, PORTS), 1) == own * OWN + iota((OWN, PORTS), 0)
 
 
-def prep_kernel(owner_ref, half_ref, port_ref, rows_ref, off_ref, diag_ref, out_ref, target_ref, z_ref, stim):
+def label_kernel(off_ref, diag_ref, z_ref):
+    z_ref[:OWN, :] = off_ref[...]
+    diag = jnp.sum(jnp.where(iota((OWN, OWN), 0) == iota((OWN, OWN), 1), diag_ref[...], 0.0), axis=1, keepdims=True)
+    placed = jnp.sum(jnp.where(own_lanes(), diag, 0.0), axis=0, keepdims=True)
+    z_ref[OWN:, :] = rows_of(split(placed, 3), DROWS)
+
+
+def label(off, diag):
+    return pl.pallas_call(
+        label_kernel,
+        out_shape=jax.ShapeDtypeStruct((ZROWS, PORTS), BF16),
+        compiler_params=params(),
+        cost_estimate=cost(OWN * PORTS, 1 << 17),
+        name="label",
+    )(hbm(off), hbm(diag))
+
+
+def prep_kernel(owner_ref, half_ref, port_ref, rows_ref, z_ref, out_ref, target_ref, stim):
     step = pl.program_id(0)
     tile = out_ref.shape[0]
 
@@ -75,47 +100,40 @@
             lanes = slice(128 * j, 128 * j + 128)
             bump = jnp.where(iota((ROWS, 128), 1) + 128 * j == port, 8.0, 0.0)
             stim[:, lanes] = (rows_ref[:, lanes].astype(F32) + bump).astype(BF16)
-        z_ref[:OWN, :] = off_ref[...]
-        diag = jnp.sum(
-            jnp.where(iota((OWN, OWN), 0) == iota((OWN, OWN), 1), diag_ref[...], 0.0), axis=1, keepdims=True
-        )
-        placed = jnp.sum(jnp.where(own_lanes(), diag, 0.0), axis=0, keepdims=True)
-        z_ref[OWN:, :] = rows_of(split(placed, 3), DROWS)
 
     scale = jnp.where(half_ref[...] == 1, HALF_SCALE, 1.0)
     route = jnp.where(iota((tile, ROWS), 0) + step * tile == target_ref[...], scale, 0.0).astype(BF16)
     out_ref[...] = jnp.dot(route, stim[...], preferred_element_type=F32).astype(BF16)
 
 
-def prep(owner, half, port, rows, off, diag):
+def prep(owner, half, port, rows, z):
     tile = 256
-    whole = lambda *shape: pl.BlockSpec(shape, lambda i: (0,) * len(shape))
     return pl.pallas_call(
         prep_kernel,
         grid=(SLOTS // tile,),
         in_specs=[
-            whole(1, ROWS), whole(1, ROWS), whole(1, ROWS), whole(ROWS, PORTS), whole(OWN, PORTS), whole(1, OWN),
-        ],
-        out_specs=[pl.BlockSpec((tile, PORTS), lambda i: (i, 0)), whole(1, ROWS), whole(ZROWS, PORTS)],
-        out_shape=[
-            jax.ShapeDtypeStruct((SLOTS, PORTS), BF16),
-            jax.ShapeDtypeStruct((1, ROWS), I32),
-            jax.ShapeDtypeStruct((ZROWS, PORTS), BF16),
-        ],
+            whole(1, ROWS), whole(1, ROWS), whole(1, ROWS), whole(ROWS, PORTS), pl.BlockSpec(memory_space=pl.ANY),
+        ],
+        out_specs=[pl.BlockSpec((tile, PORTS), lambda i: (i, 0)), whole(1, ROWS)],
+        out_shape=[pltpu.HBM((SLOTS, PORTS), BF16), jax.ShapeDtypeStruct((1, ROWS), I32)],
         scratch_shapes=[pltpu.VMEM((ROWS, PORTS), BF16)],
         compiler_params=params(),
         cost_estimate=cost(2 * SLOTS * ROWS * PORTS, 4 << 20),
         name="prep",
-    )(owner, half, port, rows, off, diag)
-
-
-def maps_kernel(x_ref, maps_ref, out_ref):
-    x = x_ref[...]
-    second = jnp.max(jnp.abs(x.astype(F32)), axis=1, keepdims=True) > HALF_MARK
-    first_rows = jnp.where(second, 0.0, x.astype(F32)).astype(BF16)
-    second_rows = jnp.where(second, x.astype(F32) * (1.0 / HALF_SCALE), 0.0).astype(BF16)
-    acc = jnp.dot(first_rows, maps_ref[0], preferred_element_type=F32)
-    acc = acc + jnp.dot(second_rows, maps_ref[1], preferred_element_type=F32)
+    )(hbm(owner), hbm(half), hbm(port), hbm(rows), z)
+
+
+def maps_kernel(x_ref, maps_ref, out_ref, first, other):
+    @pl.when(pl.program_id(0) == 0)
+    def _():
+        for r in range(0, SLOTS, 256):
+            x = x_ref[r : r + 256, :].astype(F32)
+            second = jnp.max(jnp.abs(x), axis=1, keepdims=True) > HALF_MARK
+            first[r : r + 256, :] = jnp.where(second, 0.0, x).astype(BF16)
+            other[r : r + 256, :] = jnp.where(second, x * (1.0 / HALF_SCALE), 0.0).astype(BF16)
+
+    acc = jnp.dot(first[...], maps_ref[0], preferred_element_type=F32)
+    acc = acc + jnp.dot(other[...], maps_ref[1], preferred_element_type=F32)
     out_ref[...] = acc.astype(BF16)
 
 
@@ -123,17 +141,15 @@
     tile = 256
     return pl.pallas_call(
         maps_kernel,
-        grid=(SLOTS // tile,),
-        in_specs=[
-            pl.BlockSpec((tile, PORTS), lambda i: (i, 0)),
-            pl.BlockSpec((2, PORTS, PORTS), lambda i: (0, 0, 0)),
-        ],
-        out_specs=pl.BlockSpec((tile, PORTS), lambda i: (i, 0)),
-        out_shape=jax.ShapeDtypeStruct((SLOTS, PORTS), BF16),
+        grid=(PORTS // tile,),
+        in_specs=[whole(SLOTS, PORTS), pl.BlockSpec((2, PORTS, tile), lambda i: (0, 0, i))],
+        out_specs=pl.BlockSpec((SLOTS, tile), lambda i: (0, i)),
+        out_shape=pltpu.HBM((SLOTS, PORTS), BF16),
+        scratch_shapes=[pltpu.VMEM((SLOTS, PORTS), BF16), pltpu.VMEM((SLOTS, PORTS), BF16)],
         compiler_params=params(),
         cost_estimate=cost(4 * SLOTS * PORTS * PORTS, 8 << 20),
         name="apply_maps",
-    )(x, maps)
+    )(x, hbm(maps))
 
 
 def permuted(values, order):
@@ -211,7 +227,7 @@
 
 
 def fold_kernel(*refs):
-    parts, (f_ref, diag_ref, held, marks, mid, sems) = refs[:8], refs[8:]
+    parts, (f_ref, diag_ref, held, marks, sems) = refs[:8], refs[8:]
     own = lax.axis_index("owner")
     core, x, y = own & 1, (own >> 1) & 3, own >> 3
     copies = []
@@ -244,68 +260,78 @@
     r = iota((DROWS, PORTS), 0)
     diag_ref[...] = jnp.where(r == 0, inv0, jnp.where(r == 1, inv3, 0.0))
     tile = 256
-
-    @pl.loop(0, PORTS // tile)
-    def _(t):
-        at = pl.ds(pl.multiple_of(t * tile, tile), tile)
-        acc = jnp.dot(held[1, at, :], held[0], preferred_element_type=F32)
-        on = iota((tile, PORTS), 1) == iota((tile, PORTS), 0) + t * tile
-        mid[at, :] = (jnp.where(on, ratio, 0.0) - acc).astype(BF16)
-
-    @pl.loop(0, PORTS // tile)
-    def _(t):
-        at = pl.ds(pl.multiple_of(t * tile, tile), tile)
-        f_ref[at, :] = jnp.dot(held[2, at, :], mid[...], preferred_element_type=F32).astype(BF16)
+    for t in range(0, PORTS, tile):
+        acc = jnp.dot(held[1], held[0, :, t : t + tile], preferred_element_type=F32)
+        on = iota((PORTS, tile), 0) == iota((PORTS, tile), 1) + t
+        mid = (jnp.where(on, ratio[:, t : t + tile], 0.0) - acc).astype(BF16)
+        f_ref[:, t : t + tile] = jnp.dot(held[2], mid, preferred_element_type=F32).astype(BF16)
 
 
 def fold(parts):
     return pl.pallas_call(
         fold_kernel,
         in_specs=[pl.BlockSpec(memory_space=pl.ANY)] * 8,
-        out_shape=[jax.ShapeDtypeStruct((PORTS, PORTS), BF16), jax.ShapeDtypeStruct((DROWS, PORTS), F32)],
+        out_shape=[pltpu.HBM((PORTS, PORTS), BF16), jax.ShapeDtypeStruct((DROWS, PORTS), F32)],
         scratch_shapes=[
             pltpu.VMEM((3, PORTS, PORTS), BF16),
             pltpu.VMEM((32, DROWS, PORTS), BF16),
-            pltpu.VMEM((PORTS, PORTS), BF16),
             pltpu.SemaphoreType.DMA((4,)),
         ],
-        compiler_params=params(),
+        compiler_params=params(32),
         cost_estimate=cost(4 * PORTS**3, 9 << 20),
         name="fold",
     )(*parts)
 
 
-def finish_kernel(target_ref, ret_ref, f_ref, diag_ref, out_ref):
-    tile = out_ref.shape[0]
-    target = jnp.transpose(jnp.broadcast_to(target_ref[...], (128, tile)))
-    route = jnp.concatenate(
-        [
-            jnp.where(iota((tile, 128), 1) + 128 * j == target, 1.0, 0.0).astype(BF16)
-            for j in range(SLOTS // 128)
-        ],
-        axis=1,
-    )
-    response = jnp.dot(route, ret_ref[...], preferred_element_type=F32)
-    scaled = (response * diag_ref[0:1, :]).astype(BF16)
-    coupled = lax.dot_general(scaled, f_ref[...], (((1,), (1,)), ((), ())), preferred_element_type=F32)
-    out_ref[...] = response * diag_ref[1:2, :] - coupled
+def finish_kernel(target_ref, ret_ref, f_ref, diag_ref, out_ref, route, response, scaled):
+    step = pl.program_id(0)
+    tile = ret_ref.shape[1]
+    steps = PORTS // tile
+
+    @pl.when(step == 0)
+    def _():
+        target = jnp.transpose(jnp.broadcast_to(target_ref[...], (128, ROWS)))
+        for j in range(0, SLOTS, 128):
+            route[:, j : j + 128] = jnp.where(iota((ROWS, 128), 1) + j == target, 1.0, 0.0).astype(BF16)
+
+    @pl.when(step < steps)
+    def _():
+        at = pl.ds(pl.multiple_of(step * tile, tile), tile)
+        piece = jnp.dot(route[...], ret_ref[...], preferred_element_type=F32)
+        response[:, at] = piece
+        scaled[:, at] = (piece * diag_ref[0:1, at]).astype(BF16)
+
+    @pl.when(step >= steps)
+    def _():
+        at = pl.ds(pl.multiple_of((step - steps) * tile, tile), tile)
+        coupled = lax.dot_general(scaled[...], f_ref[...], (((1,), (1,)), ((), ())), preferred_element_type=F32)
+        out_ref[...] = response[:, at] * diag_ref[1:2, at] - coupled
 
 
 def finish(target, returned, f, diag):
-    tile = 128
-    whole = lambda *shape: pl.BlockSpec(shape, lambda i: (0,) * len(shape))
+    tile = 256
+    steps = PORTS // tile
+    late = lambda i: jnp.maximum(i - steps, 0)
     return pl.pallas_call(
         finish_kernel,
-        grid=(ROWS // tile,),
+        grid=(2 * steps,),
         in_specs=[
-            pl.BlockSpec((1, tile), lambda i: (0, i)), whole(SLOTS, PORTS), whole(PORTS, PORTS), whole(DROWS, PORTS),
-        ],
-        out_specs=pl.BlockSpec((tile, PORTS), lambda i: (i, 0)),
-        out_shape=jax.ShapeDtypeStruct((ROWS, PORTS), F32),
+            whole(1, ROWS),
+            pl.BlockSpec((SLOTS, tile), lambda i: (0, jnp.minimum(i, steps - 1))),
+            pl.BlockSpec((tile, PORTS), lambda i: (late(i), 0)),
+            whole(DROWS, PORTS),
+        ],
+        out_specs=pl.BlockSpec((ROWS, tile), lambda i: (0, late(i))),
+        out_shape=pltpu.HBM((ROWS, PORTS), F32),
+        scratch_shapes=[
+            pltpu.VMEM((ROWS, SLOTS), BF16),
+            pltpu.VMEM((ROWS, PORTS), F32),
+            pltpu.VMEM((ROWS, PORTS), BF16),
+        ],
         compiler_params=params(),
         cost_estimate=cost(4 * ROWS * PORTS * PORTS, 6 << 20),
         name="finish",
-    )(target, returned, f, diag)
+    )(target, returned, hbm(f), diag)
 
 
 def group_swap(value, mask):
@@ -335,16 +361,12 @@
 
 
 def body(port_rows, defect_owner, defect_half, defect_port, subcircuit_maps, schur_off, schur_diag, pivot_order):
-    outgoing, target, z0 = prep(
-        defect_owner.reshape(1, ROWS),
-        defect_half.reshape(1, ROWS),
-        defect_port.reshape(1, ROWS),
-        port_rows,
-        schur_off,
-        schur_diag.reshape(1, OWN),
+    z0 = label(schur_off, schur_diag.reshape(1, OWN))
+    z1, z2, z3 = (group_swap(z0, mask) for mask in (1, 2, 3))
+    outgoing, target = prep(
+        defect_owner.reshape(1, ROWS), defect_half.reshape(1, ROWS), defect_port.reshape(1, ROWS), port_rows, z0
     )
     arrived = exchange(outgoing)
-    z1, z2, z3 = (group_swap(z0, mask) for mask in (1, 2, 3))
     z, off, diag, gb = low_levels(z0, z1, z2, z3, pivot_order)
     pack = top_level(group_swap(z, 4), off, diag, gb, pivot_order)
     line = jnp.stack([pack] + [chip_shift(pack, step, 0) for step in STEPS])

time: 115 us -> 114 us (level)
  the two profiles are of different devices: /device:TPU:41 before, /device:TPU:1 now
where the time goes in v2:
time: 114 us; the launch traced here: 112 us
  starting transfers between devices  56.1 us (49%)
  Pallas kernels  36.3 us (32%)
  waiting for transfers between devices  19.5 us (17%)
    ppermute x4, starting transfers between devices, core_swap(): return lax.ppermute(value, 'owner', [(o, o ^ 1) for o in range(OWNERS)])  20.7 us
    all_to_all x2, starting transfers between devices, exchange(): lax.all_to_all(value, 'owner', split_axis=0, concat_axis=0, tiled=True)  16.7 us
    pallas_call x1, Pallas kernels, fold(): pl.pallas_call(fold_kernel, in_specs=[pl.BlockSpec(memory_space=pl.ANY)]...  13.6 us
    ppermute x4, starting transfers between devices, group_swap(): return lax.ppermute(value, 'group', [(i, i ^ mask) for i in range(8)])  10.7 us
    ppermute x6, waiting for transfers between devices, chip_shift(): return lax.ppermute(value, 'owner', pairs)  8.83 us
    ppermute x4, waiting for transfers between devices, group_swap(): return lax.ppermute(value, 'group', [(i, i ^ mask) for i in range(8)])  8.49 us
    pallas_call x1, Pallas kernels, apply_maps(): pl.pallas_call(maps_kernel, grid=(PORTS // tile,), in_specs=[whole(SLOTS,...  8.06 us
    ppermute x6, starting transfers between devices, chip_shift(): return lax.ppermute(value, 'owner', pairs)  8.03 us
  transfers between devices with their start and end apart: 16, of which 8 were waited for; matrix products, arithmetic and copies ran while one was open for 0% of the time, Pallas kernels for 21%

profile of v2, /device:TPU:1, one launch (start us, length us, event | category | flops | bytes accessed | tf_op | source)
XLA Modules:
  0.0 112.2 jit_solution(1476866416296249537)
XLA Ops:
  0.0 0.9 label.1.z_ref.z0_ref
  1.0 4.7 %prep.1 = (bf16[1024,1024]{1,0:T(8,128)(2,1)}, s32[1,512]{1,0:T(1,128)S(1)}) custom-call(s32[1,512]{1,0:T(1,128)} %bitcast.21, s32[1,512]{1,0:T(1,128)} %bitcast.22, s32[1,512]{1,0:T(1,128)} %bitcast.23, bf16[512,1024]{1,0:T(8,128)(2,1)} %rows_ref.1, bf16[40,1024]{1,0:T(8,128)(2,1)S(1)} %label.1.z_ref.z0_ref), custom_call_target="tpu_custom_call" | custom-call | flops 1073741824 | bytes 4194304 | tf_op jit(solution)/shard_map/prep/pallas_call | solution.py:111
  5.7 8.7 %all-to-all-start = ((bf16[32,32,1024]{2,1,0:T(8,128)(2,1)}), bf16[32,32,1024]{2,1,0:T(8,128)(2,1)S(1)}, u32[]{:S(2)}, u32[]{:S(2)}) async-start(bf16[32,32,1024]{2,1,0:T(8,128)(2,1)} %bitcast.15), calls=%async_computation | async-start | bytes 4194304 | tf_op jit(solution)/shard_map/all_to_all | solution.py:360
  14.4 4.4 %collective-permute-start.2 = (bf16[40,1024]{1,0:T(8,128)(2,1)S(1)}, bf16[40,1024]{1,0:T(8,128)(2,1)S(1)}, u32[]{:S(2)}, u32[]{:S(2)}) collective-permute-start(bf16[40,1024]{1,0:T(8,128)(2,1)S(1)} %label.1.z_ref.z0_ref), channel_id=1, source_target_pairs={{0,96},{32,64},{64,32},{96,0},{128,224},{160,192},{192,160},{224,1... | collective-permute-start | bytes 245768 | tf_op jit(solution)/shard_map/ppermute | solution.py:338
  18.8 0.4 collective-permute-start
  19.2 2.3 %collective-permute-done.2.z3_ref = bf16[40,1024]{1,0:T(8,128)(2,1)S(1)} collective-permute-done((bf16[40,1024]{1,0:T(8,128)(2,1)S(1)}, bf16[40,1024]{1,0:T(8,128)(2,1)S(1)}, u32[]{:S(2)}, u32[]{:S(2)}) %collective-permute-start.2) | collective-permute-done | bytes 81952 | tf_op jit(solution)/shard_map/ppermute | solution.py:338
  21.5 4.0 %collective-permute-done.1.z2_ref = bf16[40,1024]{1,0:T(8,128)(2,1)S(1)} collective-permute-done((bf16[40,1024]{1,0:T(8,128)(2,1)S(1)}, bf16[40,1024]{1,0:T(8,128)(2,1)S(1)}, u32[]{:S(2)}, u32[]{:S(2)}) %collective-permute-start.1) | collective-permute-done | bytes 81952 | tf_op jit(solution)/shard_map/ppermute | solution.py:338
  25.5 1.0 low_levels.1
  26.5 5.9 %collective-permute-start.3 = (bf16[40,1024]{1,0:T(8,128)(2,1)S(1)}, bf16[40,1024]{1,0:T(8,128)(2,1)S(1)}, u32[]{:S(2)}, u32[]{:S(2)}) collective-permute-start(bf16[40,1024]{1,0:T(8,128)(2,1)S(1)} %get-tuple-element.15), channel_id=1, source_target_pairs={{0,128},{32,160},{64,192},{96,224},{128,0},{160,32},{192,64},{224,... | collective-permute-start | bytes 245768 | tf_op jit(solution)/shard_map/ppermute | solution.py:338
  32.4 2.2 %collective-permute-done.3.z4_ref = bf16[40,1024]{1,0:T(8,128)(2,1)S(1)} collective-permute-done((bf16[40,1024]{1,0:T(8,128)(2,1)S(1)}, bf16[40,1024]{1,0:T(8,128)(2,1)S(1)}, u32[]{:S(2)}, u32[]{:S(2)}) %collective-permute-start.3) | collective-permute-done | bytes 81952 | tf_op jit(solution)/shard_map/ppermute | solution.py:338
  34.6 0.5 top_level.1
  35.1 2.9 %collective-permute-start.6 = (bf16[104,1024]{1,0:T(8,128)(2,1)S(1)}, bf16[104,1024]{1,0:T(8,128)(2,1)S(1)}, u32[]{:S(2)}, u32[]{:S(2)}) collective-permute-start(bf16[104,1024]{1,0:T(8,128)(2,1)S(1)} %top_level.1), channel_id=1, source_target_pairs={{0,4},{1,17},{2,6},{3,19},{4,0},{5,21},{6,2},{7,23},{8,12},{9,25},... | collective-permute-start | bytes 638984 | tf_op jit(solution)/shard_map/ppermute | solution.py:350
  38.0 0.9 collective-permute-start.5
  38.9 0.6 collective-permute-start.4
  39.5 3.7 %collective-permute-done.6 = bf16[104,1024]{1,0:T(8,128)(2,1)S(1)} collective-permute-done((bf16[104,1024]{1,0:T(8,128)(2,1)S(1)}, bf16[104,1024]{1,0:T(8,128)(2,1)S(1)}, u32[]{:S(2)}, u32[]{:S(2)}) %collective-permute-start.6) | collective-permute-done | bytes 213024 | tf_op jit(solution)/shard_map/ppermute | solution.py:350
  43.2 1.9 %collective-permute-done.5 = bf16[104,1024]{1,0:T(8,128)(2,1)S(1)} collective-permute-done((bf16[104,1024]{1,0:T(8,128)(2,1)S(1)}, bf16[104,1024]{1,0:T(8,128)(2,1)S(1)}, u32[]{:S(2)}, u32[]{:S(2)}) %collective-permute-start.5) | collective-permute-done | bytes 213024 | tf_op jit(solution)/shard_map/ppermute | solution.py:350
  45.1 0.9 collective-permute-done.4
  46.0 0.1 pad_maximum_fusion.refs_0_
  46.1 2.2 %collective-permute-start.9 = (bf16[4,104,1024]{2,1,0:T(8,128)(2,1)S(1)}, bf16[4,104,1024]{2,1,0:T(8,128)(2,1)}, u32[]{:S(2)}, u32[]{:S(2)}) collective-permute-start(bf16[4,104,1024]{2,1,0:T(8,128)(2,1)S(1)} %pad_maximum_fusion.refs_0_), channel_id=1, source_target_pairs={{0,16},{1,5},{2,18},{3,7},{4,20},{5,1},{6,22},{7,3},{8,24},{9,13},... | collective-permute-start | bytes 2555912 | tf_op jit(solution)/shard_map/ppermute | solution.py:350
  48.3 1.0 collective-permute-start.8
  49.3 0.4 collective-permute-start.7
  49.7 8.1 %apply_maps.1 = bf16[1024,1024]{1,0:T(8,128)(2,1)} custom-call(bf16[1024,1024]{1,0:T(8,128)(2,1)S(1)} %bitcast.12, bf16[2,1024,1024]{2,1,0:T(8,128)(2,1)} %maps_ref.1), custom_call_target="tpu_custom_call" | custom-call | flops 4294967296 | bytes 8388608 | tf_op jit(solution)/shard_map/apply_maps/pallas_call | solution.py:142
  57.8 8.0 %all-to-all-start.1 = ((bf16[32,32,1024]{2,1,0:T(8,128)(2,1)}), bf16[32,32,1024]{2,1,0:T(8,128)(2,1)S(1)}, u32[]{:S(2)}, u32[]{:S(2)}) async-start(bf16[32,32,1024]{2,1,0:T(8,128)(2,1)} %bitcast.16), calls=%async_computation.1 | async-start | bytes 4194304 | tf_op jit(solution)/shard_map/all_to_all | solution.py:360
  65.8 0.3 collective-permute-start.10
  66.1 0.0 collective-permute-done.9.refs_3_
  66.1 0.3 collective-permute-start.13
  66.4 2.3 %collective-permute-done.8.refs_2_ = bf16[4,104,1024]{2,1,0:T(8,128)(2,1)} collective-permute-done((bf16[4,104,1024]{2,1,0:T(8,128)(2,1)S(1)}, bf16[4,104,1024]{2,1,0:T(8,128)(2,1)}, u32[]{:S(2)}, u32[]{:S(2)}) %collective-permute-start.8) | collective-permute-done | bytes 852000 | tf_op jit(solution)/shard_map/ppermute | solution.py:350
  68.7 14.5 %collective-permute-start.12 = (bf16[4,104,1024]{2,1,0:T(8,128)(2,1)}, bf16[4,104,1024]{2,1,0:T(8,128)(2,1)S(1)}, u32[]{:S(2)}, u32[]{:S(2)}) collective-permute-start(bf16[4,104,1024]{2,1,0:T(8,128)(2,1)} %collective-permute-done.8.refs_2_), channel_id=1, source_target_pairs={{0,1},{1,0},{2,3},{3,2},{4,5},{5,4},{6,7},{7,6},{8,9},{9,8},{10,11... | collective-permute-start | bytes 2555912 | tf_op jit(solution)/shard_map/ppermute | solution.py:354
  83.2 5.6 %collective-permute-start.11 = (bf16[4,104,1024]{2,1,0:T(8,128)(2,1)}, bf16[4,104,1024]{2,1,0:T(8,128)(2,1)S(1)}, u32[]{:S(2)}, u32[]{:S(2)}) collective-permute-start(bf16[4,104,1024]{2,1,0:T(8,128)(2,1)} %collective-permute-done.7.refs_1_), channel_id=1, source_target_pairs={{0,1},{1,0},{2,3},{3,2},{4,5},{5,4},{6,7},{7,6},{8,9},{9,8},{10,11... | collective-permute-start | bytes 2555912 | tf_op jit(solution)/shard_map/ppermute | solution.py:354
  88.8 2.2 %collective-permute-done.11.refs_5_ = bf16[4,104,1024]{2,1,0:T(8,128)(2,1)S(1)} collective-permute-done((bf16[4,104,1024]{2,1,0:T(8,128)(2,1)}, bf16[4,104,1024]{2,1,0:T(8,128)(2,1)S(1)}, u32[]{:S(2)}, u32[]{:S(2)}) %collective-permute-start.11) | collective-permute-done | bytes 852000 | tf_op jit(solution)/shard_map/ppermute | solution.py:354
  91.0 13.6 %fold.1 = (bf16[1024,1024]{1,0:T(8,128)(2,1)}, f32[8,1024]{1,0:T(8,128)S(1)}) custom-call(bf16[4,104,1024]{2,1,0:T(8,128)(2,1)S(1)} %pad_maximum_fusion.refs_0_, bf16[4,104,1024]{2,1,0:T(8,128)(2,1)} %collective-permute-done.7.refs_1_, bf16[4,104,1024]{2,1,0:T(8,128)(2,1)} %collective-permute-done.8.refs_2_, ...), custom_call_target="tpu_custom_call" | custom-call | flops 4294967296 | bytes 9437184 | tf_op jit(solution)/shard_map/fold/pallas_call | solution.py:271
  104.7 7.5 %finish.1 = f32[512,1024]{1,0:T(8,128)} custom-call(s32[1,512]{1,0:T(1,128)S(1)} %get-tuple-element.13.target_ref, bf16[1024,1024]{1,0:T(8,128)(2,1)S(1)} %bitcast.13, bf16[1024,1024]{1,0:T(8,128)(2,1)} %get-tuple-element.19.f_ref, f32[8,1024]{1,0:T(8,128)S(1)} %get-tuple-element.20.diag_ref), custom_call_target="tpu_custom_call" | custom-call | flops 2147483648 | bytes 6291456 | tf_op jit(solution)/shard_map/finish/pallas_call | solution.py:315
  (10 shorter events, 0.0 us)
Async XLA Ops:
  5.7 19.8 %copy-start = (s32[3,1024]{1,0:T(4,128)S(1)}, s32[3,1024]{1,0:T(4,128)}, u32[]{:S(2)}) copy-start(s32[3,1024]{1,0:T(4,128)} %order_ref.3) | copy-start | bytes 36868
  5.7 44.1 %all-to-all-start = ((bf16[32,32,1024]{2,1,0:T(8,128)(2,1)}), bf16[32,32,1024]{2,1,0:T(8,128)(2,1)S(1)}, u32[]{:S(2)}, u32[]{:S(2)}) async-start(bf16[32,32,1024]{2,1,0:T(8,128)(2,1)} %bitcast.15), calls=%async_computation | async-start | bytes 4194304 | tf_op jit(solution)/shard_map/all_to_all | solution.py:360
  14.4 7.1 %collective-permute-start.2 = (bf16[40,1024]{1,0:T(8,128)(2,1)S(1)}, bf16[40,1024]{1,0:T(8,128)(2,1)S(1)}, u32[]{:S(2)}, u32[]{:S(2)}) collective-permute-start(bf16[40,1024]{1,0:T(8,128)(2,1)S(1)} %label.1.z_ref.z0_ref), channel_id=1, source_target_pairs={{0,96},{32,64},{64,32},{96,0},{128,224},{160,192},{192,160},{224,1... | collective-permute-start | bytes 245768 | tf_op jit(solution)/shard_map/ppermute | solution.py:338
  18.8 6.7 %collective-permute-start.1 = (bf16[40,1024]{1,0:T(8,128)(2,1)S(1)}, bf16[40,1024]{1,0:T(8,128)(2,1)S(1)}, u32[]{:S(2)}, u32[]{:S(2)}) collective-permute-start(bf16[40,1024]{1,0:T(8,128)(2,1)S(1)} %label.1.z_ref.z0_ref), channel_id=1, source_target_pairs={{0,64},{32,96},{64,0},{96,32},{128,192},{160,224},{192,128},{224,1... | collective-permute-start | bytes 245768 | tf_op jit(solution)/shard_map/ppermute | solution.py:338
  18.8 6.7 %collective-permute-start = (bf16[40,1024]{1,0:T(8,128)(2,1)S(1)}, bf16[40,1024]{1,0:T(8,128)(2,1)S(1)}, u32[]{:S(2)}, u32[]{:S(2)}) collective-permute-start(bf16[40,1024]{1,0:T(8,128)(2,1)S(1)} %label.1.z_ref.z0_ref), channel_id=1, source_target_pairs={{0,32},{32,0},{64,96},{96,64},{128,160},{160,128},{192,224},{224,1... | collective-permute-start | bytes 245768 | tf_op jit(solution)/shard_map/ppermute | solution.py:338
  26.5 8.1 %collective-permute-start.3 = (bf16[40,1024]{1,0:T(8,128)(2,1)S(1)}, bf16[40,1024]{1,0:T(8,128)(2,1)S(1)}, u32[]{:S(2)}, u32[]{:S(2)}) collective-permute-start(bf16[40,1024]{1,0:T(8,128)(2,1)S(1)} %get-tuple-element.15), channel_id=1, source_target_pairs={{0,128},{32,160},{64,192},{96,224},{128,0},{160,32},{192,64},{224,... | collective-permute-start | bytes 245768 | tf_op jit(solution)/shard_map/ppermute | solution.py:338
  35.1 8.1 %collective-permute-start.6 = (bf16[104,1024]{1,0:T(8,128)(2,1)S(1)}, bf16[104,1024]{1,0:T(8,128)(2,1)S(1)}, u32[]{:S(2)}, u32[]{:S(2)}) collective-permute-start(bf16[104,1024]{1,0:T(8,128)(2,1)S(1)} %top_level.1), channel_id=1, source_target_pairs={{0,4},{1,17},{2,6},{3,19},{4,0},{5,21},{6,2},{7,23},{8,12},{9,25},... | collective-permute-start | bytes 638984 | tf_op jit(solution)/shard_map/ppermute | solution.py:350
  38.0 7.0 %collective-permute-start.5 = (bf16[104,1024]{1,0:T(8,128)(2,1)S(1)}, bf16[104,1024]{1,0:T(8,128)(2,1)S(1)}, u32[]{:S(2)}, u32[]{:S(2)}) collective-permute-start(bf16[104,1024]{1,0:T(8,128)(2,1)S(1)} %top_level.1), channel_id=1, source_target_pairs={{0,6},{1,25},{2,0},{3,27},{4,2},{5,29},{6,4},{7,31},{8,14},{9,1},{... | collective-permute-start | bytes 638984 | tf_op jit(solution)/shard_map/ppermute | solution.py:350
  38.9 7.1 %collective-permute-start.4 = (bf16[104,1024]{1,0:T(8,128)(2,1)S(1)}, bf16[104,1024]{1,0:T(8,128)(2,1)S(1)}, u32[]{:S(2)}, u32[]{:S(2)}) collective-permute-start(bf16[104,1024]{1,0:T(8,128)(2,1)S(1)} %top_level.1), channel_id=1, source_target_pairs={{0,2},{1,9},{2,4},{3,11},{4,6},{5,13},{6,0},{7,15},{8,10},{9,17},{... | collective-permute-start | bytes 638984 | tf_op jit(solution)/shard_map/ppermute | solution.py:350
  46.1 20.0 %collective-permute-start.9 = (bf16[4,104,1024]{2,1,0:T(8,128)(2,1)S(1)}, bf16[4,104,1024]{2,1,0:T(8,128)(2,1)}, u32[]{:S(2)}, u32[]{:S(2)}) collective-permute-start(bf16[4,104,1024]{2,1,0:T(8,128)(2,1)S(1)} %pad_maximum_fusion.refs_0_), channel_id=1, source_target_pairs={{0,16},{1,5},{2,18},{3,7},{4,20},{5,1},{6,22},{7,3},{8,24},{9,13},... | collective-permute-start | bytes 2555912 | tf_op jit(solution)/shard_map/ppermute | solution.py:350
  48.3 20.5 %collective-permute-start.8 = (bf16[4,104,1024]{2,1,0:T(8,128)(2,1)S(1)}, bf16[4,104,1024]{2,1,0:T(8,128)(2,1)}, u32[]{:S(2)}, u32[]{:S(2)}) collective-permute-start(bf16[4,104,1024]{2,1,0:T(8,128)(2,1)S(1)} %pad_maximum_fusion.refs_0_), channel_id=1, source_target_pairs={{0,24},{1,7},{2,26},{3,1},{4,28},{5,3},{6,30},{7,5},{8,0},{9,15},{... | collective-permute-start | bytes 2555912 | tf_op jit(solution)/shard_map/ppermute | solution.py:350
  49.3 33.9 %collective-permute-start.7 = (bf16[4,104,1024]{2,1,0:T(8,128)(2,1)S(1)}, bf16[4,104,1024]{2,1,0:T(8,128)(2,1)}, u32[]{:S(2)}, u32[]{:S(2)}) collective-permute-start(bf16[4,104,1024]{2,1,0:T(8,128)(2,1)S(1)} %pad_maximum_fusion.refs_0_), channel_id=1, source_target_pairs={{0,8},{1,3},{2,10},{3,5},{4,12},{5,7},{6,14},{7,1},{8,16},{9,11},{... | collective-permute-start | bytes 2555912 | tf_op jit(solution)/shard_map/ppermute | solution.py:350
  57.8 46.9 %all-to-all-start.1 = ((bf16[32,32,1024]{2,1,0:T(8,128)(2,1)}), bf16[32,32,1024]{2,1,0:T(8,128)(2,1)S(1)}, u32[]{:S(2)}, u32[]{:S(2)}) async-start(bf16[32,32,1024]{2,1,0:T(8,128)(2,1)} %bitcast.16), calls=%async_computation.1 | async-start | bytes 4194304 | tf_op jit(solution)/shard_map/all_to_all | solution.py:360
  65.8 23.0 %collective-permute-start.10 = (bf16[4,104,1024]{2,1,0:T(8,128)(2,1)S(1)}, bf16[4,104,1024]{2,1,0:T(8,128)(2,1)S(1)}, u32[]{:S(2)}, u32[]{:S(2)}) collective-permute-start(bf16[4,104,1024]{2,1,0:T(8,128)(2,1)S(1)} %pad_maximum_fusion.refs_0_), channel_id=1, source_target_pairs={{0,1},{1,0},{2,3},{3,2},{4,5},{5,4},{6,7},{7,6},{8,9},{9,8},{10,11... | collective-permute-start | bytes 2555912 | tf_op jit(solution)/shard_map/ppermute | solution.py:354
  66.1 22.7 %collective-permute-start.13 = (bf16[4,104,1024]{2,1,0:T(8,128)(2,1)}, bf16[4,104,1024]{2,1,0:T(8,128)(2,1)S(1)}, u32[]{:S(2)}, u32[]{:S(2)}) collective-permute-start(bf16[4,104,1024]{2,1,0:T(8,128)(2,1)} %collective-permute-done.9.refs_3_), channel_id=1, source_target_pairs={{0,1},{1,0},{2,3},{3,2},{4,5},{5,4},{6,7},{7,6},{8,9},{9,8},{10,11... | collective-permute-start | bytes 2555912 | tf_op jit(solution)/shard_map/ppermute | solution.py:354
  68.7 20.1 %collective-permute-start.12 = (bf16[4,104,1024]{2,1,0:T(8,128)(2,1)}, bf16[4,104,1024]{2,1,0:T(8,128)(2,1)S(1)}, u32[]{:S(2)}, u32[]{:S(2)}) collective-permute-start(bf16[4,104,1024]{2,1,0:T(8,128)(2,1)} %collective-permute-done.8.refs_2_), channel_id=1, source_target_pairs={{0,1},{1,0},{2,3},{3,2},{4,5},{5,4},{6,7},{7,6},{8,9},{9,8},{10,11... | collective-permute-start | bytes 2555912 | tf_op jit(solution)/shard_map/ppermute | solution.py:354
  83.2 7.8 %collective-permute-start.11 = (bf16[4,104,1024]{2,1,0:T(8,128)(2,1)}, bf16[4,104,1024]{2,1,0:T(8,128)(2,1)S(1)}, u32[]{:S(2)}, u32[]{:S(2)}) collective-permute-start(bf16[4,104,1024]{2,1,0:T(8,128)(2,1)} %collective-permute-done.7.refs_1_), channel_id=1, source_target_pairs={{0,1},{1,0},{2,3},{3,2},{4,5},{5,4},{6,7},{7,6},{8,9},{9,8},{10,11... | collective-permute-start | bytes 2555912 | tf_op jit(solution)/shard_map/ppermute | solution.py:354

commit v3 on v2

v3 whole, which is shorter than its diff:
```python
import jax
import jax.numpy as jnp
from jax import lax
from jax.experimental import pallas as pl
from jax.experimental.pallas import tpu as pltpu
from jax.sharding import PartitionSpec as P

BF16 = jnp.bfloat16
F32 = jnp.float32
I32 = jnp.int32

ROWS = 512
PORTS = 1024
OWNERS = 32
CAP = 32
SLOTS = OWNERS * CAP
OWN = 32
DROWS = 8
ZROWS = OWN + DROWS
PACK = 3 * OWN + DROWS
HALF_SCALE = 64.0
HALF_MARK = 32.0
STEPS = (1, -1, 2)
NEAR = (0, -1, 1, -2)
LINES = ((0, 0), (-1, 0), (1, 0), (2, 0), (2, 2))


def iota(shape, dim):
    return lax.broadcasted_iota(I32, shape, dim)


def params(limit=20, dims=None):
    return pltpu.CompilerParams(vmem_limit_bytes=limit << 20, dimension_semantics=dims)


def cost(flops, nbytes):
    return pl.CostEstimate(flops=flops, bytes_accessed=nbytes, transcendentals=0)


def hbm(value):
    return pltpu.with_memory_space_constraint(value, pltpu.HBM)


def vmem(value):
    return pltpu.with_memory_space_constraint(value, pltpu.VMEM)


ANYWHERE = pl.BlockSpec(memory_space=pl.ANY)
IN_VMEM = pl.BlockSpec(memory_space=pltpu.VMEM)


def split(value, parts):
    pieces = []
    for _ in range(parts):
        piece = value.astype(BF16).astype(F32)
        pieces.append(piece)
        value = value - piece
    return pieces


def rows_of(pieces, count):
    r = iota((count, PORTS), 0)
    out = jnp.zeros((count, PORTS), F32)
    for k, piece in enumerate(pieces):
        out = jnp.where(r == k, piece, out)
    return out.astype(BF16)


def own_lanes():
    own = lax.axis_index("owner")
    return iota((OWN, PORTS), 1) == own * OWN + iota((OWN, PORTS), 0)


def label_kernel(off_ref, diag_ref, z_ref):
    z_ref[:OWN, :] = off_ref[...]
    diag = jnp.sum(jnp.where(iota((OWN, OWN), 0) == iota((OWN, OWN), 1), diag_ref[...], 0.0), axis=1, keepdims=True)
    placed = jnp.sum(jnp.where(own_lanes(), diag, 0.0), axis=0, keepdims=True)
    z_ref[OWN:, :] = rows_of(split(placed, 3), DROWS)


def label(off, diag):
    return pl.pallas_call(
        label_kernel,
        out_shape=jax.ShapeDtypeStruct((ZROWS, PORTS), BF16),
        compiler_params=params(),
        cost_estimate=cost(OWN * PORTS, 1 << 17),
        name="label",
    )(hbm(off), hbm(diag))


def prep_kernel(
    owner_ref, half_ref, port_ref, rows_ref, out_ref, target_ref, names, rows, stim, made, in_sems, out_sems
):
    small = [
        pltpu.make_async_copy(ref, names.at[k], in_sems.at[2 + k]) for k, ref in enumerate((owner_ref, half_ref, port_ref))
    ]
    for copy in small:
        copy.start()
    half_rows = ROWS // 2
    loads = [
        pltpu.make_async_copy(rows_ref.at[r : r + half_rows], rows.at[r : r + half_rows], in_sems.at[k])
        for k, r in enumerate(range(0, ROWS, half_rows))
    ]
    for load in loads:
        load.start()
    for copy in small:
        copy.wait()
    owner = names[0]
    named = iota((OWNERS, ROWS), 0) == owner
    earlier = jnp.where(iota((ROWS, ROWS), 0) < iota((ROWS, ROWS), 1), 1.0, 0.0).astype(BF16)
    before = jnp.dot(jnp.where(named, 1.0, 0.0).astype(BF16), earlier, preferred_element_type=F32)
    rank = jnp.sum(jnp.where(named, before, 0.0), axis=0, keepdims=True)
    target = owner * CAP + rank.astype(I32)
    target_ref[...] = target + SLOTS * names[1]
    scale = jnp.where(names[1] == 1, HALF_SCALE, 1.0)
    port = jnp.transpose(jnp.broadcast_to(names[2], (128, ROWS)))
    for k, load in enumerate(loads):
        load.wait()
        at = slice(k * half_rows, (k + 1) * half_rows)
        for j in range(0, PORTS, 128):
            lanes = slice(j, j + 128)
            bump = jnp.where(iota((half_rows, 128), 1) + j == port[at], 8.0, 0.0)
            stim[at, lanes] = (rows[at, lanes].astype(F32) + bump).astype(BF16)
    stores = []
    tile = 256
    for k, u in enumerate(range(0, SLOTS, tile)):
        route = jnp.where(iota((tile, ROWS), 0) + u == target, scale, 0.0).astype(BF16)
        made[u : u + tile, :] = jnp.dot(route, stim[...], preferred_element_type=F32).astype(BF16)
        store = pltpu.make_async_copy(made.at[u : u + tile], out_ref.at[u : u + tile], out_sems.at[k])
        store.start()
        stores.append(store)
    for store in stores:
        store.wait()


def prep(owner, half, port, rows):
    return pl.pallas_call(
        prep_kernel,
        in_specs=[ANYWHERE] * 4,
        out_specs=[ANYWHERE, IN_VMEM],
        out_shape=[pltpu.HBM((SLOTS, PORTS), BF16), jax.ShapeDtypeStruct((1, ROWS), I32)],
        scratch_shapes=[
            pltpu.VMEM((3, 1, ROWS), I32),
            pltpu.VMEM((ROWS, PORTS), BF16),
            pltpu.VMEM((ROWS, PORTS), BF16),
            pltpu.VMEM((SLOTS, PORTS), BF16),
            pltpu.SemaphoreType.DMA((5,)),
            pltpu.SemaphoreType.DMA((4,)),
        ],
        compiler_params=params(),
        cost_estimate=cost(2 * SLOTS * ROWS * PORTS, 4 << 20),
        name="prep",
    )(hbm(owner), hbm(half), hbm(port), hbm(rows))


def maps_kernel(x_ref, maps_ref, out_ref, maps, first, other, total, made, in_sems, out_sems):
    tile = 256
    tiles = SLOTS // tile
    loads = [
        pltpu.make_async_copy(maps_ref.at[h, r : r + tile], maps.at[h, r : r + tile], in_sems.at[h, k])
        for h in range(2)
        for k, r in enumerate(range(0, PORTS, tile))
    ]
    for load in loads[:tiles]:
        load.start()
    for r in range(0, SLOTS, tile):
        x = x_ref[r : r + tile, :]
        peak = jnp.abs(x[:, :128])
        for j in range(128, PORTS, 128):
            peak = jnp.maximum(peak, jnp.abs(x[:, j : j + 128]))
        second = jnp.max(peak.astype(F32), axis=1, keepdims=True) > HALF_MARK
        keep = jnp.where(second, 0.0, 1.0).astype(BF16)
        kept = x * keep
        first[r : r + tile, :] = kept
        other[r : r + tile, :] = x - kept
    for load in loads[tiles:]:
        load.start()
    for load in loads[:tiles]:
        load.wait()
    for n in range(0, PORTS, tile):
        total[:, n : n + tile] = jnp.dot(first[...], maps[0, :, n : n + tile], preferred_element_type=F32)
    for load in loads[tiles:]:
        load.wait()
    stores = []
    for k, r in enumerate(range(0, SLOTS, tile)):
        at = slice(r, r + tile)
        made[at, :] = (total[at, :] + jnp.dot(other[at, :], maps[1], preferred_element_type=F32)).astype(BF16)
        store = pltpu.make_async_copy(made.at[at], out_ref.at[at], out_sems.at[k])
        store.start()
        stores.append(store)
    for store in stores:
        store.wait()


def apply_maps(x, maps):
    return pl.pallas_call(
        maps_kernel,
        in_specs=[IN_VMEM, ANYWHERE],
        out_specs=ANYWHERE,
        out_shape=pltpu.HBM((SLOTS, PORTS), BF16),
        scratch_shapes=[
            pltpu.VMEM((2, PORTS, PORTS), BF16),
            pltpu.VMEM((SLOTS, PORTS), BF16),
            pltpu.VMEM((SLOTS, PORTS), BF16),
            pltpu.VMEM((SLOTS, PORTS), F32),
            pltpu.VMEM((SLOTS, PORTS), BF16),
            pltpu.SemaphoreType.DMA((2, 4)),
            pltpu.SemaphoreType.DMA((4,)),
        ],
        compiler_params=params(28),
        cost_estimate=cost(4 * SLOTS * PORTS * PORTS, 8 << 20),
        name="apply_maps",
    )(vmem(x), hbm(maps))


def permuted(values, order):
    out = jnp.zeros(values.shape, F32)
    for j in range(0, PORTS, 256):
        pick = jnp.where(iota((256, PORTS), 0) + j == order, 1.0, 0.0).astype(BF16)
        out = out + jnp.dot(values[:, j : j + 256], pick, preferred_element_type=F32)
    return out


def read_diag(z_ref):
    z = z_ref[OWN:, :].astype(F32)
    return z[0:1] + z[1:2] + z[2:3]


def column(placed):
    return jnp.sum(jnp.where(own_lanes(), placed, 0.0), axis=1, keepdims=True)


def inverse(placed):
    held = placed > 0.0
    return jnp.where(held, 1.0 / jnp.where(held, placed, 1.0), 0.0)


def low_levels_kernel(z0_ref, z1_ref, z2_ref, z3_ref, order_ref, z_ref, off_ref, diag_ref, gb_ref):
    picked = permuted(jnp.concatenate([z1_ref[:OWN, :], z3_ref[:OWN, :]], axis=0), order_ref[0:1, :])
    off1 = z0_ref[:OWN, :].astype(F32) + picked[:OWN]
    picked2 = permuted(jnp.concatenate([z2_ref[:OWN, :], picked[OWN:].astype(BF16)], axis=0), order_ref[1:2, :])
    off2 = off1 + (picked2[:OWN] + picked2[OWN:])
    d0 = read_diag(z0_ref)
    d1 = d0 + read_diag(z1_ref)
    d2 = d1 + (read_diag(z2_ref) + read_diag(z3_ref))
    z_ref[:OWN, :] = off2.astype(BF16)
    z_ref[OWN:, :] = rows_of(split(d2, 3), DROWS)
    off_ref[...] = off2
    r = iota((DROWS, PORTS), 0)
    diag_ref[...] = jnp.where(r == 0, d0, jnp.where(r == 1, d2, 0.0))
    gb_ref[:OWN, :] = ((jnp.where(own_lanes(), d0, 0.0) - off1) / column(d1)).astype(BF16)
    gb_ref[OWN:, :] = (off2 / column(d2)).astype(BF16)


def low_levels(z0, z1, z2, z3, order):
    return pl.pallas_call(
        low_levels_kernel,
        out_shape=[
            jax.ShapeDtypeStruct((ZROWS, PORTS), BF16),
            jax.ShapeDtypeStruct((OWN, PORTS), F32),
            jax.ShapeDtypeStruct((DROWS, PORTS), F32),
            jax.ShapeDtypeStruct((2 * OWN, PORTS), BF16),
        ],
        compiler_params=params(),
        cost_estimate=cost(4 * 64 * PORTS * PORTS, 1 << 20),
        name="low_levels",
    )(z0, z1, z2, z3, order)


def top_level_kernel(z4_ref, off_ref, diag_ref, gb_ref, order_ref, pack_ref):
    off3 = off_ref[...] + permuted(z4_ref[:OWN, :], order_ref[2:3, :])
    d0, d2 = diag_ref[0:1, :], diag_ref[1:2, :]
    d3 = d2 + read_diag(z4_ref)
    pack_ref[: 2 * OWN, :] = gb_ref[...]
    pack_ref[2 * OWN : 3 * OWN, :] = (off3 / column(d3)).astype(BF16)
    pieces = split(inverse(d0), 3) + split(inverse(d3), 3) + split(d0 * inverse(d2), 2)
    pack_ref[3 * OWN :, :] = rows_of(pieces, DROWS)


def top_level(z4, off, diag, gb, order):
    return pl.pallas_call(
        top_level_kernel,
        out_shape=jax.ShapeDtypeStruct((PACK, PORTS), BF16),
        compiler_params=params(),
        cost_estimate=cost(2 * 32 * PORTS * PORTS, 1 << 20),
        name="top_level",
    )(z4, off, diag, gb, order)


def fold_kernel(*refs):
    parts, (f_ref, diag_ref, held, marks) = refs[: 2 * len(LINES)], refs[2 * len(LINES) :]
    own = lax.axis_index("owner")
    core, x, y = own & 1, (own >> 1) & 3, own >> 3
    slot = 0
    for side in range(2):
        c = core if side == 0 else 1 - core
        for m, (away, first) in enumerate(LINES):
            for k in range(parts[side * len(LINES) + m].shape[0]):
                dx = jnp.where(c == 0, NEAR[k + first], away)
                dy = jnp.where(c == 0, away, NEAR[k + first])
                start = ((((y + dy) & 3) * 4 + ((x + dx) & 3)) * 2 + c) * OWN
                at = pl.ds(pl.multiple_of(start, OWN), OWN)
                block = parts[side * len(LINES) + m]
                for j in range(3):
                    held[j, at, :] = block[k, j * OWN : (j + 1) * OWN, :]
                marks[slot] = block[k, 3 * OWN :, :]
                slot += 1
    total = jnp.sum(marks[...].astype(F32), axis=0)
    inv0 = total[0:1] + total[1:2] + total[2:3]
    inv3 = total[3:4] + total[4:5] + total[5:6]
    ratio = total[6:7] + total[7:8]
    r = iota((DROWS, PORTS), 0)
    diag_ref[...] = jnp.where(r == 0, inv0, jnp.where(r == 1, inv3, 0.0))
    tile = 256
    for t in range(0, PORTS, tile):
        acc = jnp.dot(held[1], held[0, :, t : t + tile], preferred_element_type=F32)
        on = iota((PORTS, tile), 0) == iota((PORTS, tile), 1) + t
        mid = (jnp.where(on, ratio[:, t : t + tile], 0.0) - acc).astype(BF16)
        f_ref[t : t + tile, :] = jnp.transpose(jnp.dot(held[2], mid, preferred_element_type=F32)).astype(BF16)


def fold(parts):
    return pl.pallas_call(
        fold_kernel,
        in_specs=[IN_VMEM] * (2 * len(LINES)),
        out_shape=[pltpu.HBM((PORTS, PORTS), BF16), pltpu.VMEM((DROWS, PORTS), F32)],
        scratch_shapes=[
            pltpu.VMEM((3, PORTS, PORTS), BF16),
            pltpu.VMEM((32, DROWS, PORTS), BF16),
        ],
        compiler_params=params(24),
        cost_estimate=cost(4 * PORTS**3, 9 << 20),
        name="fold",
    )(*[vmem(part) for part in parts])


def finish_kernel(target_ref, ret_ref, f_ref, diag_ref, out_ref, route, response, scaled, coupling, made, in_sem, out_sems):
    load = pltpu.make_async_copy(f_ref, coupling, in_sem)
    load.start()
    code = jnp.transpose(jnp.broadcast_to(target_ref[...], (128, ROWS)))
    scale = jnp.where(code >= SLOTS, 1.0 / HALF_SCALE, 1.0)
    target = code & (SLOTS - 1)
    for j in range(0, SLOTS, 128):
        route[:, j : j + 128] = jnp.where(iota((ROWS, 128), 1) + j == target, scale, 0.0).astype(BF16)
    for n in range(0, PORTS, 256):
        at = slice(n, n + 256)
        piece = jnp.dot(route[...], ret_ref[:, at], preferred_element_type=F32)
        response[:, at] = piece
        scaled[:, at] = (piece * diag_ref[0:1, at]).astype(BF16)
    load.wait()
    stores = []
    tile = 128
    for k, r in enumerate(range(0, ROWS, tile)):
        at = slice(r, r + tile)
        coupled = jnp.dot(scaled[at, :], coupling[...], preferred_element_type=F32)
        made[at, :] = response[at, :] * diag_ref[1:2, :] - coupled
        store = pltpu.make_async_copy(made.at[at], out_ref.at[at], out_sems.at[k])
        store.start()
        stores.append(store)
    for store in stores:
        store.wait()


def finish(target, returned, f, diag):
    return pl.pallas_call(
        finish_kernel,
        in_specs=[IN_VMEM, IN_VMEM, ANYWHERE, IN_VMEM],
        out_specs=ANYWHERE,
        out_shape=pltpu.HBM((ROWS, PORTS), F32),
        scratch_shapes=[
            pltpu.VMEM((ROWS, SLOTS), BF16),
            pltpu.VMEM((ROWS, PORTS), F32),
            pltpu.VMEM((ROWS, PORTS), BF16),
            pltpu.VMEM((PORTS, PORTS), BF16),
            pltpu.VMEM((ROWS, PORTS), F32),
            pltpu.SemaphoreType.DMA,
            pltpu.SemaphoreType.DMA((4,)),
        ],
        compiler_params=params(24),
        cost_estimate=cost(4 * ROWS * PORTS * PORTS, 6 << 20),
        name="finish",
    )(vmem(target), vmem(returned), hbm(f), vmem(diag))


def group_swap(value, mask):
    return lax.ppermute(value, "group", [(i, i ^ mask) for i in range(8)])


def chip_shift(value, step, turn):
    pairs = []
    for o in range(OWNERS):
        c, x, y = o & 1, (o >> 1) & 3, o >> 3
        if (c ^ turn) == 0:
            x = (x + step) % 4
        else:
            y = (y + step) % 4
        pairs.append((o, (y * 4 + x) * 2 + c))
    return lax.ppermute(value, "owner", pairs)


def core_swap(value):
    return lax.ppermute(value, "owner", [(o, o ^ 1) for o in range(OWNERS)])


def exchange(value):
    shape = value.shape
    value = value.reshape(OWNERS, CAP, PORTS)
    return lax.all_to_all(value, "owner", split_axis=0, concat_axis=0, tiled=True).reshape(shape)


def body(port_rows, defect_owner, defect_half, defect_port, subcircuit_maps, schur_off, schur_diag, pivot_order):
    z0 = label(schur_off, schur_diag.reshape(1, OWN))
    z1, z2, z3 = (group_swap(z0, mask) for mask in (1, 2, 3))
    outgoing, target = prep(
        defect_owner.reshape(1, ROWS), defect_half.reshape(1, ROWS), defect_port.reshape(1, ROWS), port_rows
    )
    arrived = exchange(outgoing)
    z, off, diag, gb = low_levels(z0, z1, z2, z3, pivot_order)
    pack = top_level(group_swap(z, 4), off, diag, gb, pivot_order)
    line = jnp.stack([pack] + [chip_shift(pack, step, 0) for step in STEPS])
    left, right = chip_shift(line, 1, 1), chip_shift(line, -1, 1)
    far_low, far_high = chip_shift(left[:2], 1, 1), chip_shift(right[2:], -1, 1)
    parts = [line, left, right, far_low, far_high]
    parts = parts + [core_swap(part) for part in parts]
    f, inverses = fold(parts)
    answers = apply_maps(arrived, subcircuit_maps)
    returned = exchange(answers)
    return finish(target, returned, f, inverses)


def solution(mesh):
    return jax.shard_map(
        body,
        mesh=mesh,
        in_specs=(
            P(("group", "owner"), None),
            P(("group", "owner"), None),
            P(("group", "owner")),
            P(("group", "owner")),
            P(("group", "owner"), None, None),
            P(("group", "owner"), None),
            P(("group", "owner")),
            P(),
        ),
        out_specs=P(("group", "owner"), None),
        check_vma=False,
    )
```

time: 114 us -> 109 us (0.956)
  waiting for transfers between devices: 19.5 us -> 40.7 us
  starting transfers between devices: 56.1 us -> 39 us
  Pallas kernels: 36.3 us -> 25.4 us
  local copies, waits for them, and re-layouts: 0.01 us -> 2.08 us
    ppermute x6 -> x7, waiting for transfers between devices: 8.83 us -> 30.8 us  [chip_shift(): return lax.ppermute(value, 'owner', pairs)]
    ppermute x4 -> x5, starting transfers between devices: 20.7 us -> 1.67 us  [core_swap(): return lax.ppermute(value, 'owner', [(o, o ^ 1) for o in range(OWNERS)])]
    pallas_call x4, Pallas kernels: 33.9 us -> 23 us  [the longest x1 8.71 us: fold(): pl.pallas_call(fold_kernel, in_specs=[IN_VMEM] * (2 * len(LINES)), out_sh...]
    slice x0 -> x2, local copies, waits for them, and re-layouts: none -> 2.07 us  [the longest x1 1.04 us: body(): right[2:]]
    ppermute x6 -> x7, starting transfers between devices: 8.03 us -> 9.68 us  [chip_shift(): return lax.ppermute(value, 'owner', pairs)]
  transfers between devices with their start and end apart: 16 -> 18, of which waited for: 8 -> 10; matrix products, arithmetic and copies ran while one was open for 0% -> 2% of each run, Pallas kernels for 21% -> 17%
where the time goes in v3:
time: 109 us; the launch traced here: 108 us
  waiting for transfers between devices  40.7 us (37%)
  starting transfers between devices  39 us (36%)
  Pallas kernels  25.4 us (23%)
  local copies, waits for them, and re-layouts  2.08 us (2%)
    ppermute x7, waiting for transfers between devices, chip_shift(): return lax.ppermute(value, 'owner', pairs)  30.8 us
    all_to_all x2, starting transfers between devices, exchange(): lax.all_to_all(value, 'owner', split_axis=0, concat_axis=0, tiled=True)  16.9 us
    ppermute x4, starting transfers between devices, group_swap(): return lax.ppermute(value, 'group', [(i, i ^ mask) for i in range(8)])  10.7 us
    ppermute x7, starting transfers between devices, chip_shift(): return lax.ppermute(value, 'owner', pairs)  9.68 us
    pallas_call x1, Pallas kernels, fold(): pl.pallas_call(fold_kernel, in_specs=[IN_VMEM] * (2 * len(LINES)), out_sh...  8.71 us
    ppermute x4, waiting for transfers between devices, group_swap(): return lax.ppermute(value, 'group', [(i, i ^ mask) for i in range(8)])  8.49 us
    pallas_call x1, Pallas kernels, apply_maps(): pl.pallas_call(maps_kernel, in_specs=[IN_VMEM, ANYWHERE], out_specs=ANYWH...  7.05 us
    pallas_call x1, Pallas kernels, finish(): pl.pallas_call(finish_kernel, in_specs=[IN_VMEM, IN_VMEM, ANYWHERE, IN_VM...  3.7 us
  transfers between devices with their start and end apart: 18, of which 10 were waited for; matrix products, arithmetic and copies ran while one was open for 2% of the time, Pallas kernels for 17%

profile of v3, /device:TPU:1, one launch (start us, length us, event | category | flops | bytes accessed | tf_op | source)
XLA Modules:
  0.0 107.5 jit_solution(3303960592919850361)
XLA Ops:
  0.0 3.6 %prep.1 = (bf16[1024,1024]{1,0:T(8,128)(2,1)}, s32[1,512]{1,0:T(1,128)S(1)}) custom-call(s32[1,512]{1,0:T(1,128)} %bitcast.21, s32[1,512]{1,0:T(1,128)} %bitcast.22, s32[1,512]{1,0:T(1,128)} %bitcast.23, bf16[512,1024]{1,0:T(8,128)(2,1)} %rows_ref.1), custom_call_target="tpu_custom_call" | custom-call | flops 1073741824 | bytes 4194304 | tf_op jit(solution)/shard_map/prep/pallas_call | solution.py:137
  3.6 8.6 %all-to-all-start = ((bf16[32,32,1024]{2,1,0:T(8,128)(2,1)}), bf16[32,32,1024]{2,1,0:T(8,128)(2,1)S(1)}, u32[]{:S(2)}, u32[]{:S(2)}) async-start(bf16[32,32,1024]{2,1,0:T(8,128)(2,1)} %bitcast.15), calls=%async_computation | async-start | bytes 4194304 | tf_op jit(solution)/shard_map/all_to_all | solution.py:408
  12.2 1.0 label.1.z0_ref
  13.1 4.4 %collective-permute-start.2 = (bf16[40,1024]{1,0:T(8,128)(2,1)S(1)}, bf16[40,1024]{1,0:T(8,128)(2,1)S(1)}, u32[]{:S(2)}, u32[]{:S(2)}) collective-permute-start(bf16[40,1024]{1,0:T(8,128)(2,1)S(1)} %label.1.z0_ref), channel_id=1, source_target_pairs={{0,96},{32,64},{64,32},{96,0},{128,224},{160,192},{192,160},{224,1... | collective-permute-start | bytes 245768 | tf_op jit(solution)/shard_map/ppermute | solution.py:386
  17.6 0.4 collective-permute-start
  18.0 2.3 %collective-permute-done.2.z3_ref = bf16[40,1024]{1,0:T(8,128)(2,1)S(1)} collective-permute-done((bf16[40,1024]{1,0:T(8,128)(2,1)S(1)}, bf16[40,1024]{1,0:T(8,128)(2,1)S(1)}, u32[]{:S(2)}, u32[]{:S(2)}) %collective-permute-start.2) | collective-permute-done | bytes 81952 | tf_op jit(solution)/shard_map/ppermute | solution.py:386
  20.3 4.0 %collective-permute-done.1.z2_ref = bf16[40,1024]{1,0:T(8,128)(2,1)S(1)} collective-permute-done((bf16[40,1024]{1,0:T(8,128)(2,1)S(1)}, bf16[40,1024]{1,0:T(8,128)(2,1)S(1)}, u32[]{:S(2)}, u32[]{:S(2)}) %collective-permute-start.1) | collective-permute-done | bytes 81952 | tf_op jit(solution)/shard_map/ppermute | solution.py:386
  24.2 1.0 low_levels.1
  25.2 5.9 %collective-permute-start.3 = (bf16[40,1024]{1,0:T(8,128)(2,1)S(1)}, bf16[40,1024]{1,0:T(8,128)(2,1)S(1)}, u32[]{:S(2)}, u32[]{:S(2)}) collective-permute-start(bf16[40,1024]{1,0:T(8,128)(2,1)S(1)} %get-tuple-element.15), channel_id=1, source_target_pairs={{0,128},{32,160},{64,192},{96,224},{128,0},{160,32},{192,64},{224,... | collective-permute-start | bytes 245768 | tf_op jit(solution)/shard_map/ppermute | solution.py:386
  31.1 2.2 %collective-permute-done.3.z4_ref = bf16[40,1024]{1,0:T(8,128)(2,1)S(1)} collective-permute-done((bf16[40,1024]{1,0:T(8,128)(2,1)S(1)}, bf16[40,1024]{1,0:T(8,128)(2,1)S(1)}, u32[]{:S(2)}, u32[]{:S(2)}) %collective-permute-start.3) | collective-permute-done | bytes 81952 | tf_op jit(solution)/shard_map/ppermute | solution.py:386
  33.3 0.5 top_level.1
  33.8 2.9 %collective-permute-start.6 = (bf16[104,1024]{1,0:T(8,128)(2,1)S(1)}, bf16[104,1024]{1,0:T(8,128)(2,1)S(1)}, u32[]{:S(2)}, u32[]{:S(2)}) collective-permute-start(bf16[104,1024]{1,0:T(8,128)(2,1)S(1)} %top_level.1), channel_id=1, source_target_pairs={{0,4},{1,17},{2,6},{3,19},{4,0},{5,21},{6,2},{7,23},{8,12},{9,25},... | collective-permute-start | bytes 638984 | tf_op jit(solution)/shard_map/ppermute | solution.py:398
  36.8 0.9 collective-permute-start.5
  37.6 0.6 collective-permute-start.4
  38.2 3.6 %collective-permute-done.6 = bf16[104,1024]{1,0:T(8,128)(2,1)S(1)} collective-permute-done((bf16[104,1024]{1,0:T(8,128)(2,1)S(1)}, bf16[104,1024]{1,0:T(8,128)(2,1)S(1)}, u32[]{:S(2)}, u32[]{:S(2)}) %collective-permute-start.6) | collective-permute-done | bytes 213024 | tf_op jit(solution)/shard_map/ppermute | solution.py:398
  41.8 1.8 %collective-permute-done.5 = bf16[104,1024]{1,0:T(8,128)(2,1)S(1)} collective-permute-done((bf16[104,1024]{1,0:T(8,128)(2,1)S(1)}, bf16[104,1024]{1,0:T(8,128)(2,1)S(1)}, u32[]{:S(2)}, u32[]{:S(2)}) %collective-permute-start.5) | collective-permute-done | bytes 213024 | tf_op jit(solution)/shard_map/ppermute | solution.py:398
  43.6 0.6 collective-permute-done.4
  44.3 2.4 %collective-permute-start.8 = (bf16[4,104,1024]{2,1,0:T(8,128)(2,1)S(1)}, bf16[4,104,1024]{2,1,0:T(8,128)(2,1)}, u32[]{:S(2)}, u32[]{:S(2)}) collective-permute-start(bf16[4,104,1024]{2,1,0:T(8,128)(2,1)S(1)} %pad_maximum_fusion.refs_0_), channel_id=1, source_target_pairs={{0,24},{1,7},{2,26},{3,1},{4,28},{5,3},{6,30},{7,5},{8,0},{9,15},{... | collective-permute-start | bytes 2555912 | tf_op jit(solution)/shard_map/ppermute | solution.py:398
  46.7 7.1 %apply_maps.1 = bf16[1024,1024]{1,0:T(8,128)(2,1)} custom-call(bf16[1024,1024]{1,0:T(8,128)(2,1)S(1)} %bitcast.12, bf16[2,1024,1024]{2,1,0:T(8,128)(2,1)} %maps_ref.1), custom_call_target="tpu_custom_call" | custom-call | flops 4294967296 | bytes 8388608 | tf_op jit(solution)/shard_map/apply_maps/pallas_call | solution.py:196
  53.8 8.3 %all-to-all-start.1 = ((bf16[32,32,1024]{2,1,0:T(8,128)(2,1)}), bf16[32,32,1024]{2,1,0:T(8,128)(2,1)S(1)}, u32[]{:S(2)}, u32[]{:S(2)}) async-start(bf16[32,32,1024]{2,1,0:T(8,128)(2,1)} %bitcast.16), calls=%async_computation.1 | async-start | bytes 4194304 | tf_op jit(solution)/shard_map/all_to_all | solution.py:408
  62.1 0.3 collective-permute-start.11
  62.4 1.0 slice.9
  63.5 2.8 %collective-permute-start.10 = (bf16[2,104,1024]{2,1,0:T(8,128)(2,1)S(1)}, bf16[2,104,1024]{2,1,0:T(8,128)(2,1)S(1)}, u32[]{:S(2)}, u32[]{:S(2)}) collective-permute-start(bf16[2,104,1024]{2,1,0:T(8,128)(2,1)S(1)} %slice.9), channel_id=1, source_target_pairs={{0,24},{1,7},{2,26},{3,1},{4,28},{5,3},{6,30},{7,5},{8,0},{9,15},{... | collective-permute-start | bytes 1277960 | tf_op jit(solution)/shard_map/ppermute | solution.py:398
  66.3 1.0 slice.8
  67.4 0.6 collective-permute-start.13
  68.1 24.1 %collective-permute-done.10.refs_4_ = bf16[2,104,1024]{2,1,0:T(8,128)(2,1)S(1)} collective-permute-done((bf16[2,104,1024]{2,1,0:T(8,128)(2,1)S(1)}, bf16[2,104,1024]{2,1,0:T(8,128)(2,1)S(1)}, u32[]{:S(2)}, u32[]{:S(2)}) %collective-permute-start.10) | collective-permute-done | bytes 426016 | tf_op jit(solution)/shard_map/ppermute | solution.py:398
  92.4 0.7 collective-permute-done.9.refs_3_
  93.1 0.4 collective-permute-start.14
  93.5 0.4 collective-permute-done.15.refs_9_
  93.9 1.0 collective-permute-done.14.refs_8_
  94.9 8.7 %fold.1 = (bf16[1024,1024]{1,0:T(8,128)(2,1)}, f32[8,1024]{1,0:T(8,128)S(1)}) custom-call(bf16[4,104,1024]{2,1,0:T(8,128)(2,1)S(1)} %pad_maximum_fusion.refs_0_, bf16[4,104,1024]{2,1,0:T(8,128)(2,1)} %collective-permute-done.7.refs_1_, bf16[4,104,1024]{2,1,0:T(8,128)(2,1)} %collective-permute-done.8.refs_2_, ...), custom_call_target="tpu_custom_call" | custom-call | flops 4294967296 | bytes 9437184 | tf_op jit(solution)/shard_map/fold/pallas_call | solution.py:323
  103.6 3.7 %finish.1 = f32[512,1024]{1,0:T(8,128)} custom-call(s32[1,512]{1,0:T(1,128)S(1)} %get-tuple-element.13.target_ref, bf16[1024,1024]{1,0:T(8,128)(2,1)S(1)} %bitcast.13, bf16[1024,1024]{1,0:T(8,128)(2,1)} %get-tuple-element.19.f_ref, f32[8,1024]{1,0:T(8,128)S(1)} %get-tuple-element.20.diag_ref), custom_call_target="tpu_custom_call" | custom-call | flops 2147483648 | bytes 6291456 | tf_op jit(solution)/shard_map/finish/pallas_call | solution.py:365
  (16 shorter events, 0.6 us)
Async XLA Ops:
  3.6 20.7 %copy-start = (s32[3,1024]{1,0:T(4,128)S(1)}, s32[3,1024]{1,0:T(4,128)}, u32[]{:S(2)}) copy-start(s32[3,1024]{1,0:T(4,128)} %order_ref.3) | copy-start | bytes 36868
  3.6 43.2 %all-to-all-start = ((bf16[32,32,1024]{2,1,0:T(8,128)(2,1)}), bf16[32,32,1024]{2,1,0:T(8,128)(2,1)S(1)}, u32[]{:S(2)}, u32[]{:S(2)}) async-start(bf16[32,32,1024]{2,1,0:T(8,128)(2,1)} %bitcast.15), calls=%async_computation | async-start | bytes 4194304 | tf_op jit(solution)/shard_map/all_to_all | solution.py:408
  13.1 7.1 %collective-permute-start.2 = (bf16[40,1024]{1,0:T(8,128)(2,1)S(1)}, bf16[40,1024]{1,0:T(8,128)(2,1)S(1)}, u32[]{:S(2)}, u32[]{:S(2)}) collective-permute-start(bf16[40,1024]{1,0:T(8,128)(2,1)S(1)} %label.1.z0_ref), channel_id=1, source_target_pairs={{0,96},{32,64},{64,32},{96,0},{128,224},{160,192},{192,160},{224,1... | collective-permute-start | bytes 245768 | tf_op jit(solution)/shard_map/ppermute | solution.py:386
  17.6 6.7 %collective-permute-start.1 = (bf16[40,1024]{1,0:T(8,128)(2,1)S(1)}, bf16[40,1024]{1,0:T(8,128)(2,1)S(1)}, u32[]{:S(2)}, u32[]{:S(2)}) collective-permute-start(bf16[40,1024]{1,0:T(8,128)(2,1)S(1)} %label.1.z0_ref), channel_id=1, source_target_pairs={{0,64},{32,96},{64,0},{96,32},{128,192},{160,224},{192,128},{224,1... | collective-permute-start | bytes 245768 | tf_op jit(solution)/shard_map/ppermute | solution.py:386
  17.6 6.7 %collective-permute-start = (bf16[40,1024]{1,0:T(8,128)(2,1)S(1)}, bf16[40,1024]{1,0:T(8,128)(2,1)S(1)}, u32[]{:S(2)}, u32[]{:S(2)}) collective-permute-start(bf16[40,1024]{1,0:T(8,128)(2,1)S(1)} %label.1.z0_ref), channel_id=1, source_target_pairs={{0,32},{32,0},{64,96},{96,64},{128,160},{160,128},{192,224},{224,1... | collective-permute-start | bytes 245768 | tf_op jit(solution)/shard_map/ppermute | solution.py:386
  25.2 8.1 %collective-permute-start.3 = (bf16[40,1024]{1,0:T(8,128)(2,1)S(1)}, bf16[40,1024]{1,0:T(8,128)(2,1)S(1)}, u32[]{:S(2)}, u32[]{:S(2)}) collective-permute-start(bf16[40,1024]{1,0:T(8,128)(2,1)S(1)} %get-tuple-element.15), channel_id=1, source_target_pairs={{0,128},{32,160},{64,192},{96,224},{128,0},{160,32},{192,64},{224,... | collective-permute-start | bytes 245768 | tf_op jit(solution)/shard_map/ppermute | solution.py:386
  33.8 8.0 %collective-permute-start.6 = (bf16[104,1024]{1,0:T(8,128)(2,1)S(1)}, bf16[104,1024]{1,0:T(8,128)(2,1)S(1)}, u32[]{:S(2)}, u32[]{:S(2)}) collective-permute-start(bf16[104,1024]{1,0:T(8,128)(2,1)S(1)} %top_level.1), channel_id=1, source_target_pairs={{0,4},{1,17},{2,6},{3,19},{4,0},{5,21},{6,2},{7,23},{8,12},{9,25},... | collective-permute-start | bytes 638984 | tf_op jit(solution)/shard_map/ppermute | solution.py:398
  36.8 6.8 %collective-permute-start.5 = (bf16[104,1024]{1,0:T(8,128)(2,1)S(1)}, bf16[104,1024]{1,0:T(8,128)(2,1)S(1)}, u32[]{:S(2)}, u32[]{:S(2)}) collective-permute-start(bf16[104,1024]{1,0:T(8,128)(2,1)S(1)} %top_level.1), channel_id=1, source_target_pairs={{0,6},{1,25},{2,0},{3,27},{4,2},{5,29},{6,4},{7,31},{8,14},{9,1},{... | collective-permute-start | bytes 638984 | tf_op jit(solution)/shard_map/ppermute | solution.py:398
  37.6 6.6 %collective-permute-start.4 = (bf16[104,1024]{1,0:T(8,128)(2,1)S(1)}, bf16[104,1024]{1,0:T(8,128)(2,1)S(1)}, u32[]{:S(2)}, u32[]{:S(2)}) collective-permute-start(bf16[104,1024]{1,0:T(8,128)(2,1)S(1)} %top_level.1), channel_id=1, source_target_pairs={{0,2},{1,9},{2,4},{3,11},{4,6},{5,13},{6,0},{7,15},{8,10},{9,17},{... | collective-permute-start | bytes 638984 | tf_op jit(solution)/shard_map/ppermute | solution.py:398
  44.3 18.1 %collective-permute-start.8 = (bf16[4,104,1024]{2,1,0:T(8,128)(2,1)S(1)}, bf16[4,104,1024]{2,1,0:T(8,128)(2,1)}, u32[]{:S(2)}, u32[]{:S(2)}) collective-permute-start(bf16[4,104,1024]{2,1,0:T(8,128)(2,1)S(1)} %pad_maximum_fusion.refs_0_), channel_id=1, source_target_pairs={{0,24},{1,7},{2,26},{3,1},{4,28},{5,3},{6,30},{7,5},{8,0},{9,15},{... | collective-permute-start | bytes 2555912 | tf_op jit(solution)/shard_map/ppermute | solution.py:398
  46.7 19.6 %collective-permute-start.7 = (bf16[4,104,1024]{2,1,0:T(8,128)(2,1)S(1)}, bf16[4,104,1024]{2,1,0:T(8,128)(2,1)}, u32[]{:S(2)}, u32[]{:S(2)}) collective-permute-start(bf16[4,104,1024]{2,1,0:T(8,128)(2,1)S(1)} %pad_maximum_fusion.refs_0_), channel_id=1, source_target_pairs={{0,8},{1,3},{2,10},{3,5},{4,12},{5,7},{6,14},{7,1},{8,16},{9,11},{... | collective-permute-start | bytes 2555912 | tf_op jit(solution)/shard_map/ppermute | solution.py:398
  53.8 49.9 %all-to-all-start.1 = ((bf16[32,32,1024]{2,1,0:T(8,128)(2,1)}), bf16[32,32,1024]{2,1,0:T(8,128)(2,1)S(1)}, u32[]{:S(2)}, u32[]{:S(2)}) async-start(bf16[32,32,1024]{2,1,0:T(8,128)(2,1)} %bitcast.16), calls=%async_computation.1 | async-start | bytes 4194304 | tf_op jit(solution)/shard_map/all_to_all | solution.py:408
  62.1 31.4 %collective-permute-start.11 = (bf16[4,104,1024]{2,1,0:T(8,128)(2,1)S(1)}, bf16[4,104,1024]{2,1,0:T(8,128)(2,1)S(1)}, u32[]{:S(2)}, u32[]{:S(2)}) collective-permute-start(bf16[4,104,1024]{2,1,0:T(8,128)(2,1)S(1)} %pad_maximum_fusion.refs_0_), channel_id=1, source_target_pairs={{0,1},{1,0},{2,3},{3,2},{4,5},{5,4},{6,7},{7,6},{8,9},{9,8},{10,11... | collective-permute-start | bytes 2555912 | tf_op jit(solution)/shard_map/ppermute | solution.py:402
  63.5 28.7 %collective-permute-start.10 = (bf16[2,104,1024]{2,1,0:T(8,128)(2,1)S(1)}, bf16[2,104,1024]{2,1,0:T(8,128)(2,1)S(1)}, u32[]{:S(2)}, u32[]{:S(2)}) collective-permute-start(bf16[2,104,1024]{2,1,0:T(8,128)(2,1)S(1)} %slice.9), channel_id=1, source_target_pairs={{0,24},{1,7},{2,26},{3,1},{4,28},{5,3},{6,30},{7,5},{8,0},{9,15},{... | collective-permute-start | bytes 1277960 | tf_op jit(solution)/shard_map/ppermute | solution.py:398
  67.3 25.8 %collective-permute-start.9 = (bf16[2,104,1024]{2,1,0:T(8,128)(2,1)S(1)}, bf16[2,104,1024]{2,1,0:T(8,128)(2,1)S(1)}, u32[]{:S(2)}, u32[]{:S(2)}) collective-permute-start(bf16[2,104,1024]{2,1,0:T(8,128)(2,1)S(1)} %slice.8), channel_id=1, source_target_pairs={{0,8},{1,3},{2,10},{3,5},{4,12},{5,7},{6,14},{7,1},{8,16},{9,11},{... | collective-permute-start | bytes 1277960 | tf_op jit(solution)/shard_map/ppermute | solution.py:398
  67.4 26.5 %collective-permute-start.13 = (bf16[4,104,1024]{2,1,0:T(8,128)(2,1)}, bf16[4,104,1024]{2,1,0:T(8,128)(2,1)S(1)}, u32[]{:S(2)}, u32[]{:S(2)}) collective-permute-start(bf16[4,104,1024]{2,1,0:T(8,128)(2,1)} %collective-permute-done.8.refs_2_), channel_id=1, source_target_pairs={{0,1},{1,0},{2,3},{3,2},{4,5},{5,4},{6,7},{7,6},{8,9},{9,8},{10,11... | collective-permute-start | bytes 2555912 | tf_op jit(solution)/shard_map/ppermute | solution.py:402
  68.0 27.0 %collective-permute-start.12 = (bf16[4,104,1024]{2,1,0:T(8,128)(2,1)}, bf16[4,104,1024]{2,1,0:T(8,128)(2,1)S(1)}, u32[]{:S(2)}, u32[]{:S(2)}) collective-permute-start(bf16[4,104,1024]{2,1,0:T(8,128)(2,1)} %collective-permute-done.7.refs_1_), channel_id=1, source_target_pairs={{0,1},{1,0},{2,3},{3,2},{4,5},{5,4},{6,7},{7,6},{8,9},{9,8},{10,11... | collective-permute-start | bytes 2555912 | tf_op jit(solution)/shard_map/ppermute | solution.py:402
  92.2 1.8 %collective-permute-start.15 = (bf16[2,104,1024]{2,1,0:T(8,128)(2,1)S(1)}, bf16[2,104,1024]{2,1,0:T(8,128)(2,1)S(1)}, u32[]{:S(2)}, u32[]{:S(2)}) collective-permute-start(bf16[2,104,1024]{2,1,0:T(8,128)(2,1)S(1)} %collective-permute-done.10.refs_4_), channel_id=1, source_target_pairs={{0,1},{1,0},{2,3},{3,2},{4,5},{5,4},{6,7},{7,6},{8,9},{9,8},{10,11... | collective-permute-start | bytes 1277960 | tf_op jit(solution)/shard_map/ppermute | solution.py:402
  93.1 1.8 %collective-permute-start.14 = (bf16[2,104,1024]{2,1,0:T(8,128)(2,1)S(1)}, bf16[2,104,1024]{2,1,0:T(8,128)(2,1)S(1)}, u32[]{:S(2)}, u32[]{:S(2)}) collective-permute-start(bf16[2,104,1024]{2,1,0:T(8,128)(2,1)S(1)} %collective-permute-done.9.refs_3_), channel_id=1, source_target_pairs={{0,1},{1,0},{2,3},{3,2},{4,5},{5,4},{6,7},{7,6},{8,9},{9,8},{10,11... | collective-permute-start | bytes 1277960 | tf_op jit(solution)/shard_map/ppermute | solution.py:402

commit v4 on v3

--- a/solution.py
+++ b/solution.py
@@ -287,20 +287,27 @@
     )(z4, off, diag, gb, order)
 
 
-def fold_kernel(*refs):
-    parts, (f_ref, diag_ref, held, marks) = refs[: 2 * len(LINES)], refs[2 * len(LINES) :]
+def finish_kernel(target_ref, ret_ref, *refs):
+    pieces = 2 * len(LINES)
+    parts = refs[:pieces]
+    out_ref, route, held, marks, response, panel, made, out_sems = refs[pieces:]
+    code = jnp.transpose(jnp.broadcast_to(target_ref[...], (128, ROWS)))
+    scale = jnp.where(code >= SLOTS, 1.0 / HALF_SCALE, 1.0)
+    target = code & (SLOTS - 1)
+    for j in range(0, SLOTS, 128):
+        route[:, j : j + 128] = jnp.where(iota((ROWS, 128), 1) + j == target, scale, 0.0).astype(BF16)
     own = lax.axis_index("owner")
     core, x, y = own & 1, (own >> 1) & 3, own >> 3
     slot = 0
     for side in range(2):
         c = core if side == 0 else 1 - core
         for m, (away, first) in enumerate(LINES):
-            for k in range(parts[side * len(LINES) + m].shape[0]):
+            block = parts[side * len(LINES) + m]
+            for k in range(block.shape[0]):
                 dx = jnp.where(c == 0, NEAR[k + first], away)
                 dy = jnp.where(c == 0, away, NEAR[k + first])
                 start = ((((y + dy) & 3) * 4 + ((x + dx) & 3)) * 2 + c) * OWN
                 at = pl.ds(pl.multiple_of(start, OWN), OWN)
-                block = parts[side * len(LINES) + m]
                 for j in range(3):
                     held[j, at, :] = block[k, j * OWN : (j + 1) * OWN, :]
                 marks[slot] = block[k, 3 * OWN :, :]
@@ -308,52 +315,24 @@
     total = jnp.sum(marks[...].astype(F32), axis=0)
     inv0 = total[0:1] + total[1:2] + total[2:3]
     inv3 = total[3:4] + total[4:5] + total[5:6]
-    ratio = total[6:7] + total[7:8]
-    r = iota((DROWS, PORTS), 0)
-    diag_ref[...] = jnp.where(r == 0, inv0, jnp.where(r == 1, inv3, 0.0))
-    tile = 256
-    for t in range(0, PORTS, tile):
-        acc = jnp.dot(held[1], held[0, :, t : t + tile], preferred_element_type=F32)
-        on = iota((PORTS, tile), 0) == iota((PORTS, tile), 1) + t
-        mid = (jnp.where(on, ratio[:, t : t + tile], 0.0) - acc).astype(BF16)
-        f_ref[t : t + tile, :] = jnp.transpose(jnp.dot(held[2], mid, preferred_element_type=F32)).astype(BF16)
-
-
-def fold(parts):
-    return pl.pallas_call(
-        fold_kernel,
-        in_specs=[IN_VMEM] * (2 * len(LINES)),
-        out_shape=[pltpu.HBM((PORTS, PORTS), BF16), pltpu.VMEM((DROWS, PORTS), F32)],
-        scratch_shapes=[
-            pltpu.VMEM((3, PORTS, PORTS), BF16),
-            pltpu.VMEM((32, DROWS, PORTS), BF16),
-        ],
-        compiler_params=params(24),
-        cost_estimate=cost(4 * PORTS**3, 9 << 20),
-        name="fold",
-    )(*[vmem(part) for part in parts])
-
-
-def finish_kernel(target_ref, ret_ref, f_ref, diag_ref, out_ref, route, response, scaled, coupling, made, in_sem, out_sems):
-    load = pltpu.make_async_copy(f_ref, coupling, in_sem)
-    load.start()
-    code = jnp.transpose(jnp.broadcast_to(target_ref[...], (128, ROWS)))
-    scale = jnp.where(code >= SLOTS, 1.0 / HALF_SCALE, 1.0)
-    target = code & (SLOTS - 1)
-    for j in range(0, SLOTS, 128):
-        route[:, j : j + 128] = jnp.where(iota((ROWS, 128), 1) + j == target, scale, 0.0).astype(BF16)
-    for n in range(0, PORTS, 256):
-        at = slice(n, n + 256)
+    inv2 = inv0 * (total[6:7] + total[7:8])
+    wide = 256
+    for n in range(0, PORTS, wide):
+        at = slice(n, n + wide)
         piece = jnp.dot(route[...], ret_ref[:, at], preferred_element_type=F32)
         response[:, at] = piece
-        scaled[:, at] = (piece * diag_ref[0:1, at]).astype(BF16)
-    load.wait()
+        panel[0, :, at] = (piece * inv0[:, at]).astype(BF16)
+    for n in range(0, PORTS, wide):
+        at = slice(n, n + wide)
+        panel[1, :, at] = across(panel[0], held[0, at, :]).astype(BF16)
+    for n in range(0, PORTS, wide):
+        at = slice(n, n + wide)
+        panel[0, :, at] = (response[:, at] * inv2[:, at] - across(panel[1], held[1, at, :])).astype(BF16)
     stores = []
-    tile = 128
+    tile = 256
     for k, r in enumerate(range(0, ROWS, tile)):
         at = slice(r, r + tile)
-        coupled = jnp.dot(scaled[at, :], coupling[...], preferred_element_type=F32)
-        made[at, :] = response[at, :] * diag_ref[1:2, :] - coupled
+        made[at, :] = response[at, :] * inv3 - across(panel[0, at, :], held[2])
         store = pltpu.make_async_copy(made.at[at], out_ref.at[at], out_sems.at[k])
         store.start()
         stores.append(store)
@@ -361,25 +340,29 @@
         store.wait()
 
 
-def finish(target, returned, f, diag):
+def across(rows, matrix):
+    return lax.dot_general(rows, matrix, (((1,), (1,)), ((), ())), preferred_element_type=F32)
+
+
+def finish(target, returned, parts):
     return pl.pallas_call(
         finish_kernel,
-        in_specs=[IN_VMEM, IN_VMEM, ANYWHERE, IN_VMEM],
+        in_specs=[IN_VMEM] * (2 + len(parts)),
         out_specs=ANYWHERE,
         out_shape=pltpu.HBM((ROWS, PORTS), F32),
         scratch_shapes=[
             pltpu.VMEM((ROWS, SLOTS), BF16),
+            pltpu.VMEM((3, PORTS, PORTS), BF16),
+            pltpu.VMEM((32, DROWS, PORTS), BF16),
             pltpu.VMEM((ROWS, PORTS), F32),
-            pltpu.VMEM((ROWS, PORTS), BF16),
-            pltpu.VMEM((PORTS, PORTS), BF16),
+            pltpu.VMEM((2, ROWS, PORTS), BF16),
             pltpu.VMEM((ROWS, PORTS), F32),
-            pltpu.SemaphoreType.DMA,
-            pltpu.SemaphoreType.DMA((4,)),
+            pltpu.SemaphoreType.DMA((2,)),
         ],
-        compiler_params=params(24),
-        cost_estimate=cost(4 * ROWS * PORTS * PORTS, 6 << 20),
+        compiler_params=params(28),
+        cost_estimate=cost(8 * ROWS * PORTS * PORTS, 6 << 20),
         name="finish",
-    )(vmem(target), vmem(returned), hbm(f), vmem(diag))
+    )(vmem(target), vmem(returned), *[vmem(part) for part in parts])
 
 
 def group_swap(value, mask):
@@ -422,10 +405,9 @@
     far_low, far_high = chip_shift(left[:2], 1, 1), chip_shift(right[2:], -1, 1)
     parts = [line, left, right, far_low, far_high]
     parts = parts + [core_swap(part) for part in parts]
-    f, inverses = fold(parts)
     answers = apply_maps(arrived, subcircuit_maps)
     returned = exchange(answers)
-    return finish(target, returned, f, inverses)
+    return finish(target, returned, parts)
 
 
 def solution(mesh):

time: 109 us -> 121 us (1.11)
  local copies, waits for them, and re-layouts: 2.08 us -> 14.6 us
  Pallas kernels: 25.4 us -> 19.1 us
  waiting for transfers between devices: 40.7 us -> 46.3 us
    unnamed x2 -> x38, local copies, waits for them, and re-layouts: 0.01 us -> 14.6 us
    pallas_call x2 -> x1, Pallas kernels: 12.4 us -> 6.02 us  [finish(): pl.pallas_call(finish_kernel, in_specs=[IN_VMEM] * (2 + len(parts)), out_...]
    ppermute x7, waiting for transfers between devices: 30.8 us -> 35.1 us  [chip_shift(): return lax.ppermute(value, 'owner', pairs)]
    all_to_all x2, waiting for transfers between devices: 0.01 us -> 3.58 us  [exchange(): lax.all_to_all(value, 'owner', split_axis=0, concat_axis=0, tiled=True)]
    ppermute x5, starting transfers between devices: 1.67 us -> 3.12 us  [core_swap(): return lax.ppermute(value, 'owner', [(o, o ^ 1) for o in range(OWNERS)])]
    ppermute x5, waiting for transfers between devices: 1.4 us -> 0.01 us  [core_swap(): return lax.ppermute(value, 'owner', [(o, o ^ 1) for o in range(OWNERS)])]
  transfers between devices with their start and end apart: 18 -> 18, of which waited for: 10 -> 6; matrix products, arithmetic and copies ran while one was open for 2% -> 1% of each run, Pallas kernels for 17% -> 8%
where the time goes in v4:
time: 121 us; the launch traced here: 120 us
  waiting for transfers between devices  46.3 us (38%)
  starting transfers between devices  38.4 us (32%)
  Pallas kernels  19.1 us (16%)
  local copies, waits for them, and re-layouts  14.6 us (12%)
    ppermute x7, waiting for transfers between devices, chip_shift(): return lax.ppermute(value, 'owner', pairs)  35.1 us
    all_to_all x2, starting transfers between devices, exchange(): lax.all_to_all(value, 'owner', split_axis=0, concat_axis=0, tiled=True)  15.7 us
    unnamed x38, local copies, waits for them, and re-layouts  14.6 us
    ppermute x4, starting transfers between devices, group_swap(): return lax.ppermute(value, 'group', [(i, i ^ mask) for i in range(8)])  10 us
    ppermute x7, starting transfers between devices, chip_shift(): return lax.ppermute(value, 'owner', pairs)  9.57 us
    ppermute x4, waiting for transfers between devices, group_swap(): return lax.ppermute(value, 'group', [(i, i ^ mask) for i in range(8)])  7.66 us
    pallas_call x1, Pallas kernels, apply_maps(): pl.pallas_call(maps_kernel, in_specs=[IN_VMEM, ANYWHERE], out_specs=ANYWH...  7.05 us
    pallas_call x1, Pallas kernels, finish(): pl.pallas_call(finish_kernel, in_specs=[IN_VMEM] * (2 + len(parts)), out_...  6.02 us
  transfers between devices with their start and end apart: 18, of which 6 were waited for; matrix products, arithmetic and copies ran while one was open for 1% of the time, Pallas kernels for 8%

profile of v4, /device:TPU:1, one launch (start us, length us, event | category | flops | bytes accessed | tf_op | source)
XLA Modules:
  0.0 119.9 jit_solution(12996319864317103810)
XLA Ops:
  0.0 3.6 %prep.1 = (bf16[1024,1024]{1,0:T(8,128)(2,1)}, s32[1,512]{1,0:T(1,128)S(1)}) custom-call(s32[1,512]{1,0:T(1,128)} %bitcast.21, s32[1,512]{1,0:T(1,128)} %bitcast.22, s32[1,512]{1,0:T(1,128)} %bitcast.23, bf16[512,1024]{1,0:T(8,128)(2,1)} %rows_ref.1), custom_call_target="tpu_custom_call" | custom-call | flops 1073741824 | bytes 4194304 | tf_op jit(solution)/shard_map/prep/pallas_call | solution.py:137
  3.6 8.6 %all-to-all-start = ((bf16[32,32,1024]{2,1,0:T(8,128)(2,1)}), bf16[32,32,1024]{2,1,0:T(8,128)(2,1)S(1)}, u32[]{:S(2)}, u32[]{:S(2)}) async-start(bf16[32,32,1024]{2,1,0:T(8,128)(2,1)} %bitcast.16), calls=%async_computation | async-start | bytes 4194304 | tf_op jit(solution)/shard_map/all_to_all | solution.py:391
  12.2 1.0 label.1.z0_ref
  13.1 1.7 %collective-permute-start = (bf16[40,1024]{1,0:T(8,128)(2,1)S(1)}, bf16[40,1024]{1,0:T(8,128)(2,1)S(1)}, u32[]{:S(2)}, u32[]{:S(2)}) collective-permute-start(bf16[40,1024]{1,0:T(8,128)(2,1)S(1)} %label.1.z0_ref), channel_id=1, source_target_pairs={{0,32},{32,0},{64,96},{96,64},{128,160},{160,128},{192,224},{224,1... | collective-permute-start | bytes 245768 | tf_op jit(solution)/shard_map/ppermute | solution.py:369
  14.9 3.0 %collective-permute-start.1 = (bf16[40,1024]{1,0:T(8,128)(2,1)S(1)}, bf16[40,1024]{1,0:T(8,128)(2,1)S(1)}, u32[]{:S(2)}, u32[]{:S(2)}) collective-permute-start(bf16[40,1024]{1,0:T(8,128)(2,1)S(1)} %label.1.z0_ref), channel_id=1, source_target_pairs={{0,64},{32,96},{64,0},{96,32},{128,192},{160,224},{192,128},{224,1... | collective-permute-start | bytes 245768 | tf_op jit(solution)/shard_map/ppermute | solution.py:369
  17.9 2.4 %collective-permute-done.1.z2_ref = bf16[40,1024]{1,0:T(8,128)(2,1)S(1)} collective-permute-done((bf16[40,1024]{1,0:T(8,128)(2,1)S(1)}, bf16[40,1024]{1,0:T(8,128)(2,1)S(1)}, u32[]{:S(2)}, u32[]{:S(2)}) %collective-permute-start.1) | collective-permute-done | bytes 81952 | tf_op jit(solution)/shard_map/ppermute | solution.py:369
  20.3 3.0 %collective-permute-done.2.z3_ref = bf16[40,1024]{1,0:T(8,128)(2,1)S(1)} collective-permute-done((bf16[40,1024]{1,0:T(8,128)(2,1)S(1)}, bf16[40,1024]{1,0:T(8,128)(2,1)S(1)}, u32[]{:S(2)}, u32[]{:S(2)}) %collective-permute-start.2) | collective-permute-done | bytes 81952 | tf_op jit(solution)/shard_map/ppermute | solution.py:369
  23.3 1.0 low_levels.1
  24.2 5.3 %collective-permute-start.3 = (bf16[40,1024]{1,0:T(8,128)(2,1)S(1)}, bf16[40,1024]{1,0:T(8,128)(2,1)S(1)}, u32[]{:S(2)}, u32[]{:S(2)}) collective-permute-start(bf16[40,1024]{1,0:T(8,128)(2,1)S(1)} %get-tuple-element.13), channel_id=1, source_target_pairs={{0,128},{32,160},{64,192},{96,224},{128,0},{160,32},{192,64},{224,... | collective-permute-start | bytes 245768 | tf_op jit(solution)/shard_map/ppermute | solution.py:369
  29.5 2.3 %collective-permute-done.3.z4_ref = bf16[40,1024]{1,0:T(8,128)(2,1)S(1)} collective-permute-done((bf16[40,1024]{1,0:T(8,128)(2,1)S(1)}, bf16[40,1024]{1,0:T(8,128)(2,1)S(1)}, u32[]{:S(2)}, u32[]{:S(2)}) %collective-permute-start.3) | collective-permute-done | bytes 81952 | tf_op jit(solution)/shard_map/ppermute | solution.py:369
  32.3 2.7 %collective-permute-start.6 = (bf16[104,1024]{1,0:T(8,128)(2,1)S(1)}, bf16[104,1024]{1,0:T(8,128)(2,1)S(1)}, u32[]{:S(2)}, u32[]{:S(2)}) collective-permute-start(bf16[104,1024]{1,0:T(8,128)(2,1)S(1)} %top_level.1), channel_id=1, source_target_pairs={{0,4},{1,17},{2,6},{3,19},{4,0},{5,21},{6,2},{7,23},{8,12},{9,25},... | collective-permute-start | bytes 638984 | tf_op jit(solution)/shard_map/ppermute | solution.py:381
  36.5 3.6 %all-to-all-done = bf16[32,32,1024]{2,1,0:T(8,128)(2,1)S(1)} async-done(((bf16[32,32,1024]{2,1,0:T(8,128)(2,1)}), bf16[32,32,1024]{2,1,0:T(8,128)(2,1)S(1)}, u32[]{:S(2)}, u32[]{:S(2)}) %all-to-all-start) | async-done | bytes 2097184 | tf_op jit(solution)/shard_map/all_to_all | solution.py:391
  40.0 7.1 %apply_maps.1 = bf16[1024,1024]{1,0:T(8,128)(2,1)} custom-call(bf16[1024,1024]{1,0:T(8,128)(2,1)S(1)} %bitcast.13, bf16[2,1024,1024]{2,1,0:T(8,128)(2,1)} %maps_ref.1), custom_call_target="tpu_custom_call" | custom-call | flops 4294967296 | bytes 8388608 | tf_op jit(solution)/shard_map/apply_maps/pallas_call | solution.py:196
  47.1 7.1 %all-to-all-start.1 = ((bf16[32,32,1024]{2,1,0:T(8,128)(2,1)}), bf16[32,32,1024]{2,1,0:T(8,128)(2,1)S(1)}, u32[]{:S(2)}, u32[]{:S(2)}) async-start(bf16[32,32,1024]{2,1,0:T(8,128)(2,1)} %bitcast.15), calls=%async_computation.1 | async-start | bytes 4194304 | tf_op jit(solution)/shard_map/all_to_all | solution.py:391
  55.0 1.1 pad_maximum_fusion.refs_0_
  56.1 1.5 %collective-permute-start.7 = (bf16[4,104,1024]{2,1,0:T(8,128)(2,1)S(1)}, bf16[4,104,1024]{2,1,0:T(8,128)(2,1)S(1)}, u32[]{:S(2)}, u32[]{:S(2)}) collective-permute-start(bf16[4,104,1024]{2,1,0:T(8,128)(2,1)S(1)} %pad_maximum_fusion.refs_0_), channel_id=1, source_target_pairs={{0,8},{1,3},{2,10},{3,5},{4,12},{5,7},{6,14},{7,1},{8,16},{9,11},{... | collective-permute-start | bytes 2555912 | tf_op jit(solution)/shard_map/ppermute | solution.py:381
  57.6 1.3 %collective-permute-start.8 = (bf16[4,104,1024]{2,1,0:T(8,128)(2,1)S(1)}, bf16[4,104,1024]{2,1,0:T(8,128)(2,1)S(1)}, u32[]{:S(2)}, u32[]{:S(2)}) collective-permute-start(bf16[4,104,1024]{2,1,0:T(8,128)(2,1)S(1)} %pad_maximum_fusion.refs_0_), channel_id=1, source_target_pairs={{0,24},{1,7},{2,26},{3,1},{4,28},{5,3},{6,30},{7,5},{8,0},{9,15},{... | collective-permute-start | bytes 2555912 | tf_op jit(solution)/shard_map/ppermute | solution.py:381
  58.9 1.0 collective-permute-start.11
  59.9 29.9 %collective-permute-done.7.refs_1_ = bf16[4,104,1024]{2,1,0:T(8,128)(2,1)S(1)} collective-permute-done((bf16[4,104,1024]{2,1,0:T(8,128)(2,1)S(1)}, bf16[4,104,1024]{2,1,0:T(8,128)(2,1)S(1)}, u32[]{:S(2)}, u32[]{:S(2)}) %collective-permute-start.7) | collective-permute-done | bytes 852000 | tf_op jit(solution)/shard_map/ppermute | solution.py:381
  90.6 2.6 %collective-permute-start.10 = (bf16[2,104,1024]{2,1,0:T(8,128)(2,1)S(1)}, bf16[2,104,1024]{2,1,0:T(8,128)(2,1)S(1)}, u32[]{:S(2)}, u32[]{:S(2)}) collective-permute-start(bf16[2,104,1024]{2,1,0:T(8,128)(2,1)S(1)} %slice.9), channel_id=1, source_target_pairs={{0,24},{1,7},{2,26},{3,1},{4,28},{5,3},{6,30},{7,5},{8,0},{9,15},{... | collective-permute-start | bytes 1277960 | tf_op jit(solution)/shard_map/ppermute | solution.py:381
  93.2 5.2 %collective-permute-done.9.refs_3_ = bf16[2,104,1024]{2,1,0:T(8,128)(2,1)S(1)} collective-permute-done((bf16[2,104,1024]{2,1,0:T(8,128)(2,1)S(1)}, bf16[2,104,1024]{2,1,0:T(8,128)(2,1)S(1)}, u32[]{:S(2)}, u32[]{:S(2)}) %collective-permute-start.9) | collective-permute-done | bytes 426016 | tf_op jit(solution)/shard_map/ppermute | solution.py:381
  98.3 1.3 %collective-permute-start.14 = (bf16[2,104,1024]{2,1,0:T(8,128)(2,1)S(1)}, bf16[2,104,1024]{2,1,0:T(8,128)(2,1)S(1)}, u32[]{:S(2)}, u32[]{:S(2)}) collective-permute-start(bf16[2,104,1024]{2,1,0:T(8,128)(2,1)S(1)} %collective-permute-done.9.refs_3_), channel_id=1, source_target_pairs={{0,1},{1,0},{2,3},{3,2},{4,5},{5,4},{6,7},{7,6},{8,9},{9,8},{10,11... | collective-permute-start | bytes 1277960 | tf_op jit(solution)/shard_map/ppermute | solution.py:385
  100.6 0.9 copy-done.5
  104.9 1.2 copy-done.1
  106.0 1.2 copy-done.3
  107.2 1.2 copy-done.6
  108.4 1.2 copy-done.8
  109.5 1.2 copy-done.10
  110.7 1.0 copy-done.12
  111.7 1.0 copy-done.14
  112.7 1.0 copy-done.16
  113.7 6.0 %finish.1 = f32[512,1024]{1,0:T(8,128)} custom-call(s32[1,512]{1,0:T(1,128)S(1)} %get-tuple-element.11.target_ref, bf16[1024,1024]{1,0:T(8,128)(2,1)S(1)} %bitcast.12, bf16[4,104,1024]{2,1,0:T(8,128)(2,1)S(1)} %pad_maximum_fusion.refs_0_, bf16[4,104,1024]{2,1,0:T(8,128)(2,1)S(1)} %copy-done.1, bf16[4,104,1024]{2,1,0:T(8,128)(2,1)S(1)} %copy-done.3, ...), custom_call_target="tpu_custom_call" | custom-call | flops 4294967296 | bytes 6291456 | tf_op jit(solution)/shard_map/finish/pallas_call | solution.py:348
  (51 shorter events, 7.9 us)
Async XLA Ops:
  3.6 19.7 %copy-start.4 = (s32[3,1024]{1,0:T(4,128)S(1)}, s32[3,1024]{1,0:T(4,128)}, u32[]{:S(2)}) copy-start(s32[3,1024]{1,0:T(4,128)} %order_ref.3) | copy-start | bytes 36868
  3.6 36.5 %all-to-all-start = ((bf16[32,32,1024]{2,1,0:T(8,128)(2,1)}), bf16[32,32,1024]{2,1,0:T(8,128)(2,1)S(1)}, u32[]{:S(2)}, u32[]{:S(2)}) async-start(bf16[32,32,1024]{2,1,0:T(8,128)(2,1)} %bitcast.16), calls=%async_computation | async-start | bytes 4194304 | tf_op jit(solution)/shard_map/all_to_all | solution.py:391
  13.1 4.7 %collective-permute-start = (bf16[40,1024]{1,0:T(8,128)(2,1)S(1)}, bf16[40,1024]{1,0:T(8,128)(2,1)S(1)}, u32[]{:S(2)}, u32[]{:S(2)}) collective-permute-start(bf16[40,1024]{1,0:T(8,128)(2,1)S(1)} %label.1.z0_ref), channel_id=1, source_target_pairs={{0,32},{32,0},{64,96},{96,64},{128,160},{160,128},{192,224},{224,1... | collective-permute-start | bytes 245768 | tf_op jit(solution)/shard_map/ppermute | solution.py:369
  14.9 5.4 %collective-permute-start.1 = (bf16[40,1024]{1,0:T(8,128)(2,1)S(1)}, bf16[40,1024]{1,0:T(8,128)(2,1)S(1)}, u32[]{:S(2)}, u32[]{:S(2)}) collective-permute-start(bf16[40,1024]{1,0:T(8,128)(2,1)S(1)} %label.1.z0_ref), channel_id=1, source_target_pairs={{0,64},{32,96},{64,0},{96,32},{128,192},{160,224},{192,128},{224,1... | collective-permute-start | bytes 245768 | tf_op jit(solution)/shard_map/ppermute | solution.py:369
  17.9 5.4 %collective-permute-start.2 = (bf16[40,1024]{1,0:T(8,128)(2,1)S(1)}, bf16[40,1024]{1,0:T(8,128)(2,1)S(1)}, u32[]{:S(2)}, u32[]{:S(2)}) collective-permute-start(bf16[40,1024]{1,0:T(8,128)(2,1)S(1)} %label.1.z0_ref), channel_id=1, source_target_pairs={{0,96},{32,64},{64,32},{96,0},{128,224},{160,192},{192,160},{224,1... | collective-permute-start | bytes 245768 | tf_op jit(solution)/shard_map/ppermute | solution.py:369
  24.2 7.6 %collective-permute-start.3 = (bf16[40,1024]{1,0:T(8,128)(2,1)S(1)}, bf16[40,1024]{1,0:T(8,128)(2,1)S(1)}, u32[]{:S(2)}, u32[]{:S(2)}) collective-permute-start(bf16[40,1024]{1,0:T(8,128)(2,1)S(1)} %get-tuple-element.13), channel_id=1, source_target_pairs={{0,128},{32,160},{64,192},{96,224},{128,0},{160,32},{192,64},{224,... | collective-permute-start | bytes 245768 | tf_op jit(solution)/shard_map/ppermute | solution.py:369
  32.3 21.9 %collective-permute-start.6 = (bf16[104,1024]{1,0:T(8,128)(2,1)S(1)}, bf16[104,1024]{1,0:T(8,128)(2,1)S(1)}, u32[]{:S(2)}, u32[]{:S(2)}) collective-permute-start(bf16[104,1024]{1,0:T(8,128)(2,1)S(1)} %top_level.1), channel_id=1, source_target_pairs={{0,4},{1,17},{2,6},{3,19},{4,0},{5,21},{6,2},{7,23},{8,12},{9,25},... | collective-permute-start | bytes 638984 | tf_op jit(solution)/shard_map/ppermute | solution.py:381
  35.0 19.2 %collective-permute-start.5 = (bf16[104,1024]{1,0:T(8,128)(2,1)S(1)}, bf16[104,1024]{1,0:T(8,128)(2,1)S(1)}, u32[]{:S(2)}, u32[]{:S(2)}) collective-permute-start(bf16[104,1024]{1,0:T(8,128)(2,1)S(1)} %top_level.1), channel_id=1, source_target_pairs={{0,6},{1,25},{2,0},{3,27},{4,2},{5,29},{6,4},{7,31},{8,14},{9,1},{... | collective-permute-start | bytes 638984 | tf_op jit(solution)/shard_map/ppermute | solution.py:381
  35.9 18.4 %collective-permute-start.4 = (bf16[104,1024]{1,0:T(8,128)(2,1)S(1)}, bf16[104,1024]{1,0:T(8,128)(2,1)S(1)}, u32[]{:S(2)}, u32[]{:S(2)}) collective-permute-start(bf16[104,1024]{1,0:T(8,128)(2,1)S(1)} %top_level.1), channel_id=1, source_target_pairs={{0,2},{1,9},{2,4},{3,11},{4,6},{5,13},{6,0},{7,15},{8,10},{9,17},{... | collective-permute-start | bytes 638984 | tf_op jit(solution)/shard_map/ppermute | solution.py:381
  47.1 57.8 %all-to-all-start.1 = ((bf16[32,32,1024]{2,1,0:T(8,128)(2,1)}), bf16[32,32,1024]{2,1,0:T(8,128)(2,1)S(1)}, u32[]{:S(2)}, u32[]{:S(2)}) async-start(bf16[32,32,1024]{2,1,0:T(8,128)(2,1)} %bitcast.15), calls=%async_computation.1 | async-start | bytes 4194304 | tf_op jit(solution)/shard_map/all_to_all | solution.py:391
  56.1 33.6 %collective-permute-start.7 = (bf16[4,104,1024]{2,1,0:T(8,128)(2,1)S(1)}, bf16[4,104,1024]{2,1,0:T(8,128)(2,1)S(1)}, u32[]{:S(2)}, u32[]{:S(2)}) collective-permute-start(bf16[4,104,1024]{2,1,0:T(8,128)(2,1)S(1)} %pad_maximum_fusion.refs_0_), channel_id=1, source_target_pairs={{0,8},{1,3},{2,10},{3,5},{4,12},{5,7},{6,14},{7,1},{8,16},{9,11},{... | collective-permute-start | bytes 2555912 | tf_op jit(solution)/shard_map/ppermute | solution.py:381
  57.6 32.8 %collective-permute-start.8 = (bf16[4,104,1024]{2,1,0:T(8,128)(2,1)S(1)}, bf16[4,104,1024]{2,1,0:T(8,128)(2,1)S(1)}, u32[]{:S(2)}, u32[]{:S(2)}) collective-permute-start(bf16[4,104,1024]{2,1,0:T(8,128)(2,1)S(1)} %pad_maximum_fusion.refs_0_), channel_id=1, source_target_pairs={{0,24},{1,7},{2,26},{3,1},{4,28},{5,3},{6,30},{7,5},{8,0},{9,15},{... | collective-permute-start | bytes 2555912 | tf_op jit(solution)/shard_map/ppermute | solution.py:381
  58.9 41.7 %collective-permute-start.11 = (bf16[4,104,1024]{2,1,0:T(8,128)(2,1)S(1)}, bf16[4,104,1024]{2,1,0:T(8,128)(2,1)S(1)}, u32[]{:S(2)}, u32[]{:S(2)}) collective-permute-start(bf16[4,104,1024]{2,1,0:T(8,128)(2,1)S(1)} %pad_maximum_fusion.refs_0_), channel_id=1, source_target_pairs={{0,1},{1,0},{2,3},{3,2},{4,5},{5,4},{6,7},{7,6},{8,9},{9,8},{10,11... | collective-permute-start | bytes 2555912 | tf_op jit(solution)/shard_map/ppermute | solution.py:385
  89.8 13.6 %copy-start = (bf16[4,104,1024]{2,1,0:T(8,128)(2,1)}, bf16[4,104,1024]{2,1,0:T(8,128)(2,1)S(1)}, u32[]{:S(2)}) copy-start(bf16[4,104,1024]{2,1,0:T(8,128)(2,1)S(1)} %collective-permute-done.7.refs_1_) | copy-start | bytes 2555908
  89.8 8.6 %collective-permute-start.9 = (bf16[2,104,1024]{2,1,0:T(8,128)(2,1)S(1)}, bf16[2,104,1024]{2,1,0:T(8,128)(2,1)S(1)}, u32[]{:S(2)}, u32[]{:S(2)}) collective-permute-start(bf16[2,104,1024]{2,1,0:T(8,128)(2,1)S(1)} %slice.8), channel_id=1, source_target_pairs={{0,8},{1,3},{2,10},{3,5},{4,12},{5,7},{6,14},{7,1},{8,16},{9,11},{... | collective-permute-start | bytes 1277960 | tf_op jit(solution)/shard_map/ppermute | solution.py:381
  89.9 11.6 %collective-permute-start.12 = (bf16[4,104,1024]{2,1,0:T(8,128)(2,1)S(1)}, bf16[4,104,1024]{2,1,0:T(8,128)(2,1)S(1)}, u32[]{:S(2)}, u32[]{:S(2)}) collective-permute-start(bf16[4,104,1024]{2,1,0:T(8,128)(2,1)S(1)} %collective-permute-done.7.refs_1_), channel_id=1, source_target_pairs={{0,1},{1,0},{2,3},{3,2},{4,5},{5,4},{6,7},{7,6},{8,9},{9,8},{10,11... | collective-permute-start | bytes 2555912 | tf_op jit(solution)/shard_map/ppermute | solution.py:385
  90.4 12.9 %copy-start.2 = (bf16[4,104,1024]{2,1,0:T(8,128)(2,1)}, bf16[4,104,1024]{2,1,0:T(8,128)(2,1)S(1)}, u32[]{:S(2)}) copy-start(bf16[4,104,1024]{2,1,0:T(8,128)(2,1)S(1)} %collective-permute-done.8.refs_2_) | copy-start | bytes 2555908
  90.4 12.0 %collective-permute-start.13 = (bf16[4,104,1024]{2,1,0:T(8,128)(2,1)S(1)}, bf16[4,104,1024]{2,1,0:T(8,128)(2,1)S(1)}, u32[]{:S(2)}, u32[]{:S(2)}) collective-permute-start(bf16[4,104,1024]{2,1,0:T(8,128)(2,1)S(1)} %collective-permute-done.8.refs_2_), channel_id=1, source_target_pairs={{0,1},{1,0},{2,3},{3,2},{4,5},{5,4},{6,7},{7,6},{8,9},{9,8},{10,11... | collective-permute-start | bytes 2555912 | tf_op jit(solution)/shard_map/ppermute | solution.py:385
  90.6 9.0 %collective-permute-start.10 = (bf16[2,104,1024]{2,1,0:T(8,128)(2,1)S(1)}, bf16[2,104,1024]{2,1,0:T(8,128)(2,1)S(1)}, u32[]{:S(2)}, u32[]{:S(2)}) collective-permute-start(bf16[2,104,1024]{2,1,0:T(8,128)(2,1)S(1)} %slice.9), channel_id=1, source_target_pairs={{0,24},{1,7},{2,26},{3,1},{4,28},{5,3},{6,30},{7,5},{8,0},{9,15},{... | collective-permute-start | bytes 1277960 | tf_op jit(solution)/shard_map/ppermute | solution.py:381
  98.3 5.0 %collective-permute-start.14 = (bf16[2,104,1024]{2,1,0:T(8,128)(2,1)S(1)}, bf16[2,104,1024]{2,1,0:T(8,128)(2,1)S(1)}, u32[]{:S(2)}, u32[]{:S(2)}) collective-permute-start(bf16[2,104,1024]{2,1,0:T(8,128)(2,1)S(1)} %collective-permute-done.9.refs_3_), channel_id=1, source_target_pairs={{0,1},{1,0},{2,3},{3,2},{4,5},{5,4},{6,7},{7,6},{8,9},{9,8},{10,11... | collective-permute-start | bytes 1277960 | tf_op jit(solution)/shard_map/ppermute | solution.py:385
  99.6 4.5 %collective-permute-start.15 = (bf16[2,104,1024]{2,1,0:T(8,128)(2,1)S(1)}, bf16[2,104,1024]{2,1,0:T(8,128)(2,1)S(1)}, u32[]{:S(2)}, u32[]{:S(2)}) collective-permute-start(bf16[2,104,1024]{2,1,0:T(8,128)(2,1)S(1)} %collective-permute-done.10.refs_4_), channel_id=1, source_target_pairs={{0,1},{1,0},{2,3},{3,2},{4,5},{5,4},{6,7},{7,6},{8,9},{9,8},{10,11... | collective-permute-start | bytes 1277960 | tf_op jit(solution)/shard_map/ppermute | solution.py:385
  100.6 0.9 copy-start.5
  101.5 0.9 copy-start.7
  102.4 0.9 copy-start.9
  104.9 1.2 copy-start.1
  106.0 1.2 copy-start.3
  107.2 1.2 copy-start.6
  108.4 1.2 copy-start.8
  109.5 1.2 copy-start.10
  110.7 1.0 copy-start.12
  111.7 1.0 copy-start.14
  112.7 1.0 copy-start.16
  (5 other events, 3.7 us)

commit v5 on v4

--- a/solution.py
+++ b/solution.py
@@ -22,7 +22,8 @@
 HALF_MARK = 32.0
 STEPS = (1, -1, 2)
 NEAR = (0, -1, 1, -2)
-LINES = ((0, 0), (-1, 0), (1, 0), (2, 0), (2, 2))
+NEAR_LINES = ((0, range(4)), (-1, range(4)), (1, range(4)))
+FAR_LINES = ((2, range(2)), (2, range(2, 4)))
 
 
 def iota(shape, dim):
@@ -207,7 +208,7 @@
             pltpu.SemaphoreType.DMA((2, 4)),
             pltpu.SemaphoreType.DMA((4,)),
         ],
-        compiler_params=params(28),
+        compiler_params=params(60),
         cost_estimate=cost(4 * SLOTS * PORTS * PORTS, 8 << 20),
         name="apply_maps",
     )(vmem(x), hbm(maps))
@@ -287,47 +288,97 @@
     )(z4, off, diag, gb, order)
 
 
-def finish_kernel(target_ref, ret_ref, *refs):
-    pieces = 2 * len(LINES)
-    parts = refs[:pieces]
-    out_ref, route, held, marks, response, panel, made, out_sems = refs[pieces:]
+def row_starts(side, lines):
+    own = lax.axis_index("owner")
+    core, x, y = own & 1, (own >> 1) & 3, own >> 3
+    c = core if side == 0 else 1 - core
+    starts = []
+    for away, blocks in lines:
+        for k in blocks:
+            dx = jnp.where(c == 0, NEAR[k], away)
+            dy = jnp.where(c == 0, away, NEAR[k])
+            start = ((((y + dy) & 3) * 4 + ((x + dx) & 3)) * 2 + c) * OWN
+            starts.append(pl.multiple_of(start, OWN))
+    return starts
+
+
+def arrange_kernel(*refs):
+    parts, (held_ref, diag_ref, marks, sems) = refs[:6], refs[6:]
+    copies = []
+    for side in range(2):
+        for n, start in enumerate(row_starts(side, NEAR_LINES)):
+            block = parts[3 * side + n // 4].at[n % 4]
+            for j in range(3):
+                copies.append(
+                    pltpu.make_async_copy(
+                        block.at[j * OWN : (j + 1) * OWN], held_ref.at[j, pl.ds(start, OWN), :], sems.at[j]
+                    )
+                )
+            copies.append(pltpu.make_async_copy(block.at[3 * OWN :], marks.at[12 * side + n], sems.at[3]))
+    for copy in copies:
+        copy.start()
+    for copy in copies:
+        copy.wait()
+    diag_ref[...] = jnp.sum(marks[...].astype(F32), axis=0)
+
+
+def arrange(parts):
+    return pl.pallas_call(
+        arrange_kernel,
+        in_specs=[ANYWHERE] * 6,
+        out_specs=[ANYWHERE, IN_VMEM],
+        out_shape=[pltpu.HBM((3, PORTS, PORTS), BF16), pltpu.VMEM((DROWS, PORTS), F32)],
+        scratch_shapes=[pltpu.VMEM((24, DROWS, PORTS), BF16), pltpu.SemaphoreType.DMA((4,))],
+        compiler_params=params(),
+        cost_estimate=cost(1 << 20, 11 << 20),
+        name="arrange",
+    )(*parts)
+
+
+def finish_kernel(target_ref, ret_ref, diag_ref, held_ref, *refs):
+    far_refs = refs[:4]
+    out_ref, route, held, far, response, panel, made, held_sems, far_sems, out_sems = refs[4:]
+    held_loads = [pltpu.make_async_copy(held_ref.at[j], held.at[j], held_sems.at[j]) for j in range(3)]
+    far_loads = [pltpu.make_async_copy(far_refs[p], far.at[p], far_sems.at[p]) for p in range(4)]
+    for load in held_loads[:1] + far_loads + held_loads[1:]:
+        load.start()
     code = jnp.transpose(jnp.broadcast_to(target_ref[...], (128, ROWS)))
     scale = jnp.where(code >= SLOTS, 1.0 / HALF_SCALE, 1.0)
     target = code & (SLOTS - 1)
     for j in range(0, SLOTS, 128):
         route[:, j : j + 128] = jnp.where(iota((ROWS, 128), 1) + j == target, scale, 0.0).astype(BF16)
-    own = lax.axis_index("owner")
-    core, x, y = own & 1, (own >> 1) & 3, own >> 3
-    slot = 0
-    for side in range(2):
-        c = core if side == 0 else 1 - core
-        for m, (away, first) in enumerate(LINES):
-            block = parts[side * len(LINES) + m]
-            for k in range(block.shape[0]):
-                dx = jnp.where(c == 0, NEAR[k + first], away)
-                dy = jnp.where(c == 0, away, NEAR[k + first])
-                start = ((((y + dy) & 3) * 4 + ((x + dx) & 3)) * 2 + c) * OWN
-                at = pl.ds(pl.multiple_of(start, OWN), OWN)
-                for j in range(3):
-                    held[j, at, :] = block[k, j * OWN : (j + 1) * OWN, :]
-                marks[slot] = block[k, 3 * OWN :, :]
-                slot += 1
-    total = jnp.sum(marks[...].astype(F32), axis=0)
+    wide = 256
+    for n in range(0, PORTS, wide):
+        at = slice(n, n + wide)
+        response[:, at] = jnp.dot(route[...], ret_ref[:, at], preferred_element_type=F32)
+    for load in far_loads:
+        load.wait()
+    total = diag_ref[...]
+    for p in range(4):
+        for k in range(2):
+            total = total + far[p, k, 3 * OWN :, :].astype(F32)
     inv0 = total[0:1] + total[1:2] + total[2:3]
     inv3 = total[3:4] + total[4:5] + total[5:6]
     inv2 = inv0 * (total[6:7] + total[7:8])
-    wide = 256
-    for n in range(0, PORTS, wide):
-        at = slice(n, n + wide)
-        piece = jnp.dot(route[...], ret_ref[:, at], preferred_element_type=F32)
-        response[:, at] = piece
-        panel[0, :, at] = (piece * inv0[:, at]).astype(BF16)
+    starts = [row_starts(side, FAR_LINES) for side in range(2)]
+
+    def ready(level):
+        held_loads[level].wait()
+        for p in range(4):
+            for k in range(2):
+                at = pl.ds(starts[p // 2][2 * (p % 2) + k], OWN)
+                held[level, at, :] = far[p, k, level * OWN : (level + 1) * OWN, :]
+
+    panel[0] = (response[...] * inv0).astype(BF16)
+    ready(0)
     for n in range(0, PORTS, wide):
         at = slice(n, n + wide)
         panel[1, :, at] = across(panel[0], held[0, at, :]).astype(BF16)
+    ready(1)
     for n in range(0, PORTS, wide):
         at = slice(n, n + wide)
         panel[0, :, at] = (response[:, at] * inv2[:, at] - across(panel[1], held[1, at, :])).astype(BF16)
+    ready(2)
     stores = []
     tile = 256
     for k, r in enumerate(range(0, ROWS, tile)):
@@ -344,25 +395,27 @@
     return lax.dot_general(rows, matrix, (((1,), (1,)), ((), ())), preferred_element_type=F32)
 
 
-def finish(target, returned, parts):
+def finish(target, returned, diag, held, far):
     return pl.pallas_call(
         finish_kernel,
-        in_specs=[IN_VMEM] * (2 + len(parts)),
+        in_specs=[IN_VMEM] * 3 + [ANYWHERE] * 5,
         out_specs=ANYWHERE,
         out_shape=pltpu.HBM((ROWS, PORTS), F32),
         scratch_shapes=[
             pltpu.VMEM((ROWS, SLOTS), BF16),
             pltpu.VMEM((3, PORTS, PORTS), BF16),
-            pltpu.VMEM((32, DROWS, PORTS), BF16),
+            pltpu.VMEM((4, 2, PACK, PORTS), BF16),
             pltpu.VMEM((ROWS, PORTS), F32),
             pltpu.VMEM((2, ROWS, PORTS), BF16),
             pltpu.VMEM((ROWS, PORTS), F32),
+            pltpu.SemaphoreType.DMA((3,)),
+            pltpu.SemaphoreType.DMA((4,)),
             pltpu.SemaphoreType.DMA((2,)),
         ],
         compiler_params=params(28),
-        cost_estimate=cost(8 * ROWS * PORTS * PORTS, 6 << 20),
+        cost_estimate=cost(8 * ROWS * PORTS * PORTS, 12 << 20),
         name="finish",
-    )(vmem(target), vmem(returned), *[vmem(part) for part in parts])
+    )(vmem(target), vmem(returned), vmem(diag), hbm(held), *far)
 
 
 def group_swap(value, mask):
@@ -401,13 +454,17 @@
     z, off, diag, gb = low_levels(z0, z1, z2, z3, pivot_order)
     pack = top_level(group_swap(z, 4), off, diag, gb, pivot_order)
     line = jnp.stack([pack] + [chip_shift(pack, step, 0) for step in STEPS])
+    line, arrived = lax.optimization_barrier((line, arrived))
     left, right = chip_shift(line, 1, 1), chip_shift(line, -1, 1)
+    answers = apply_maps(arrived, subcircuit_maps)
+    answers, left, right = lax.optimization_barrier((answers, left, right))
     far_low, far_high = chip_shift(left[:2], 1, 1), chip_shift(right[2:], -1, 1)
-    parts = [line, left, right, far_low, far_high]
-    parts = parts + [core_swap(part) for part in parts]
-    answers = apply_maps(arrived, subcircuit_maps)
+    near = [line, left, right]
+    held, diag_sum = arrange(near + [core_swap(part) for part in near])
     returned = exchange(answers)
-    return finish(target, returned, parts)
+    far_low, far_high, held, returned = lax.optimization_barrier((far_low, far_high, held, returned))
+    far = [far_low, far_high, core_swap(far_low), core_swap(far_high)]
+    return finish(target, returned, diag_sum, held, far)
 
 
 def solution(mesh):

time: 121 us -> 110 us (0.909)
  Pallas kernels: 19.1 us -> 49 us
  waiting for transfers between devices: 46.3 us -> 19.8 us
  local copies, waits for them, and re-layouts: 14.6 us -> 1.07 us
    pallas_call x1 -> x2, Pallas kernels: 6.02 us -> 34.3 us  [the longest x1 25.2 us: arrange(): pl.pallas_call(arrange_kernel, in_specs=[ANYWHERE] * 6, out_specs=[ANYWHE...]
    ppermute x7, waiting for transfers between devices: 35.1 us -> 9.53 us  [chip_shift(): return lax.ppermute(value, 'owner', pairs)]
    unnamed x38 -> x2, local copies, waits for them, and re-layouts: 14.6 us -> 0.01 us
    all_to_all x2, waiting for transfers between devices: 3.58 us -> 0.01 us  [exchange(): lax.all_to_all(value, 'owner', split_axis=0, concat_axis=0, tiled=True)]
    all_to_all x2, starting transfers between devices: 15.7 us -> 18.2 us  [exchange(): lax.all_to_all(value, 'owner', split_axis=0, concat_axis=0, tiled=True)]
    ppermute x5, waiting for transfers between devices: 0.01 us -> 2.33 us  [core_swap(): return lax.ppermute(value, 'owner', [(o, o ^ 1) for o in range(OWNERS)])]
    ppermute x5, starting transfers between devices: 3.12 us -> 1.42 us  [core_swap(): return lax.ppermute(value, 'owner', [(o, o ^ 1) for o in range(OWNERS)])]
    pallas_call x1, Pallas kernels: 7.05 us -> 8.64 us  [apply_maps(): pl.pallas_call(maps_kernel, in_specs=[IN_VMEM, ANYWHERE], out_specs=ANYWH...]
  transfers between devices with their start and end apart: 18 -> 18, of which waited for: 6 -> 11; matrix products, arithmetic and copies ran while one was open for 1% -> 1% of each run, Pallas kernels for 8% -> 33%
where the time goes in v5:
time: 110 us; the launch traced here: 109 us
  Pallas kernels  49 us (45%)
  starting transfers between devices  39.1 us (36%)
  waiting for transfers between devices  19.8 us (18%)
    pallas_call x1, Pallas kernels, arrange(): pl.pallas_call(arrange_kernel, in_specs=[ANYWHERE] * 6, out_specs=[ANYWHE...  25.2 us
    all_to_all x2, starting transfers between devices, exchange(): lax.all_to_all(value, 'owner', split_axis=0, concat_axis=0, tiled=True)  18.2 us
    ppermute x4, starting transfers between devices, group_swap(): return lax.ppermute(value, 'group', [(i, i ^ mask) for i in range(8)])  9.95 us
    ppermute x7, waiting for transfers between devices, chip_shift(): return lax.ppermute(value, 'owner', pairs)  9.53 us
    ppermute x7, starting transfers between devices, chip_shift(): return lax.ppermute(value, 'owner', pairs)  9.51 us
    pallas_call x1, Pallas kernels, finish(): pl.pallas_call(finish_kernel, in_specs=[IN_VMEM] * 3 + [ANYWHERE] * 5, ou...  9.12 us
    pallas_call x1, Pallas kernels, apply_maps(): pl.pallas_call(maps_kernel, in_specs=[IN_VMEM, ANYWHERE], out_specs=ANYWH...  8.64 us
    ppermute x4, waiting for transfers between devices, group_swap(): return lax.ppermute(value, 'group', [(i, i ^ mask) for i in range(8)])  7.95 us
  transfers between devices with their start and end apart: 18, of which 11 were waited for; matrix products, arithmetic and copies ran while one was open for 1% of the time, Pallas kernels for 33%

profile of v5, /device:TPU:1, one launch (start us, length us, event | category | flops | bytes accessed | tf_op | source)
XLA Modules:
  0.0 109.4 jit_solution(12223401143145070214)
XLA Ops:
  0.0 3.6 %prep.1 = (bf16[1024,1024]{1,0:T(8,128)(2,1)}, s32[1,512]{1,0:T(1,128)S(1)}) custom-call(s32[1,512]{1,0:T(1,128)} %bitcast.19, s32[1,512]{1,0:T(1,128)} %bitcast.20, s32[1,512]{1,0:T(1,128)} %bitcast.21, bf16[512,1024]{1,0:T(8,128)(2,1)} %rows_ref.1), custom_call_target="tpu_custom_call" | custom-call | flops 1073741824 | bytes 4194304 | tf_op jit(solution)/shard_map/prep/pallas_call | solution.py:138
  3.6 8.7 %all-to-all-start = ((bf16[32,32,1024]{2,1,0:T(8,128)(2,1)}), bf16[32,32,1024]{2,1,0:T(8,128)(2,1)}, u32[]{:S(2)}, u32[]{:S(2)}) async-start(bf16[32,32,1024]{2,1,0:T(8,128)(2,1)} %bitcast.13), calls=%async_computation | async-start | bytes 4194304 | tf_op jit(solution)/shard_map/all_to_all | solution.py:444
  12.2 1.0 label.1.z0_ref
  13.2 1.7 %collective-permute-start = (bf16[40,1024]{1,0:T(8,128)(2,1)S(1)}, bf16[40,1024]{1,0:T(8,128)(2,1)S(1)}, u32[]{:S(2)}, u32[]{:S(2)}) collective-permute-start(bf16[40,1024]{1,0:T(8,128)(2,1)S(1)} %label.1.z0_ref), channel_id=1, source_target_pairs={{0,32},{32,0},{64,96},{96,64},{128,160},{160,128},{192,224},{224,1... | collective-permute-start | bytes 245768 | tf_op jit(solution)/shard_map/ppermute | solution.py:422
  14.9 3.0 %collective-permute-start.1 = (bf16[40,1024]{1,0:T(8,128)(2,1)S(1)}, bf16[40,1024]{1,0:T(8,128)(2,1)S(1)}, u32[]{:S(2)}, u32[]{:S(2)}) collective-permute-start(bf16[40,1024]{1,0:T(8,128)(2,1)S(1)} %label.1.z0_ref), channel_id=1, source_target_pairs={{0,64},{32,96},{64,0},{96,32},{128,192},{160,224},{192,128},{224,1... | collective-permute-start | bytes 245768 | tf_op jit(solution)/shard_map/ppermute | solution.py:422
  17.9 2.4 %collective-permute-done.1.z2_ref = bf16[40,1024]{1,0:T(8,128)(2,1)S(1)} collective-permute-done((bf16[40,1024]{1,0:T(8,128)(2,1)S(1)}, bf16[40,1024]{1,0:T(8,128)(2,1)S(1)}, u32[]{:S(2)}, u32[]{:S(2)}) %collective-permute-start.1) | collective-permute-done | bytes 81952 | tf_op jit(solution)/shard_map/ppermute | solution.py:422
  20.3 3.1 %collective-permute-done.2.z3_ref = bf16[40,1024]{1,0:T(8,128)(2,1)S(1)} collective-permute-done((bf16[40,1024]{1,0:T(8,128)(2,1)S(1)}, bf16[40,1024]{1,0:T(8,128)(2,1)S(1)}, u32[]{:S(2)}, u32[]{:S(2)}) %collective-permute-start.2) | collective-permute-done | bytes 81952 | tf_op jit(solution)/shard_map/ppermute | solution.py:422
  23.4 1.0 low_levels.1
  24.4 5.2 %collective-permute-start.3 = (bf16[40,1024]{1,0:T(8,128)(2,1)S(1)}, bf16[40,1024]{1,0:T(8,128)(2,1)S(1)}, u32[]{:S(2)}, u32[]{:S(2)}) collective-permute-start(bf16[40,1024]{1,0:T(8,128)(2,1)S(1)} %get-tuple-element.23), channel_id=1, source_target_pairs={{0,128},{32,160},{64,192},{96,224},{128,0},{160,32},{192,64},{224,... | collective-permute-start | bytes 245768 | tf_op jit(solution)/shard_map/ppermute | solution.py:422
  29.6 2.4 %collective-permute-done.3.z4_ref = bf16[40,1024]{1,0:T(8,128)(2,1)S(1)} collective-permute-done((bf16[40,1024]{1,0:T(8,128)(2,1)S(1)}, bf16[40,1024]{1,0:T(8,128)(2,1)S(1)}, u32[]{:S(2)}, u32[]{:S(2)}) %collective-permute-start.3) | collective-permute-done | bytes 81952 | tf_op jit(solution)/shard_map/ppermute | solution.py:422
  32.1 0.5 top_level.1
  32.6 1.1 collective-permute-start.4
  33.6 1.7 %collective-permute-start.5 = (bf16[104,1024]{1,0:T(8,128)(2,1)S(1)}, bf16[104,1024]{1,0:T(8,128)(2,1)S(1)}, u32[]{:S(2)}, u32[]{:S(2)}) collective-permute-start(bf16[104,1024]{1,0:T(8,128)(2,1)S(1)} %top_level.1), channel_id=1, source_target_pairs={{0,6},{1,25},{2,0},{3,27},{4,2},{5,29},{6,4},{7,31},{8,14},{9,1},{... | collective-permute-start | bytes 638984 | tf_op jit(solution)/shard_map/ppermute | solution.py:434
  35.4 1.2 %collective-permute-start.6 = (bf16[104,1024]{1,0:T(8,128)(2,1)S(1)}, bf16[104,1024]{1,0:T(8,128)(2,1)S(1)}, u32[]{:S(2)}, u32[]{:S(2)}) collective-permute-start(bf16[104,1024]{1,0:T(8,128)(2,1)S(1)} %top_level.1), channel_id=1, source_target_pairs={{0,4},{1,17},{2,6},{3,19},{4,0},{5,21},{6,2},{7,23},{8,12},{9,25},... | collective-permute-start | bytes 638984 | tf_op jit(solution)/shard_map/ppermute | solution.py:434
  36.6 4.3 %collective-permute-done.4 = bf16[104,1024]{1,0:T(8,128)(2,1)S(1)} collective-permute-done((bf16[104,1024]{1,0:T(8,128)(2,1)S(1)}, bf16[104,1024]{1,0:T(8,128)(2,1)S(1)}, u32[]{:S(2)}, u32[]{:S(2)}) %collective-permute-start.4) | collective-permute-done | bytes 213024 | tf_op jit(solution)/shard_map/ppermute | solution.py:434
  40.9 2.9 %collective-permute-done.6 = bf16[104,1024]{1,0:T(8,128)(2,1)S(1)} collective-permute-done((bf16[104,1024]{1,0:T(8,128)(2,1)S(1)}, bf16[104,1024]{1,0:T(8,128)(2,1)S(1)}, u32[]{:S(2)}, u32[]{:S(2)}) %collective-permute-start.6) | collective-permute-done | bytes 213024 | tf_op jit(solution)/shard_map/ppermute | solution.py:434
  44.0 0.6 collective-permute-start.7
  44.5 2.2 %collective-permute-start.8 = (bf16[4,104,1024]{2,1,0:T(8,128)(2,1)S(1)}, bf16[4,104,1024]{2,1,0:T(8,128)(2,1)}, u32[]{:S(2)}, u32[]{:S(2)}) collective-permute-start(bf16[4,104,1024]{2,1,0:T(8,128)(2,1)S(1)} %pad_maximum_fusion.refs_0_), channel_id=1, source_target_pairs={{0,24},{1,7},{2,26},{3,1},{4,28},{5,3},{6,30},{7,5},{8,0},{9,15},{... | collective-permute-start | bytes 2555912 | tf_op jit(solution)/shard_map/ppermute | solution.py:434
  46.7 8.6 %apply_maps.1 = bf16[1024,1024]{1,0:T(8,128)(2,1)} custom-call(bf16[1024,1024]{1,0:T(8,128)(2,1)} %bitcast.9.x_ref, bf16[2,1024,1024]{2,1,0:T(8,128)(2,1)} %maps_ref.1), custom_call_target="tpu_custom_call" | custom-call | flops 4294967296 | bytes 8388608 | tf_op jit(solution)/shard_map/apply_maps/pallas_call | solution.py:197
  55.4 1.7 %collective-permute-done.7.refs_1_ = bf16[4,104,1024]{2,1,0:T(8,128)(2,1)S(1)} collective-permute-done((bf16[4,104,1024]{2,1,0:T(8,128)(2,1)S(1)}, bf16[4,104,1024]{2,1,0:T(8,128)(2,1)S(1)}, u32[]{:S(2)}, u32[]{:S(2)}) %collective-permute-start.7) | collective-permute-done | bytes 852000 | tf_op jit(solution)/shard_map/ppermute | solution.py:434
  57.1 9.6 %all-to-all-start.1 = ((bf16[32,32,1024]{2,1,0:T(8,128)(2,1)}), bf16[32,32,1024]{2,1,0:T(8,128)(2,1)}, u32[]{:S(2)}, u32[]{:S(2)}) async-start(bf16[32,32,1024]{2,1,0:T(8,128)(2,1)} %bitcast.14), calls=%async_computation.1 | async-start | bytes 4194304 | tf_op jit(solution)/shard_map/all_to_all | solution.py:444
  66.7 0.4 collective-permute-start.11
  67.3 0.3 collective-permute-start.13
  67.6 1.0 slice.7
  68.7 2.7 %collective-permute-start.10 = (bf16[2,104,1024]{2,1,0:T(8,128)(2,1)S(1)}, bf16[2,104,1024]{2,1,0:T(8,128)(2,1)S(1)}, u32[]{:S(2)}, u32[]{:S(2)}) collective-permute-start(bf16[2,104,1024]{2,1,0:T(8,128)(2,1)S(1)} %slice.7), channel_id=1, source_target_pairs={{0,24},{1,7},{2,26},{3,1},{4,28},{5,3},{6,30},{7,5},{8,0},{9,15},{... | collective-permute-start | bytes 1277960 | tf_op jit(solution)/shard_map/ppermute | solution.py:434
  71.6 0.2 collective-permute-done.13.refs_5_
  71.8 25.2 %arrange.1 = (bf16[3,1024,1024]{2,1,0:T(8,128)(2,1)}, f32[8,1024]{1,0:T(8,128)S(1)}) custom-call(bf16[4,104,1024]{2,1,0:T(8,128)(2,1)S(1)} %pad_maximum_fusion.refs_0_, bf16[4,104,1024]{2,1,0:T(8,128)(2,1)S(1)} %collective-permute-done.7.refs_1_, bf16[4,104,1024]{2,1,0:T(8,128)(2,1)} %collective-permute-done.8.refs_2_, ...), custom_call_target="tpu_custom_call" | custom-call | flops 1048576 | bytes 11534336 | tf_op jit(solution)/shard_map/arrange/pallas_call | solution.py:326
  97.0 0.6 collective-permute-done.9.refs_0_
  97.6 0.4 collective-permute-start.14
  98.1 1.3 %collective-permute-done.14.refs_2_ = bf16[2,104,1024]{2,1,0:T(8,128)(2,1)S(1)} collective-permute-done((bf16[2,104,1024]{2,1,0:T(8,128)(2,1)S(1)}, bf16[2,104,1024]{2,1,0:T(8,128)(2,1)S(1)}, u32[]{:S(2)}, u32[]{:S(2)}) %collective-permute-start.14) | collective-permute-done | bytes 426016 | tf_op jit(solution)/shard_map/ppermute | solution.py:438
  99.4 0.6 collective-permute-done.15.refs_3_
  100.1 9.1 %finish.1 = f32[512,1024]{1,0:T(8,128)} custom-call(s32[1,512]{1,0:T(1,128)S(1)} %get-tuple-element.22.target_ref, bf16[1024,1024]{1,0:T(8,128)(2,1)} %bitcast.11.ret_ref, f32[8,1024]{1,0:T(8,128)S(1)} %get-tuple-element.35.diag_ref, bf16[3,1024,1024]{2,1,0:T(8,128)(2,1)} %get-tuple-element.36.held_ref, ...), custom_call_target="tpu_custom_call" | custom-call | flops 4294967296 | bytes 12582912 | tf_op jit(solution)/shard_map/finish/pallas_call | solution.py:399
  (16 shorter events, 0.6 us)
Async XLA Ops:
  3.6 19.9 %copy-start = (s32[3,1024]{1,0:T(4,128)S(1)}, s32[3,1024]{1,0:T(4,128)}, u32[]{:S(2)}) copy-start(s32[3,1024]{1,0:T(4,128)} %order_ref.3) | copy-start | bytes 36868
  3.6 40.4 %all-to-all-start = ((bf16[32,32,1024]{2,1,0:T(8,128)(2,1)}), bf16[32,32,1024]{2,1,0:T(8,128)(2,1)}, u32[]{:S(2)}, u32[]{:S(2)}) async-start(bf16[32,32,1024]{2,1,0:T(8,128)(2,1)} %bitcast.13), calls=%async_computation | async-start | bytes 4194304 | tf_op jit(solution)/shard_map/all_to_all | solution.py:444
  13.2 4.7 %collective-permute-start = (bf16[40,1024]{1,0:T(8,128)(2,1)S(1)}, bf16[40,1024]{1,0:T(8,128)(2,1)S(1)}, u32[]{:S(2)}, u32[]{:S(2)}) collective-permute-start(bf16[40,1024]{1,0:T(8,128)(2,1)S(1)} %label.1.z0_ref), channel_id=1, source_target_pairs={{0,32},{32,0},{64,96},{96,64},{128,160},{160,128},{192,224},{224,1... | collective-permute-start | bytes 245768 | tf_op jit(solution)/shard_map/ppermute | solution.py:422
  14.9 5.4 %collective-permute-start.1 = (bf16[40,1024]{1,0:T(8,128)(2,1)S(1)}, bf16[40,1024]{1,0:T(8,128)(2,1)S(1)}, u32[]{:S(2)}, u32[]{:S(2)}) collective-permute-start(bf16[40,1024]{1,0:T(8,128)(2,1)S(1)} %label.1.z0_ref), channel_id=1, source_target_pairs={{0,64},{32,96},{64,0},{96,32},{128,192},{160,224},{192,128},{224,1... | collective-permute-start | bytes 245768 | tf_op jit(solution)/shard_map/ppermute | solution.py:422
  17.9 5.5 %collective-permute-start.2 = (bf16[40,1024]{1,0:T(8,128)(2,1)S(1)}, bf16[40,1024]{1,0:T(8,128)(2,1)S(1)}, u32[]{:S(2)}, u32[]{:S(2)}) collective-permute-start(bf16[40,1024]{1,0:T(8,128)(2,1)S(1)} %label.1.z0_ref), channel_id=1, source_target_pairs={{0,96},{32,64},{64,32},{96,0},{128,224},{160,192},{192,160},{224,1... | collective-permute-start | bytes 245768 | tf_op jit(solution)/shard_map/ppermute | solution.py:422
  24.4 7.7 %collective-permute-start.3 = (bf16[40,1024]{1,0:T(8,128)(2,1)S(1)}, bf16[40,1024]{1,0:T(8,128)(2,1)S(1)}, u32[]{:S(2)}, u32[]{:S(2)}) collective-permute-start(bf16[40,1024]{1,0:T(8,128)(2,1)S(1)} %get-tuple-element.23), channel_id=1, source_target_pairs={{0,128},{32,160},{64,192},{96,224},{128,0},{160,32},{192,64},{224,... | collective-permute-start | bytes 245768 | tf_op jit(solution)/shard_map/ppermute | solution.py:422
  32.6 8.3 %collective-permute-start.4 = (bf16[104,1024]{1,0:T(8,128)(2,1)S(1)}, bf16[104,1024]{1,0:T(8,128)(2,1)S(1)}, u32[]{:S(2)}, u32[]{:S(2)}) collective-permute-start(bf16[104,1024]{1,0:T(8,128)(2,1)S(1)} %top_level.1), channel_id=1, source_target_pairs={{0,2},{1,9},{2,4},{3,11},{4,6},{5,13},{6,0},{7,15},{8,10},{9,17},{... | collective-permute-start | bytes 638984 | tf_op jit(solution)/shard_map/ppermute | solution.py:434
  33.6 7.3 %collective-permute-start.5 = (bf16[104,1024]{1,0:T(8,128)(2,1)S(1)}, bf16[104,1024]{1,0:T(8,128)(2,1)S(1)}, u32[]{:S(2)}, u32[]{:S(2)}) collective-permute-start(bf16[104,1024]{1,0:T(8,128)(2,1)S(1)} %top_level.1), channel_id=1, source_target_pairs={{0,6},{1,25},{2,0},{3,27},{4,2},{5,29},{6,4},{7,31},{8,14},{9,1},{... | collective-permute-start | bytes 638984 | tf_op jit(solution)/shard_map/ppermute | solution.py:434
  35.4 8.5 %collective-permute-start.6 = (bf16[104,1024]{1,0:T(8,128)(2,1)S(1)}, bf16[104,1024]{1,0:T(8,128)(2,1)S(1)}, u32[]{:S(2)}, u32[]{:S(2)}) collective-permute-start(bf16[104,1024]{1,0:T(8,128)(2,1)S(1)} %top_level.1), channel_id=1, source_target_pairs={{0,4},{1,17},{2,6},{3,19},{4,0},{5,21},{6,2},{7,23},{8,12},{9,25},... | collective-permute-start | bytes 638984 | tf_op jit(solution)/shard_map/ppermute | solution.py:434
  44.0 13.1 %collective-permute-start.7 = (bf16[4,104,1024]{2,1,0:T(8,128)(2,1)S(1)}, bf16[4,104,1024]{2,1,0:T(8,128)(2,1)S(1)}, u32[]{:S(2)}, u32[]{:S(2)}) collective-permute-start(bf16[4,104,1024]{2,1,0:T(8,128)(2,1)S(1)} %pad_maximum_fusion.refs_0_), channel_id=1, source_target_pairs={{0,8},{1,3},{2,10},{3,5},{4,12},{5,7},{6,14},{7,1},{8,16},{9,11},{... | collective-permute-start | bytes 2555912 | tf_op jit(solution)/shard_map/ppermute | solution.py:434
  44.5 12.5 %collective-permute-start.8 = (bf16[4,104,1024]{2,1,0:T(8,128)(2,1)S(1)}, bf16[4,104,1024]{2,1,0:T(8,128)(2,1)}, u32[]{:S(2)}, u32[]{:S(2)}) collective-permute-start(bf16[4,104,1024]{2,1,0:T(8,128)(2,1)S(1)} %pad_maximum_fusion.refs_0_), channel_id=1, source_target_pairs={{0,24},{1,7},{2,26},{3,1},{4,28},{5,3},{6,30},{7,5},{8,0},{9,15},{... | collective-permute-start | bytes 2555912 | tf_op jit(solution)/shard_map/ppermute | solution.py:434
  57.1 40.5 %all-to-all-start.1 = ((bf16[32,32,1024]{2,1,0:T(8,128)(2,1)}), bf16[32,32,1024]{2,1,0:T(8,128)(2,1)}, u32[]{:S(2)}, u32[]{:S(2)}) async-start(bf16[32,32,1024]{2,1,0:T(8,128)(2,1)} %bitcast.14), calls=%async_computation.1 | async-start | bytes 4194304 | tf_op jit(solution)/shard_map/all_to_all | solution.py:444
  66.7 4.7 %collective-permute-start.11 = (bf16[4,104,1024]{2,1,0:T(8,128)(2,1)S(1)}, bf16[4,104,1024]{2,1,0:T(8,128)(2,1)S(1)}, u32[]{:S(2)}, u32[]{:S(2)}) collective-permute-start(bf16[4,104,1024]{2,1,0:T(8,128)(2,1)S(1)} %pad_maximum_fusion.refs_0_), channel_id=1, source_target_pairs={{0,1},{1,0},{2,3},{3,2},{4,5},{5,4},{6,7},{7,6},{8,9},{9,8},{10,11... | collective-permute-start | bytes 2555912 | tf_op jit(solution)/shard_map/ppermute | solution.py:438
  67.1 4.5 %collective-permute-start.12 = (bf16[4,104,1024]{2,1,0:T(8,128)(2,1)S(1)}, bf16[4,104,1024]{2,1,0:T(8,128)(2,1)S(1)}, u32[]{:S(2)}, u32[]{:S(2)}) collective-permute-start(bf16[4,104,1024]{2,1,0:T(8,128)(2,1)S(1)} %collective-permute-done.7.refs_1_), channel_id=1, source_target_pairs={{0,1},{1,0},{2,3},{3,2},{4,5},{5,4},{6,7},{7,6},{8,9},{9,8},{10,11... | collective-permute-start | bytes 2555912 | tf_op jit(solution)/shard_map/ppermute | solution.py:438
  67.3 4.5 %collective-permute-start.13 = (bf16[4,104,1024]{2,1,0:T(8,128)(2,1)}, bf16[4,104,1024]{2,1,0:T(8,128)(2,1)S(1)}, u32[]{:S(2)}, u32[]{:S(2)}) collective-permute-start(bf16[4,104,1024]{2,1,0:T(8,128)(2,1)} %collective-permute-done.8.refs_2_), channel_id=1, source_target_pairs={{0,1},{1,0},{2,3},{3,2},{4,5},{5,4},{6,7},{7,6},{8,9},{9,8},{10,11... | collective-permute-start | bytes 2555912 | tf_op jit(solution)/shard_map/ppermute | solution.py:438
  68.7 28.4 %collective-permute-start.10 = (bf16[2,104,1024]{2,1,0:T(8,128)(2,1)S(1)}, bf16[2,104,1024]{2,1,0:T(8,128)(2,1)S(1)}, u32[]{:S(2)}, u32[]{:S(2)}) collective-permute-start(bf16[2,104,1024]{2,1,0:T(8,128)(2,1)S(1)} %slice.7), channel_id=1, source_target_pairs={{0,24},{1,7},{2,26},{3,1},{4,28},{5,3},{6,30},{7,5},{8,0},{9,15},{... | collective-permute-start | bytes 1277960 | tf_op jit(solution)/shard_map/ppermute | solution.py:434
  71.4 26.2 %collective-permute-start.9 = (bf16[2,104,1024]{2,1,0:T(8,128)(2,1)S(1)}, bf16[2,104,1024]{2,1,0:T(8,128)(2,1)S(1)}, u32[]{:S(2)}, u32[]{:S(2)}) collective-permute-start(bf16[2,104,1024]{2,1,0:T(8,128)(2,1)S(1)} %slice.6), channel_id=1, source_target_pairs={{0,8},{1,3},{2,10},{3,5},{4,12},{5,7},{6,14},{7,1},{8,16},{9,11},{... | collective-permute-start | bytes 1277960 | tf_op jit(solution)/shard_map/ppermute | solution.py:434
  97.6 1.8 %collective-permute-start.14 = (bf16[2,104,1024]{2,1,0:T(8,128)(2,1)S(1)}, bf16[2,104,1024]{2,1,0:T(8,128)(2,1)S(1)}, u32[]{:S(2)}, u32[]{:S(2)}) collective-permute-start(bf16[2,104,1024]{2,1,0:T(8,128)(2,1)S(1)} %collective-permute-done.9.refs_0_), channel_id=1, source_target_pairs={{0,1},{1,0},{2,3},{3,2},{4,5},{5,4},{6,7},{7,6},{8,9},{9,8},{10,11... | collective-permute-start | bytes 1277960 | tf_op jit(solution)/shard_map/ppermute | solution.py:438
  98.1 2.0 %collective-permute-start.15 = (bf16[2,104,1024]{2,1,0:T(8,128)(2,1)S(1)}, bf16[2,104,1024]{2,1,0:T(8,128)(2,1)S(1)}, u32[]{:S(2)}, u32[]{:S(2)}) collective-permute-start(bf16[2,104,1024]{2,1,0:T(8,128)(2,1)S(1)} %collective-permute-done.10.refs_1_), channel_id=1, source_target_pairs={{0,1},{1,0},{2,3},{3,2},{4,5},{5,4},{6,7},{7,6},{8,9},{9,8},{10,11... | collective-permute-start | bytes 1277960 | tf_op jit(solution)/shard_map/ppermute | solution.py:438

commit v6 on v3

--- a/solution.py
+++ b/solution.py
@@ -288,7 +288,7 @@
 
 
 def fold_kernel(*refs):
-    parts, (f_ref, diag_ref, held, marks) = refs[: 2 * len(LINES)], refs[2 * len(LINES) :]
+    parts, (f_ref, diag_ref, held, marks, mid, made, sems) = refs[: 2 * len(LINES)], refs[2 * len(LINES) :]
     own = lax.axis_index("owner")
     core, x, y = own & 1, (own >> 1) & 3, own >> 3
     slot = 0
@@ -315,18 +315,30 @@
     for t in range(0, PORTS, tile):
         acc = jnp.dot(held[1], held[0, :, t : t + tile], preferred_element_type=F32)
         on = iota((PORTS, tile), 0) == iota((PORTS, tile), 1) + t
-        mid = (jnp.where(on, ratio[:, t : t + tile], 0.0) - acc).astype(BF16)
-        f_ref[t : t + tile, :] = jnp.transpose(jnp.dot(held[2], mid, preferred_element_type=F32)).astype(BF16)
+        mid[:, t : t + tile] = (jnp.where(on, ratio[:, t : t + tile], 0.0) - acc).astype(BF16)
+    stores = []
+    for k, t in enumerate(range(0, PORTS, tile)):
+        at = slice(t, t + tile)
+        made[at, :] = jnp.dot(held[2, at, :], mid[...], preferred_element_type=F32).astype(BF16)
+        store = pltpu.make_async_copy(made.at[at], f_ref.at[at], sems.at[k])
+        store.start()
+        stores.append(store)
+    for store in stores:
+        store.wait()
 
 
 def fold(parts):
     return pl.pallas_call(
         fold_kernel,
         in_specs=[IN_VMEM] * (2 * len(LINES)),
+        out_specs=[ANYWHERE, IN_VMEM],
         out_shape=[pltpu.HBM((PORTS, PORTS), BF16), pltpu.VMEM((DROWS, PORTS), F32)],
         scratch_shapes=[
             pltpu.VMEM((3, PORTS, PORTS), BF16),
             pltpu.VMEM((32, DROWS, PORTS), BF16),
+            pltpu.VMEM((PORTS, PORTS), BF16),
+            pltpu.VMEM((PORTS, PORTS), BF16),
+            pltpu.SemaphoreType.DMA((4,)),
         ],
         compiler_params=params(24),
         cost_estimate=cost(4 * PORTS**3, 9 << 20),
@@ -349,12 +361,14 @@
         scaled[:, at] = (piece * diag_ref[0:1, at]).astype(BF16)
     load.wait()
     stores = []
-    tile = 128
-    for k, r in enumerate(range(0, ROWS, tile)):
-        at = slice(r, r + tile)
-        coupled = jnp.dot(scaled[at, :], coupling[...], preferred_element_type=F32)
-        made[at, :] = response[at, :] * diag_ref[1:2, :] - coupled
-        store = pltpu.make_async_copy(made.at[at], out_ref.at[at], out_sems.at[k])
+    tile = 256
+    for k, n in enumerate(range(0, PORTS, tile)):
+        at = slice(n, n + tile)
+        coupled = lax.dot_general(
+            scaled[...], coupling[at, :], (((1,), (1,)), ((), ())), preferred_element_type=F32
+        )
+        made[:, at] = response[:, at] * diag_ref[1:2, at] - coupled
+        store = pltpu.make_async_copy(made.at[:, at], out_ref.at[:, at], out_sems.at[k])
         store.start()
         stores.append(store)
     for store in stores:

time: 109 us -> 108 us (level)
  Pallas kernels: 25.4 us -> 24.3 us
    pallas_call x1, Pallas kernels: 8.71 us -> 7.17 us  [fold(): pl.pallas_call(fold_kernel, in_specs=[IN_VMEM] * (2 * len(LINES)), out_sp...]
  transfers between devices with their start and end apart: 18 -> 18, of which waited for: 10 -> 10; matrix products, arithmetic and copies ran while one was open for 2% -> 2% of each run, Pallas kernels for 17% -> 16%
where the time goes in v6:
time: 108 us; the launch traced here: 106 us
  waiting for transfers between devices  40.7 us (38%)
  starting transfers between devices  39 us (36%)
  Pallas kernels  24.3 us (22%)
  local copies, waits for them, and re-layouts  2.08 us (2%)
    ppermute x7, waiting for transfers between devices, chip_shift(): return lax.ppermute(value, 'owner', pairs)  30.8 us
    all_to_all x2, starting transfers between devices, exchange(): lax.all_to_all(value, 'owner', split_axis=0, concat_axis=0, tiled=True)  16.9 us
    ppermute x4, starting transfers between devices, group_swap(): return lax.ppermute(value, 'group', [(i, i ^ mask) for i in range(8)])  10.7 us
    ppermute x7, starting transfers between devices, chip_shift(): return lax.ppermute(value, 'owner', pairs)  9.68 us
    ppermute x4, waiting for transfers between devices, group_swap(): return lax.ppermute(value, 'group', [(i, i ^ mask) for i in range(8)])  8.49 us
    pallas_call x1, Pallas kernels, fold(): pl.pallas_call(fold_kernel, in_specs=[IN_VMEM] * (2 * len(LINES)), out_sp...  7.17 us
    pallas_call x1, Pallas kernels, apply_maps(): pl.pallas_call(maps_kernel, in_specs=[IN_VMEM, ANYWHERE], out_specs=ANYWH...  7.05 us
    pallas_call x1, Pallas kernels, finish(): pl.pallas_call(finish_kernel, in_specs=[IN_VMEM, IN_VMEM, ANYWHERE, IN_VM...  4.08 us
  transfers between devices with their start and end apart: 18, of which 10 were waited for; matrix products, arithmetic and copies ran while one was open for 2% of the time, Pallas kernels for 16%

profile of v6, /device:TPU:1, one launch (start us, length us, event | category | flops | bytes accessed | tf_op | source)
XLA Modules:
  0.0 106.4 jit_solution(13970612992093295515)
XLA Ops:
  0.0 3.6 %prep.1 = (bf16[1024,1024]{1,0:T(8,128)(2,1)}, s32[1,512]{1,0:T(1,128)S(1)}) custom-call(s32[1,512]{1,0:T(1,128)} %bitcast.21, s32[1,512]{1,0:T(1,128)} %bitcast.22, s32[1,512]{1,0:T(1,128)} %bitcast.23, bf16[512,1024]{1,0:T(8,128)(2,1)} %rows_ref.1), custom_call_target="tpu_custom_call" | custom-call | flops 1073741824 | bytes 4194304 | tf_op jit(solution)/shard_map/prep/pallas_call | solution.py:137
  3.6 8.6 %all-to-all-start = ((bf16[32,32,1024]{2,1,0:T(8,128)(2,1)}), bf16[32,32,1024]{2,1,0:T(8,128)(2,1)S(1)}, u32[]{:S(2)}, u32[]{:S(2)}) async-start(bf16[32,32,1024]{2,1,0:T(8,128)(2,1)} %bitcast.15), calls=%async_computation | async-start | bytes 4194304 | tf_op jit(solution)/shard_map/all_to_all | solution.py:422
  12.2 1.0 label.1.z0_ref
  13.1 4.4 %collective-permute-start.2 = (bf16[40,1024]{1,0:T(8,128)(2,1)S(1)}, bf16[40,1024]{1,0:T(8,128)(2,1)S(1)}, u32[]{:S(2)}, u32[]{:S(2)}) collective-permute-start(bf16[40,1024]{1,0:T(8,128)(2,1)S(1)} %label.1.z0_ref), channel_id=1, source_target_pairs={{0,96},{32,64},{64,32},{96,0},{128,224},{160,192},{192,160},{224,1... | collective-permute-start | bytes 245768 | tf_op jit(solution)/shard_map/ppermute | solution.py:400
  17.6 0.4 collective-permute-start
  18.0 2.3 %collective-permute-done.2.z3_ref = bf16[40,1024]{1,0:T(8,128)(2,1)S(1)} collective-permute-done((bf16[40,1024]{1,0:T(8,128)(2,1)S(1)}, bf16[40,1024]{1,0:T(8,128)(2,1)S(1)}, u32[]{:S(2)}, u32[]{:S(2)}) %collective-permute-start.2) | collective-permute-done | bytes 81952 | tf_op jit(solution)/shard_map/ppermute | solution.py:400
  20.3 4.0 %collective-permute-done.1.z2_ref = bf16[40,1024]{1,0:T(8,128)(2,1)S(1)} collective-permute-done((bf16[40,1024]{1,0:T(8,128)(2,1)S(1)}, bf16[40,1024]{1,0:T(8,128)(2,1)S(1)}, u32[]{:S(2)}, u32[]{:S(2)}) %collective-permute-start.1) | collective-permute-done | bytes 81952 | tf_op jit(solution)/shard_map/ppermute | solution.py:400
  24.2 1.0 low_levels.1
  25.2 5.9 %collective-permute-start.3 = (bf16[40,1024]{1,0:T(8,128)(2,1)S(1)}, bf16[40,1024]{1,0:T(8,128)(2,1)S(1)}, u32[]{:S(2)}, u32[]{:S(2)}) collective-permute-start(bf16[40,1024]{1,0:T(8,128)(2,1)S(1)} %get-tuple-element.15), channel_id=1, source_target_pairs={{0,128},{32,160},{64,192},{96,224},{128,0},{160,32},{192,64},{224,... | collective-permute-start | bytes 245768 | tf_op jit(solution)/shard_map/ppermute | solution.py:400
  31.1 2.2 %collective-permute-done.3.z4_ref = bf16[40,1024]{1,0:T(8,128)(2,1)S(1)} collective-permute-done((bf16[40,1024]{1,0:T(8,128)(2,1)S(1)}, bf16[40,1024]{1,0:T(8,128)(2,1)S(1)}, u32[]{:S(2)}, u32[]{:S(2)}) %collective-permute-start.3) | collective-permute-done | bytes 81952 | tf_op jit(solution)/shard_map/ppermute | solution.py:400
  33.3 0.5 top_level.1
  33.8 2.9 %collective-permute-start.6 = (bf16[104,1024]{1,0:T(8,128)(2,1)S(1)}, bf16[104,1024]{1,0:T(8,128)(2,1)S(1)}, u32[]{:S(2)}, u32[]{:S(2)}) collective-permute-start(bf16[104,1024]{1,0:T(8,128)(2,1)S(1)} %top_level.1), channel_id=1, source_target_pairs={{0,4},{1,17},{2,6},{3,19},{4,0},{5,21},{6,2},{7,23},{8,12},{9,25},... | collective-permute-start | bytes 638984 | tf_op jit(solution)/shard_map/ppermute | solution.py:412
  36.8 0.9 collective-permute-start.5
  37.6 0.6 collective-permute-start.4
  38.2 3.6 %collective-permute-done.6 = bf16[104,1024]{1,0:T(8,128)(2,1)S(1)} collective-permute-done((bf16[104,1024]{1,0:T(8,128)(2,1)S(1)}, bf16[104,1024]{1,0:T(8,128)(2,1)S(1)}, u32[]{:S(2)}, u32[]{:S(2)}) %collective-permute-start.6) | collective-permute-done | bytes 213024 | tf_op jit(solution)/shard_map/ppermute | solution.py:412
  41.8 1.8 %collective-permute-done.5 = bf16[104,1024]{1,0:T(8,128)(2,1)S(1)} collective-permute-done((bf16[104,1024]{1,0:T(8,128)(2,1)S(1)}, bf16[104,1024]{1,0:T(8,128)(2,1)S(1)}, u32[]{:S(2)}, u32[]{:S(2)}) %collective-permute-start.5) | collective-permute-done | bytes 213024 | tf_op jit(solution)/shard_map/ppermute | solution.py:412
  43.6 0.6 collective-permute-done.4
  44.3 2.4 %collective-permute-start.8 = (bf16[4,104,1024]{2,1,0:T(8,128)(2,1)S(1)}, bf16[4,104,1024]{2,1,0:T(8,128)(2,1)}, u32[]{:S(2)}, u32[]{:S(2)}) collective-permute-start(bf16[4,104,1024]{2,1,0:T(8,128)(2,1)S(1)} %pad_maximum_fusion.refs_0_), channel_id=1, source_target_pairs={{0,24},{1,7},{2,26},{3,1},{4,28},{5,3},{6,30},{7,5},{8,0},{9,15},{... | collective-permute-start | bytes 2555912 | tf_op jit(solution)/shard_map/ppermute | solution.py:412
  46.7 7.1 %apply_maps.1 = bf16[1024,1024]{1,0:T(8,128)(2,1)} custom-call(bf16[1024,1024]{1,0:T(8,128)(2,1)S(1)} %bitcast.12, bf16[2,1024,1024]{2,1,0:T(8,128)(2,1)} %maps_ref.1), custom_call_target="tpu_custom_call" | custom-call | flops 4294967296 | bytes 8388608 | tf_op jit(solution)/shard_map/apply_maps/pallas_call | solution.py:196
  53.8 8.3 %all-to-all-start.1 = ((bf16[32,32,1024]{2,1,0:T(8,128)(2,1)}), bf16[32,32,1024]{2,1,0:T(8,128)(2,1)S(1)}, u32[]{:S(2)}, u32[]{:S(2)}) async-start(bf16[32,32,1024]{2,1,0:T(8,128)(2,1)} %bitcast.16), calls=%async_computation.1 | async-start | bytes 4194304 | tf_op jit(solution)/shard_map/all_to_all | solution.py:422
  62.1 0.3 collective-permute-start.11
  62.4 1.0 slice.9
  63.5 2.8 %collective-permute-start.10 = (bf16[2,104,1024]{2,1,0:T(8,128)(2,1)S(1)}, bf16[2,104,1024]{2,1,0:T(8,128)(2,1)S(1)}, u32[]{:S(2)}, u32[]{:S(2)}) collective-permute-start(bf16[2,104,1024]{2,1,0:T(8,128)(2,1)S(1)} %slice.9), channel_id=1, source_target_pairs={{0,24},{1,7},{2,26},{3,1},{4,28},{5,3},{6,30},{7,5},{8,0},{9,15},{... | collective-permute-start | bytes 1277960 | tf_op jit(solution)/shard_map/ppermute | solution.py:412
  66.3 1.0 slice.8
  67.4 0.6 collective-permute-start.13
  68.1 24.1 %collective-permute-done.10.refs_4_ = bf16[2,104,1024]{2,1,0:T(8,128)(2,1)S(1)} collective-permute-done((bf16[2,104,1024]{2,1,0:T(8,128)(2,1)S(1)}, bf16[2,104,1024]{2,1,0:T(8,128)(2,1)S(1)}, u32[]{:S(2)}, u32[]{:S(2)}) %collective-permute-start.10) | collective-permute-done | bytes 426016 | tf_op jit(solution)/shard_map/ppermute | solution.py:412
  92.4 0.7 collective-permute-done.9.refs_3_
  93.1 0.4 collective-permute-start.14
  93.5 0.4 collective-permute-done.15.refs_9_
  93.9 1.0 collective-permute-done.14.refs_8_
  94.9 7.2 %fold.1 = (bf16[1024,1024]{1,0:T(8,128)(2,1)}, f32[8,1024]{1,0:T(8,128)S(1)}) custom-call(bf16[4,104,1024]{2,1,0:T(8,128)(2,1)S(1)} %pad_maximum_fusion.refs_0_, bf16[4,104,1024]{2,1,0:T(8,128)(2,1)} %collective-permute-done.7.refs_1_, bf16[4,104,1024]{2,1,0:T(8,128)(2,1)} %collective-permute-done.8.refs_2_, ...), custom_call_target="tpu_custom_call" | custom-call | flops 4294967296 | bytes 9437184 | tf_op jit(solution)/shard_map/fold/pallas_call | solution.py:331
  102.1 4.1 %finish.1 = f32[512,1024]{1,0:T(8,128)} custom-call(s32[1,512]{1,0:T(1,128)S(1)} %get-tuple-element.13.target_ref, bf16[1024,1024]{1,0:T(8,128)(2,1)S(1)} %bitcast.13, bf16[1024,1024]{1,0:T(8,128)(2,1)} %get-tuple-element.19.f_ref, f32[8,1024]{1,0:T(8,128)S(1)} %get-tuple-element.20.diag_ref), custom_call_target="tpu_custom_call" | custom-call | flops 2147483648 | bytes 6291456 | tf_op jit(solution)/shard_map/finish/pallas_call | solution.py:379
  (16 shorter events, 0.6 us)
Async XLA Ops:
  3.6 20.7 %copy-start = (s32[3,1024]{1,0:T(4,128)S(1)}, s32[3,1024]{1,0:T(4,128)}, u32[]{:S(2)}) copy-start(s32[3,1024]{1,0:T(4,128)} %order_ref.3) | copy-start | bytes 36868
  3.6 43.2 %all-to-all-start = ((bf16[32,32,1024]{2,1,0:T(8,128)(2,1)}), bf16[32,32,1024]{2,1,0:T(8,128)(2,1)S(1)}, u32[]{:S(2)}, u32[]{:S(2)}) async-start(bf16[32,32,1024]{2,1,0:T(8,128)(2,1)} %bitcast.15), calls=%async_computation | async-start | bytes 4194304 | tf_op jit(solution)/shard_map/all_to_all | solution.py:422
  13.1 7.1 %collective-permute-start.2 = (bf16[40,1024]{1,0:T(8,128)(2,1)S(1)}, bf16[40,1024]{1,0:T(8,128)(2,1)S(1)}, u32[]{:S(2)}, u32[]{:S(2)}) collective-permute-start(bf16[40,1024]{1,0:T(8,128)(2,1)S(1)} %label.1.z0_ref), channel_id=1, source_target_pairs={{0,96},{32,64},{64,32},{96,0},{128,224},{160,192},{192,160},{224,1... | collective-permute-start | bytes 245768 | tf_op jit(solution)/shard_map/ppermute | solution.py:400
  17.6 6.7 %collective-permute-start.1 = (bf16[40,1024]{1,0:T(8,128)(2,1)S(1)}, bf16[40,1024]{1,0:T(8,128)(2,1)S(1)}, u32[]{:S(2)}, u32[]{:S(2)}) collective-permute-start(bf16[40,1024]{1,0:T(8,128)(2,1)S(1)} %label.1.z0_ref), channel_id=1, source_target_pairs={{0,64},{32,96},{64,0},{96,32},{128,192},{160,224},{192,128},{224,1... | collective-permute-start | bytes 245768 | tf_op jit(solution)/shard_map/ppermute | solution.py:400
  17.6 6.7 %collective-permute-start = (bf16[40,1024]{1,0:T(8,128)(2,1)S(1)}, bf16[40,1024]{1,0:T(8,128)(2,1)S(1)}, u32[]{:S(2)}, u32[]{:S(2)}) collective-permute-start(bf16[40,1024]{1,0:T(8,128)(2,1)S(1)} %label.1.z0_ref), channel_id=1, source_target_pairs={{0,32},{32,0},{64,96},{96,64},{128,160},{160,128},{192,224},{224,1... | collective-permute-start | bytes 245768 | tf_op jit(solution)/shard_map/ppermute | solution.py:400
  25.2 8.1 %collective-permute-start.3 = (bf16[40,1024]{1,0:T(8,128)(2,1)S(1)}, bf16[40,1024]{1,0:T(8,128)(2,1)S(1)}, u32[]{:S(2)}, u32[]{:S(2)}) collective-permute-start(bf16[40,1024]{1,0:T(8,128)(2,1)S(1)} %get-tuple-element.15), channel_id=1, source_target_pairs={{0,128},{32,160},{64,192},{96,224},{128,0},{160,32},{192,64},{224,... | collective-permute-start | bytes 245768 | tf_op jit(solution)/shard_map/ppermute | solution.py:400
  33.8 8.0 %collective-permute-start.6 = (bf16[104,1024]{1,0:T(8,128)(2,1)S(1)}, bf16[104,1024]{1,0:T(8,128)(2,1)S(1)}, u32[]{:S(2)}, u32[]{:S(2)}) collective-permute-start(bf16[104,1024]{1,0:T(8,128)(2,1)S(1)} %top_level.1), channel_id=1, source_target_pairs={{0,4},{1,17},{2,6},{3,19},{4,0},{5,21},{6,2},{7,23},{8,12},{9,25},... | collective-permute-start | bytes 638984 | tf_op jit(solution)/shard_map/ppermute | solution.py:412
  36.8 6.8 %collective-permute-start.5 = (bf16[104,1024]{1,0:T(8,128)(2,1)S(1)}, bf16[104,1024]{1,0:T(8,128)(2,1)S(1)}, u32[]{:S(2)}, u32[]{:S(2)}) collective-permute-start(bf16[104,1024]{1,0:T(8,128)(2,1)S(1)} %top_level.1), channel_id=1, source_target_pairs={{0,6},{1,25},{2,0},{3,27},{4,2},{5,29},{6,4},{7,31},{8,14},{9,1},{... | collective-permute-start | bytes 638984 | tf_op jit(solution)/shard_map/ppermute | solution.py:412
  37.6 6.6 %collective-permute-start.4 = (bf16[104,1024]{1,0:T(8,128)(2,1)S(1)}, bf16[104,1024]{1,0:T(8,128)(2,1)S(1)}, u32[]{:S(2)}, u32[]{:S(2)}) collective-permute-start(bf16[104,1024]{1,0:T(8,128)(2,1)S(1)} %top_level.1), channel_id=1, source_target_pairs={{0,2},{1,9},{2,4},{3,11},{4,6},{5,13},{6,0},{7,15},{8,10},{9,17},{... | collective-permute-start | bytes 638984 | tf_op jit(solution)/shard_map/ppermute | solution.py:412
  44.3 18.1 %collective-permute-start.8 = (bf16[4,104,1024]{2,1,0:T(8,128)(2,1)S(1)}, bf16[4,104,1024]{2,1,0:T(8,128)(2,1)}, u32[]{:S(2)}, u32[]{:S(2)}) collective-permute-start(bf16[4,104,1024]{2,1,0:T(8,128)(2,1)S(1)} %pad_maximum_fusion.refs_0_), channel_id=1, source_target_pairs={{0,24},{1,7},{2,26},{3,1},{4,28},{5,3},{6,30},{7,5},{8,0},{9,15},{... | collective-permute-start | bytes 2555912 | tf_op jit(solution)/shard_map/ppermute | solution.py:412
  46.7 19.6 %collective-permute-start.7 = (bf16[4,104,1024]{2,1,0:T(8,128)(2,1)S(1)}, bf16[4,104,1024]{2,1,0:T(8,128)(2,1)}, u32[]{:S(2)}, u32[]{:S(2)}) collective-permute-start(bf16[4,104,1024]{2,1,0:T(8,128)(2,1)S(1)} %pad_maximum_fusion.refs_0_), channel_id=1, source_target_pairs={{0,8},{1,3},{2,10},{3,5},{4,12},{5,7},{6,14},{7,1},{8,16},{9,11},{... | collective-permute-start | bytes 2555912 | tf_op jit(solution)/shard_map/ppermute | solution.py:412
  53.8 48.3 %all-to-all-start.1 = ((bf16[32,32,1024]{2,1,0:T(8,128)(2,1)}), bf16[32,32,1024]{2,1,0:T(8,128)(2,1)S(1)}, u32[]{:S(2)}, u32[]{:S(2)}) async-start(bf16[32,32,1024]{2,1,0:T(8,128)(2,1)} %bitcast.16), calls=%async_computation.1 | async-start | bytes 4194304 | tf_op jit(solution)/shard_map/all_to_all | solution.py:422
  62.1 31.4 %collective-permute-start.11 = (bf16[4,104,1024]{2,1,0:T(8,128)(2,1)S(1)}, bf16[4,104,1024]{2,1,0:T(8,128)(2,1)S(1)}, u32[]{:S(2)}, u32[]{:S(2)}) collective-permute-start(bf16[4,104,1024]{2,1,0:T(8,128)(2,1)S(1)} %pad_maximum_fusion.refs_0_), channel_id=1, source_target_pairs={{0,1},{1,0},{2,3},{3,2},{4,5},{5,4},{6,7},{7,6},{8,9},{9,8},{10,11... | collective-permute-start | bytes 2555912 | tf_op jit(solution)/shard_map/ppermute | solution.py:416
  63.5 28.7 %collective-permute-start.10 = (bf16[2,104,1024]{2,1,0:T(8,128)(2,1)S(1)}, bf16[2,104,1024]{2,1,0:T(8,128)(2,1)S(1)}, u32[]{:S(2)}, u32[]{:S(2)}) collective-permute-start(bf16[2,104,1024]{2,1,0:T(8,128)(2,1)S(1)} %slice.9), channel_id=1, source_target_pairs={{0,24},{1,7},{2,26},{3,1},{4,28},{5,3},{6,30},{7,5},{8,0},{9,15},{... | collective-permute-start | bytes 1277960 | tf_op jit(solution)/shard_map/ppermute | solution.py:412
  67.3 25.8 %collective-permute-start.9 = (bf16[2,104,1024]{2,1,0:T(8,128)(2,1)S(1)}, bf16[2,104,1024]{2,1,0:T(8,128)(2,1)S(1)}, u32[]{:S(2)}, u32[]{:S(2)}) collective-permute-start(bf16[2,104,1024]{2,1,0:T(8,128)(2,1)S(1)} %slice.8), channel_id=1, source_target_pairs={{0,8},{1,3},{2,10},{3,5},{4,12},{5,7},{6,14},{7,1},{8,16},{9,11},{... | collective-permute-start | bytes 1277960 | tf_op jit(solution)/shard_map/ppermute | solution.py:412
  67.4 26.5 %collective-permute-start.13 = (bf16[4,104,1024]{2,1,0:T(8,128)(2,1)}, bf16[4,104,1024]{2,1,0:T(8,128)(2,1)S(1)}, u32[]{:S(2)}, u32[]{:S(2)}) collective-permute-start(bf16[4,104,1024]{2,1,0:T(8,128)(2,1)} %collective-permute-done.8.refs_2_), channel_id=1, source_target_pairs={{0,1},{1,0},{2,3},{3,2},{4,5},{5,4},{6,7},{7,6},{8,9},{9,8},{10,11... | collective-permute-start | bytes 2555912 | tf_op jit(solution)/shard_map/ppermute | solution.py:416
  68.0 27.0 %collective-permute-start.12 = (bf16[4,104,1024]{2,1,0:T(8,128)(2,1)}, bf16[4,104,1024]{2,1,0:T(8,128)(2,1)S(1)}, u32[]{:S(2)}, u32[]{:S(2)}) collective-permute-start(bf16[4,104,1024]{2,1,0:T(8,128)(2,1)} %collective-permute-done.7.refs_1_), channel_id=1, source_target_pairs={{0,1},{1,0},{2,3},{3,2},{4,5},{5,4},{6,7},{7,6},{8,9},{9,8},{10,11... | collective-permute-start | bytes 2555912 | tf_op jit(solution)/shard_map/ppermute | solution.py:416
  92.2 1.8 %collective-permute-start.15 = (bf16[2,104,1024]{2,1,0:T(8,128)(2,1)S(1)}, bf16[2,104,1024]{2,1,0:T(8,128)(2,1)S(1)}, u32[]{:S(2)}, u32[]{:S(2)}) collective-permute-start(bf16[2,104,1024]{2,1,0:T(8,128)(2,1)S(1)} %collective-permute-done.10.refs_4_), channel_id=1, source_target_pairs={{0,1},{1,0},{2,3},{3,2},{4,5},{5,4},{6,7},{7,6},{8,9},{9,8},{10,11... | collective-permute-start | bytes 1277960 | tf_op jit(solution)/shard_map/ppermute | solution.py:416
  93.1 1.8 %collective-permute-start.14 = (bf16[2,104,1024]{2,1,0:T(8,128)(2,1)S(1)}, bf16[2,104,1024]{2,1,0:T(8,128)(2,1)S(1)}, u32[]{:S(2)}, u32[]{:S(2)}) collective-permute-start(bf16[2,104,1024]{2,1,0:T(8,128)(2,1)S(1)} %collective-permute-done.9.refs_3_), channel_id=1, source_target_pairs={{0,1},{1,0},{2,3},{3,2},{4,5},{5,4},{6,7},{7,6},{8,9},{9,8},{10,11... | collective-permute-start | bytes 1277960 | tf_op jit(solution)/shard_map/ppermute | solution.py:416

commit v7 on v6

--- a/solution.py
+++ b/solution.py
@@ -207,7 +207,7 @@
             pltpu.SemaphoreType.DMA((2, 4)),
             pltpu.SemaphoreType.DMA((4,)),
         ],
-        compiler_params=params(28),
+        compiler_params=params(60),
         cost_estimate=cost(4 * SLOTS * PORTS * PORTS, 8 << 20),
         name="apply_maps",
     )(vmem(x), hbm(maps))
@@ -341,7 +341,7 @@
             pltpu.SemaphoreType.DMA((4,)),
         ],
         compiler_params=params(24),
-        cost_estimate=cost(4 * PORTS**3, 9 << 20),
+        cost_estimate=cost(14 * PORTS**3, 9 << 20),
         name="fold",
     )(*[vmem(part) for part in parts])
 
@@ -433,11 +433,12 @@
     pack = top_level(group_swap(z, 4), off, diag, gb, pivot_order)
     line = jnp.stack([pack] + [chip_shift(pack, step, 0) for step in STEPS])
     left, right = chip_shift(line, 1, 1), chip_shift(line, -1, 1)
+    answers = apply_maps(arrived, subcircuit_maps)
+    answers, left, right = lax.optimization_barrier((answers, left, right))
     far_low, far_high = chip_shift(left[:2], 1, 1), chip_shift(right[2:], -1, 1)
     parts = [line, left, right, far_low, far_high]
     parts = parts + [core_swap(part) for part in parts]
     f, inverses = fold(parts)
-    answers = apply_maps(arrived, subcircuit_maps)
     returned = exchange(answers)
     return finish(target, returned, f, inverses)
 

time: 108 us -> 108 us (level)
  the two profiles are of different devices: /device:TPU:1 before, /device:TPU:32 now
where the time goes in v7:
time: 108 us; the launch traced here: 107 us
  waiting for transfers between devices  46.5 us (43%)
  starting transfers between devices  31.6 us (29%)
  Pallas kernels  25.2 us (23%)
  local copies, waits for them, and re-layouts  3.58 us (3%)
    all_to_all x2, waiting for transfers between devices, exchange(): lax.all_to_all(value, 'owner', split_axis=0, concat_axis=0, tiled=True)  16.8 us
    ppermute x7, waiting for transfers between devices, chip_shift(): return lax.ppermute(value, 'owner', pairs)  16 us
    ppermute x4, waiting for transfers between devices, group_swap(): return lax.ppermute(value, 'group', [(i, i ^ mask) for i in range(8)])  11.8 us
    all_to_all x2, starting transfers between devices, exchange(): lax.all_to_all(value, 'owner', split_axis=0, concat_axis=0, tiled=True)  11.3 us
    ppermute x7, starting transfers between devices, chip_shift(): return lax.ppermute(value, 'owner', pairs)  10.1 us
    ppermute x4, starting transfers between devices, group_swap(): return lax.ppermute(value, 'group', [(i, i ^ mask) for i in range(8)])  9.4 us
    pallas_call x1, Pallas kernels, fold(): pl.pallas_call(fold_kernel, in_specs=[IN_VMEM] * (2 * len(LINES)), out_sp...  8.07 us
    pallas_call x1, Pallas kernels, apply_maps(): pl.pallas_call(maps_kernel, in_specs=[IN_VMEM, ANYWHERE], out_specs=ANYWH...  7.06 us
  transfers between devices with their start and end apart: 18, of which 12 were waited for; matrix products, arithmetic and copies ran while one was open for 3% of the time, Pallas kernels for 16%

profile of v7, /device:TPU:32, one launch (start us, length us, event | category | flops | bytes accessed | tf_op | source)
XLA Modules:
  0.0 107.3 jit_solution(9648266434708260336)
XLA Ops:
  0.0 3.6 %prep.1 = (bf16[1024,1024]{1,0:T(8,128)(2,1)}, s32[1,512]{1,0:T(1,128)S(1)}) custom-call(s32[1,512]{1,0:T(1,128)} %bitcast.21, s32[1,512]{1,0:T(1,128)} %bitcast.22, s32[1,512]{1,0:T(1,128)} %bitcast.23, bf16[512,1024]{1,0:T(8,128)(2,1)} %rows_ref.1), custom_call_target="tpu_custom_call" | custom-call | flops 1073741824 | bytes 4194304 | tf_op jit(solution)/shard_map/prep/pallas_call | solution.py:137
  3.6 7.3 %all-to-all-start = ((bf16[32,32,1024]{2,1,0:T(8,128)(2,1)}), bf16[32,32,1024]{2,1,0:T(8,128)(2,1)S(1)}, u32[]{:S(2)}, u32[]{:S(2)}) async-start(bf16[32,32,1024]{2,1,0:T(8,128)(2,1)} %bitcast.15), calls=%async_computation | async-start | bytes 4194304 | tf_op jit(solution)/shard_map/all_to_all | solution.py:422
  10.9 1.0 label.1.z0_ref
  11.9 2.0 %collective-permute-start.2 = (bf16[40,1024]{1,0:T(8,128)(2,1)S(1)}, bf16[40,1024]{1,0:T(8,128)(2,1)S(1)}, u32[]{:S(2)}, u32[]{:S(2)}) collective-permute-start(bf16[40,1024]{1,0:T(8,128)(2,1)S(1)} %label.1.z0_ref), channel_id=1, source_target_pairs={{0,96},{32,64},{64,32},{96,0},{128,224},{160,192},{192,160},{224,1... | collective-permute-start | bytes 245768 | tf_op jit(solution)/shard_map/ppermute | solution.py:400
  13.9 1.5 %collective-permute-start.1 = (bf16[40,1024]{1,0:T(8,128)(2,1)S(1)}, bf16[40,1024]{1,0:T(8,128)(2,1)S(1)}, u32[]{:S(2)}, u32[]{:S(2)}) collective-permute-start(bf16[40,1024]{1,0:T(8,128)(2,1)S(1)} %label.1.z0_ref), channel_id=1, source_target_pairs={{0,64},{32,96},{64,0},{96,32},{128,192},{160,224},{192,128},{224,1... | collective-permute-start | bytes 245768 | tf_op jit(solution)/shard_map/ppermute | solution.py:400
  15.3 1.4 %collective-permute-start = (bf16[40,1024]{1,0:T(8,128)(2,1)S(1)}, bf16[40,1024]{1,0:T(8,128)(2,1)S(1)}, u32[]{:S(2)}, u32[]{:S(2)}) collective-permute-start(bf16[40,1024]{1,0:T(8,128)(2,1)S(1)} %label.1.z0_ref), channel_id=1, source_target_pairs={{0,32},{32,0},{64,96},{96,64},{128,160},{160,128},{192,224},{224,1... | collective-permute-start | bytes 245768 | tf_op jit(solution)/shard_map/ppermute | solution.py:400
  16.7 3.8 %collective-permute-done.2.z3_ref = bf16[40,1024]{1,0:T(8,128)(2,1)S(1)} collective-permute-done((bf16[40,1024]{1,0:T(8,128)(2,1)S(1)}, bf16[40,1024]{1,0:T(8,128)(2,1)S(1)}, u32[]{:S(2)}, u32[]{:S(2)}) %collective-permute-start.2) | collective-permute-done | bytes 81952 | tf_op jit(solution)/shard_map/ppermute | solution.py:400
  20.5 0.8 collective-permute-done.1.z2_ref
  21.3 1.5 %collective-permute-done.z1_ref = bf16[40,1024]{1,0:T(8,128)(2,1)S(1)} collective-permute-done((bf16[40,1024]{1,0:T(8,128)(2,1)S(1)}, bf16[40,1024]{1,0:T(8,128)(2,1)S(1)}, u32[]{:S(2)}, u32[]{:S(2)}) %collective-permute-start) | collective-permute-done | bytes 81952 | tf_op jit(solution)/shard_map/ppermute | solution.py:400
  22.8 1.0 low_levels.1
  23.8 4.6 %collective-permute-start.3 = (bf16[40,1024]{1,0:T(8,128)(2,1)S(1)}, bf16[40,1024]{1,0:T(8,128)(2,1)S(1)}, u32[]{:S(2)}, u32[]{:S(2)}) collective-permute-start(bf16[40,1024]{1,0:T(8,128)(2,1)S(1)} %get-tuple-element.18), channel_id=1, source_target_pairs={{0,128},{32,160},{64,192},{96,224},{128,0},{160,32},{192,64},{224,... | collective-permute-start | bytes 245768 | tf_op jit(solution)/shard_map/ppermute | solution.py:400
  28.4 5.6 %collective-permute-done.3.z4_ref = bf16[40,1024]{1,0:T(8,128)(2,1)S(1)} collective-permute-done((bf16[40,1024]{1,0:T(8,128)(2,1)S(1)}, bf16[40,1024]{1,0:T(8,128)(2,1)S(1)}, u32[]{:S(2)}, u32[]{:S(2)}) %collective-permute-start.3) | collective-permute-done | bytes 81952 | tf_op jit(solution)/shard_map/ppermute | solution.py:400
  34.0 0.5 top_level.1
  34.5 3.2 %collective-permute-start.6 = (bf16[104,1024]{1,0:T(8,128)(2,1)S(1)}, bf16[104,1024]{1,0:T(8,128)(2,1)S(1)}, u32[]{:S(2)}, u32[]{:S(2)}) collective-permute-start(bf16[104,1024]{1,0:T(8,128)(2,1)S(1)} %top_level.1), channel_id=1, source_target_pairs={{0,4},{1,17},{2,6},{3,19},{4,0},{5,21},{6,2},{7,23},{8,12},{9,25},... | collective-permute-start | bytes 638984 | tf_op jit(solution)/shard_map/ppermute | solution.py:412
  37.7 1.2 %collective-permute-start.5 = (bf16[104,1024]{1,0:T(8,128)(2,1)S(1)}, bf16[104,1024]{1,0:T(8,128)(2,1)S(1)}, u32[]{:S(2)}, u32[]{:S(2)}) collective-permute-start(bf16[104,1024]{1,0:T(8,128)(2,1)S(1)} %top_level.1), channel_id=1, source_target_pairs={{0,6},{1,25},{2,0},{3,27},{4,2},{5,29},{6,4},{7,31},{8,14},{9,1},{... | collective-permute-start | bytes 638984 | tf_op jit(solution)/shard_map/ppermute | solution.py:412
  38.9 0.9 collective-permute-start.4
  39.8 2.2 %collective-permute-done.6 = bf16[104,1024]{1,0:T(8,128)(2,1)S(1)} collective-permute-done((bf16[104,1024]{1,0:T(8,128)(2,1)S(1)}, bf16[104,1024]{1,0:T(8,128)(2,1)S(1)}, u32[]{:S(2)}, u32[]{:S(2)}) %collective-permute-start.6) | collective-permute-done | bytes 213024 | tf_op jit(solution)/shard_map/ppermute | solution.py:412
  42.0 2.4 %collective-permute-done.5 = bf16[104,1024]{1,0:T(8,128)(2,1)S(1)} collective-permute-done((bf16[104,1024]{1,0:T(8,128)(2,1)S(1)}, bf16[104,1024]{1,0:T(8,128)(2,1)S(1)}, u32[]{:S(2)}, u32[]{:S(2)}) %collective-permute-start.5) | collective-permute-done | bytes 213024 | tf_op jit(solution)/shard_map/ppermute | solution.py:412
  44.4 1.6 %collective-permute-done.4 = bf16[104,1024]{1,0:T(8,128)(2,1)S(1)} collective-permute-done((bf16[104,1024]{1,0:T(8,128)(2,1)S(1)}, bf16[104,1024]{1,0:T(8,128)(2,1)S(1)}, u32[]{:S(2)}, u32[]{:S(2)}) %collective-permute-start.4) | collective-permute-done | bytes 213024 | tf_op jit(solution)/shard_map/ppermute | solution.py:412
  46.1 2.8 %collective-permute-start.8 = (bf16[4,104,1024]{2,1,0:T(8,128)(2,1)S(1)}, bf16[4,104,1024]{2,1,0:T(8,128)(2,1)}, u32[]{:S(2)}, u32[]{:S(2)}) collective-permute-start(bf16[4,104,1024]{2,1,0:T(8,128)(2,1)S(1)} %pad_maximum_fusion.refs_0_), channel_id=1, source_target_pairs={{0,24},{1,7},{2,26},{3,1},{4,28},{5,3},{6,30},{7,5},{8,0},{9,15},{... | collective-permute-start | bytes 2555912 | tf_op jit(solution)/shard_map/ppermute | solution.py:412
  48.9 7.1 %apply_maps.1 = bf16[1024,1024]{1,0:T(8,128)(2,1)} custom-call(bf16[1024,1024]{1,0:T(8,128)(2,1)S(1)} %bitcast.12, bf16[2,1024,1024]{2,1,0:T(8,128)(2,1)} %maps_ref.1), custom_call_target="tpu_custom_call" | custom-call | flops 4294967296 | bytes 8388608 | tf_op jit(solution)/shard_map/apply_maps/pallas_call | solution.py:196
  56.0 3.1 %collective-permute-done.8.refs_2_ = bf16[4,104,1024]{2,1,0:T(8,128)(2,1)} collective-permute-done((bf16[4,104,1024]{2,1,0:T(8,128)(2,1)S(1)}, bf16[4,104,1024]{2,1,0:T(8,128)(2,1)}, u32[]{:S(2)}, u32[]{:S(2)}) %collective-permute-start.8) | collective-permute-done | bytes 852000 | tf_op jit(solution)/shard_map/ppermute | solution.py:412
  59.1 3.8 %collective-permute-done.7.refs_1_ = bf16[4,104,1024]{2,1,0:T(8,128)(2,1)} collective-permute-done((bf16[4,104,1024]{2,1,0:T(8,128)(2,1)S(1)}, bf16[4,104,1024]{2,1,0:T(8,128)(2,1)}, u32[]{:S(2)}, u32[]{:S(2)}) %collective-permute-start.7) | collective-permute-done | bytes 852000 | tf_op jit(solution)/shard_map/ppermute | solution.py:412
  62.9 1.8 %slice.7 = bf16[2,104,1024]{2,1,0:T(8,128)(2,1)} slice(bf16[4,104,1024]{2,1,0:T(8,128)(2,1)} %collective-permute-done.8.refs_2_), slice={[2:4], [0:104], [0:1024]} | slice | bytes 851968 | tf_op jit(solution)/shard_map/slice | solution.py:438
  64.7 1.8 %slice.6 = bf16[2,104,1024]{2,1,0:T(8,128)(2,1)} slice(bf16[4,104,1024]{2,1,0:T(8,128)(2,1)} %collective-permute-done.7.refs_1_), slice={[0:2], [0:104], [0:1024]} | slice | bytes 851968 | tf_op jit(solution)/shard_map/slice | solution.py:438
  66.5 2.0 %collective-permute-start.9 = (bf16[2,104,1024]{2,1,0:T(8,128)(2,1)}, bf16[2,104,1024]{2,1,0:T(8,128)(2,1)}, u32[]{:S(2)}, u32[]{:S(2)}) collective-permute-start(bf16[2,104,1024]{2,1,0:T(8,128)(2,1)} %slice.6), channel_id=1, source_target_pairs={{0,8},{1,3},{2,10},{3,5},{4,12},{5,7},{6,14},{7,1},{8,16},{9,11},{... | collective-permute-start | bytes 1277960 | tf_op jit(solution)/shard_map/ppermute | solution.py:412
  69.0 4.0 %all-to-all-start.1 = ((bf16[32,32,1024]{2,1,0:T(8,128)(2,1)}), bf16[32,32,1024]{2,1,0:T(8,128)(2,1)S(1)}, u32[]{:S(2)}, u32[]{:S(2)}) async-start(bf16[32,32,1024]{2,1,0:T(8,128)(2,1)} %bitcast.16), calls=%async_computation.1 | async-start | bytes 4194304 | tf_op jit(solution)/shard_map/all_to_all | solution.py:422
  73.3 2.8 %collective-permute-done.9.refs_3_ = bf16[2,104,1024]{2,1,0:T(8,128)(2,1)} collective-permute-done((bf16[2,104,1024]{2,1,0:T(8,128)(2,1)}, bf16[2,104,1024]{2,1,0:T(8,128)(2,1)}, u32[]{:S(2)}, u32[]{:S(2)}) %collective-permute-start.9) | collective-permute-done | bytes 426016 | tf_op jit(solution)/shard_map/ppermute | solution.py:412
  76.1 2.0 %collective-permute-done.14.refs_8_ = bf16[2,104,1024]{2,1,0:T(8,128)(2,1)S(1)} collective-permute-done((bf16[2,104,1024]{2,1,0:T(8,128)(2,1)}, bf16[2,104,1024]{2,1,0:T(8,128)(2,1)S(1)}, u32[]{:S(2)}, u32[]{:S(2)}) %collective-permute-start.14) | collective-permute-done | bytes 426016 | tf_op jit(solution)/shard_map/ppermute | solution.py:416
  78.1 8.1 %fold.1 = (bf16[1024,1024]{1,0:T(8,128)(2,1)}, f32[8,1024]{1,0:T(8,128)S(1)}) custom-call(bf16[4,104,1024]{2,1,0:T(8,128)(2,1)S(1)} %pad_maximum_fusion.refs_0_, bf16[4,104,1024]{2,1,0:T(8,128)(2,1)} %collective-permute-done.7.refs_1_, bf16[4,104,1024]{2,1,0:T(8,128)(2,1)} %collective-permute-done.8.refs_2_, ...), custom_call_target="tpu_custom_call" | custom-call | flops 15032385536 | bytes 9437184 | tf_op jit(solution)/shard_map/fold/pallas_call | solution.py:331
  86.2 16.8 %all-to-all-done.1 = bf16[32,32,1024]{2,1,0:T(8,128)(2,1)S(1)} async-done(((bf16[32,32,1024]{2,1,0:T(8,128)(2,1)}), bf16[32,32,1024]{2,1,0:T(8,128)(2,1)S(1)}, u32[]{:S(2)}, u32[]{:S(2)}) %all-to-all-start.1) | async-done | bytes 2097184 | tf_op jit(solution)/shard_map/all_to_all | solution.py:422
  103.0 4.1 %finish.1 = f32[512,1024]{1,0:T(8,128)} custom-call(s32[1,512]{1,0:T(1,128)S(1)} %get-tuple-element.16.target_ref, bf16[1024,1024]{1,0:T(8,128)(2,1)S(1)} %bitcast.13, bf16[1024,1024]{1,0:T(8,128)(2,1)} %get-tuple-element.25.f_ref, f32[8,1024]{1,0:T(8,128)S(1)} %get-tuple-element.26.diag_ref), custom_call_target="tpu_custom_call" | custom-call | flops 2147483648 | bytes 6291456 | tf_op jit(solution)/shard_map/finish/pallas_call | solution.py:379
  (16 shorter events, 0.9 us)
Async XLA Ops:
  3.6 19.3 %copy-start = (s32[3,1024]{1,0:T(4,128)S(1)}, s32[3,1024]{1,0:T(4,128)}, u32[]{:S(2)}) copy-start(s32[3,1024]{1,0:T(4,128)} %order_ref.3) | copy-start | bytes 36868
  3.6 45.3 %all-to-all-start = ((bf16[32,32,1024]{2,1,0:T(8,128)(2,1)}), bf16[32,32,1024]{2,1,0:T(8,128)(2,1)S(1)}, u32[]{:S(2)}, u32[]{:S(2)}) async-start(bf16[32,32,1024]{2,1,0:T(8,128)(2,1)} %bitcast.15), calls=%async_computation | async-start | bytes 4194304 | tf_op jit(solution)/shard_map/all_to_all | solution.py:422
  11.9 8.6 %collective-permute-start.2 = (bf16[40,1024]{1,0:T(8,128)(2,1)S(1)}, bf16[40,1024]{1,0:T(8,128)(2,1)S(1)}, u32[]{:S(2)}, u32[]{:S(2)}) collective-permute-start(bf16[40,1024]{1,0:T(8,128)(2,1)S(1)} %label.1.z0_ref), channel_id=1, source_target_pairs={{0,96},{32,64},{64,32},{96,0},{128,224},{160,192},{192,160},{224,1... | collective-permute-start | bytes 245768 | tf_op jit(solution)/shard_map/ppermute | solution.py:400
  13.9 7.4 %collective-permute-start.1 = (bf16[40,1024]{1,0:T(8,128)(2,1)S(1)}, bf16[40,1024]{1,0:T(8,128)(2,1)S(1)}, u32[]{:S(2)}, u32[]{:S(2)}) collective-permute-start(bf16[40,1024]{1,0:T(8,128)(2,1)S(1)} %label.1.z0_ref), channel_id=1, source_target_pairs={{0,64},{32,96},{64,0},{96,32},{128,192},{160,224},{192,128},{224,1... | collective-permute-start | bytes 245768 | tf_op jit(solution)/shard_map/ppermute | solution.py:400
  15.3 7.5 %collective-permute-start = (bf16[40,1024]{1,0:T(8,128)(2,1)S(1)}, bf16[40,1024]{1,0:T(8,128)(2,1)S(1)}, u32[]{:S(2)}, u32[]{:S(2)}) collective-permute-start(bf16[40,1024]{1,0:T(8,128)(2,1)S(1)} %label.1.z0_ref), channel_id=1, source_target_pairs={{0,32},{32,0},{64,96},{96,64},{128,160},{160,128},{192,224},{224,1... | collective-permute-start | bytes 245768 | tf_op jit(solution)/shard_map/ppermute | solution.py:400
  23.8 10.2 %collective-permute-start.3 = (bf16[40,1024]{1,0:T(8,128)(2,1)S(1)}, bf16[40,1024]{1,0:T(8,128)(2,1)S(1)}, u32[]{:S(2)}, u32[]{:S(2)}) collective-permute-start(bf16[40,1024]{1,0:T(8,128)(2,1)S(1)} %get-tuple-element.18), channel_id=1, source_target_pairs={{0,128},{32,160},{64,192},{96,224},{128,0},{160,32},{192,64},{224,... | collective-permute-start | bytes 245768 | tf_op jit(solution)/shard_map/ppermute | solution.py:400
  34.5 7.4 %collective-permute-start.6 = (bf16[104,1024]{1,0:T(8,128)(2,1)S(1)}, bf16[104,1024]{1,0:T(8,128)(2,1)S(1)}, u32[]{:S(2)}, u32[]{:S(2)}) collective-permute-start(bf16[104,1024]{1,0:T(8,128)(2,1)S(1)} %top_level.1), channel_id=1, source_target_pairs={{0,4},{1,17},{2,6},{3,19},{4,0},{5,21},{6,2},{7,23},{8,12},{9,25},... | collective-permute-start | bytes 638984 | tf_op jit(solution)/shard_map/ppermute | solution.py:412
  37.7 6.7 %collective-permute-start.5 = (bf16[104,1024]{1,0:T(8,128)(2,1)S(1)}, bf16[104,1024]{1,0:T(8,128)(2,1)S(1)}, u32[]{:S(2)}, u32[]{:S(2)}) collective-permute-start(bf16[104,1024]{1,0:T(8,128)(2,1)S(1)} %top_level.1), channel_id=1, source_target_pairs={{0,6},{1,25},{2,0},{3,27},{4,2},{5,29},{6,4},{7,31},{8,14},{9,1},{... | collective-permute-start | bytes 638984 | tf_op jit(solution)/shard_map/ppermute | solution.py:412
  38.9 7.1 %collective-permute-start.4 = (bf16[104,1024]{1,0:T(8,128)(2,1)S(1)}, bf16[104,1024]{1,0:T(8,128)(2,1)S(1)}, u32[]{:S(2)}, u32[]{:S(2)}) collective-permute-start(bf16[104,1024]{1,0:T(8,128)(2,1)S(1)} %top_level.1), channel_id=1, source_target_pairs={{0,2},{1,9},{2,4},{3,11},{4,6},{5,13},{6,0},{7,15},{8,10},{9,17},{... | collective-permute-start | bytes 638984 | tf_op jit(solution)/shard_map/ppermute | solution.py:412
  46.1 13.0 %collective-permute-start.8 = (bf16[4,104,1024]{2,1,0:T(8,128)(2,1)S(1)}, bf16[4,104,1024]{2,1,0:T(8,128)(2,1)}, u32[]{:S(2)}, u32[]{:S(2)}) collective-permute-start(bf16[4,104,1024]{2,1,0:T(8,128)(2,1)S(1)} %pad_maximum_fusion.refs_0_), channel_id=1, source_target_pairs={{0,24},{1,7},{2,26},{3,1},{4,28},{5,3},{6,30},{7,5},{8,0},{9,15},{... | collective-permute-start | bytes 2555912 | tf_op jit(solution)/shard_map/ppermute | solution.py:412
  48.9 14.0 %collective-permute-start.7 = (bf16[4,104,1024]{2,1,0:T(8,128)(2,1)S(1)}, bf16[4,104,1024]{2,1,0:T(8,128)(2,1)}, u32[]{:S(2)}, u32[]{:S(2)}) collective-permute-start(bf16[4,104,1024]{2,1,0:T(8,128)(2,1)S(1)} %pad_maximum_fusion.refs_0_), channel_id=1, source_target_pairs={{0,8},{1,3},{2,10},{3,5},{4,12},{5,7},{6,14},{7,1},{8,16},{9,11},{... | collective-permute-start | bytes 2555912 | tf_op jit(solution)/shard_map/ppermute | solution.py:412
  48.9 27.2 %collective-permute-start.11 = (bf16[4,104,1024]{2,1,0:T(8,128)(2,1)S(1)}, bf16[4,104,1024]{2,1,0:T(8,128)(2,1)}, u32[]{:S(2)}, u32[]{:S(2)}) collective-permute-start(bf16[4,104,1024]{2,1,0:T(8,128)(2,1)S(1)} %pad_maximum_fusion.refs_0_), channel_id=1, source_target_pairs={{0,1},{1,0},{2,3},{3,2},{4,5},{5,4},{6,7},{7,6},{8,9},{9,8},{10,11... | collective-permute-start | bytes 2555912 | tf_op jit(solution)/shard_map/ppermute | solution.py:416
  64.7 8.3 %collective-permute-start.10 = (bf16[2,104,1024]{2,1,0:T(8,128)(2,1)}, bf16[2,104,1024]{2,1,0:T(8,128)(2,1)S(1)}, u32[]{:S(2)}, u32[]{:S(2)}) collective-permute-start(bf16[2,104,1024]{2,1,0:T(8,128)(2,1)} %slice.7), channel_id=1, source_target_pairs={{0,24},{1,7},{2,26},{3,1},{4,28},{5,3},{6,30},{7,5},{8,0},{9,15},{... | collective-permute-start | bytes 1277960 | tf_op jit(solution)/shard_map/ppermute | solution.py:412
  66.5 9.7 %collective-permute-start.9 = (bf16[2,104,1024]{2,1,0:T(8,128)(2,1)}, bf16[2,104,1024]{2,1,0:T(8,128)(2,1)}, u32[]{:S(2)}, u32[]{:S(2)}) collective-permute-start(bf16[2,104,1024]{2,1,0:T(8,128)(2,1)} %slice.6), channel_id=1, source_target_pairs={{0,8},{1,3},{2,10},{3,5},{4,12},{5,7},{6,14},{7,1},{8,16},{9,11},{... | collective-permute-start | bytes 1277960 | tf_op jit(solution)/shard_map/ppermute | solution.py:412
  68.5 9.6 %collective-permute-start.12 = (bf16[4,104,1024]{2,1,0:T(8,128)(2,1)}, bf16[4,104,1024]{2,1,0:T(8,128)(2,1)}, u32[]{:S(2)}, u32[]{:S(2)}) collective-permute-start(bf16[4,104,1024]{2,1,0:T(8,128)(2,1)} %collective-permute-done.7.refs_1_), channel_id=1, source_target_pairs={{0,1},{1,0},{2,3},{3,2},{4,5},{5,4},{6,7},{7,6},{8,9},{9,8},{10,11... | collective-permute-start | bytes 2555912 | tf_op jit(solution)/shard_map/ppermute | solution.py:416
  68.5 9.6 %collective-permute-start.13 = (bf16[4,104,1024]{2,1,0:T(8,128)(2,1)}, bf16[4,104,1024]{2,1,0:T(8,128)(2,1)}, u32[]{:S(2)}, u32[]{:S(2)}) collective-permute-start(bf16[4,104,1024]{2,1,0:T(8,128)(2,1)} %collective-permute-done.8.refs_2_), channel_id=1, source_target_pairs={{0,1},{1,0},{2,3},{3,2},{4,5},{5,4},{6,7},{7,6},{8,9},{9,8},{10,11... | collective-permute-start | bytes 2555912 | tf_op jit(solution)/shard_map/ppermute | solution.py:416
  69.0 34.0 %all-to-all-start.1 = ((bf16[32,32,1024]{2,1,0:T(8,128)(2,1)}), bf16[32,32,1024]{2,1,0:T(8,128)(2,1)S(1)}, u32[]{:S(2)}, u32[]{:S(2)}) async-start(bf16[32,32,1024]{2,1,0:T(8,128)(2,1)} %bitcast.16), calls=%async_computation.1 | async-start | bytes 4194304 | tf_op jit(solution)/shard_map/all_to_all | solution.py:422
  73.0 3.1 %collective-permute-start.15 = (bf16[2,104,1024]{2,1,0:T(8,128)(2,1)S(1)}, bf16[2,104,1024]{2,1,0:T(8,128)(2,1)S(1)}, u32[]{:S(2)}, u32[]{:S(2)}) collective-permute-start(bf16[2,104,1024]{2,1,0:T(8,128)(2,1)S(1)} %collective-permute-done.10.refs_4_), channel_id=1, source_target_pairs={{0,1},{1,0},{2,3},{3,2},{4,5},{5,4},{6,7},{7,6},{8,9},{9,8},{10,11... | collective-permute-start | bytes 1277960 | tf_op jit(solution)/shard_map/ppermute | solution.py:416
  76.1 2.0 %collective-permute-start.14 = (bf16[2,104,1024]{2,1,0:T(8,128)(2,1)}, bf16[2,104,1024]{2,1,0:T(8,128)(2,1)S(1)}, u32[]{:S(2)}, u32[]{:S(2)}) collective-permute-start(bf16[2,104,1024]{2,1,0:T(8,128)(2,1)} %collective-permute-done.9.refs_3_), channel_id=1, source_target_pairs={{0,1},{1,0},{2,3},{3,2},{4,5},{5,4},{6,7},{7,6},{8,9},{9,8},{10,11... | collective-permute-start | bytes 1277960 | tf_op jit(solution)/shard_map/ppermute | solution.py:416
